TPU v7x, 32 devices: a whole 2x2x4 slice. The times are simulated.
32 devices in a mesh: narrow: 4 (over y, x), wide: 2 (over core), tensor: 4 (over z).
Axes of the slice: x: 2, y: 2, z: 4, core: 2. Of those that a mesh axis runs over, the one named last changes fastest.
Arguments:
- frames: bfloat16 [4, 8, 4, 32, 1152], P('narrow', None, 'wide'), may hold values from -6 to 6
- cotangent: bfloat16 [4, 8, 4, 32, 1152], P('narrow', None, 'wide'), may hold values from -6 to 6
- prompt: bfloat16 [4, 120, 4096], P('narrow'), may hold values from -6 to 6
- timestep: int32 [4], P('narrow'), may hold values from 0 to 999
- clip_lengths: int32 [4], P('narrow'), may hold values from 1 to 8, as said below
- text_lengths: int32 [4], P('narrow'), may hold values from 1 to 120, as said below
- modulation_weight: bfloat16 [1152, 6912], P('wide', 'tensor'), may hold values from -0.1875 to 0.1875
- modulation_bias: float32 [6912], replicated, may hold values from -0.5 to 0.5
- space_query: bfloat16 [1152, 1152], P('wide', 'tensor'), may hold values from -0.1875 to 0.1875
- space_key: bfloat16 [1152, 1152], P('wide', 'tensor'), may hold values from -0.1875 to 0.1875
- space_value: bfloat16 [1152, 1152], P('wide', 'tensor'), may hold values from -0.1875 to 0.1875
- space_out: bfloat16 [1152, 1152], P('wide', 'tensor'), may hold values from -1 to 1
- time_gain: float32 [1152], replicated, may hold values from 0.5 to 1.5
- time_query: bfloat16 [1152, 1152], P('wide', 'tensor'), may hold values from -0.1875 to 0.1875
- time_key: bfloat16 [1152, 1152], P('wide', 'tensor'), may hold values from -0.1875 to 0.1875
- time_value: bfloat16 [1152, 1152], P('wide', 'tensor'), may hold values from -0.1875 to 0.1875
- time_out: bfloat16 [1152, 1152], P('wide', 'tensor'), may hold values from -0.375 to 0.375
- time_gate: float32 [1152], replicated, may hold values from 0.3 to 1.5
- cross_gain: float32 [1152], replicated, may hold values from 0.5 to 1.5
- cross_query: bfloat16 [1152, 1152], P('wide', 'tensor'), may hold values from -0.1875 to 0.1875
- prompt_key: bfloat16 [4096, 1152], P('wide', 'tensor'), may hold values from -0.09375 to 0.09375
- prompt_value: bfloat16 [4096, 1152], P('wide', 'tensor'), may hold values from -0.09375 to 0.09375
- cross_out: bfloat16 [1152, 1152], P('wide', 'tensor'), may hold values from -0.75 to 0.75
- feed_up: bfloat16 [1152, 4608], P('wide', 'tensor'), may hold values from -0.1875 to 0.1875
- feed_down: bfloat16 [1152, 4608], P('wide', 'tensor'), may hold values from -0.09375 to 0.09375
Outputs:
- output: bfloat16 [4, 8, 4, 32, 1152], P('narrow', None, 'wide')
- frames_grad: bfloat16 [4, 8, 4, 32, 1152], P('narrow', None, 'wide')
- modulation_weight_grad: float32 [1152, 6912], P(('narrow', 'wide'), 'tensor')
- modulation_bias_grad: float32 [6912], P(('narrow', 'wide'))
- space_query_grad: float32 [1152, 1152], P(('narrow', 'wide'), 'tensor')
- space_key_grad: float32 [1152, 1152], P(('narrow', 'wide'), 'tensor')
- space_value_grad: float32 [1152, 1152], P(('narrow', 'wide'), 'tensor')
- space_out_grad: float32 [1152, 1152], P(('narrow', 'wide'), 'tensor')
- time_gain_grad: float32 [1152], P(('narrow', 'wide'))
- time_query_grad: float32 [1152, 1152], P(('narrow', 'wide'), 'tensor')
- time_key_grad: float32 [1152, 1152], P(('narrow', 'wide'), 'tensor')
- time_value_grad: float32 [1152, 1152], P(('narrow', 'wide'), 'tensor')
- time_out_grad: float32 [1152, 1152], P(('narrow', 'wide'), 'tensor')
- time_gate_grad: float32 [1152], P(('narrow', 'wide'))
- cross_gain_grad: float32 [1152], P(('narrow', 'wide'))
- cross_query_grad: float32 [1152, 1152], P(('narrow', 'wide'), 'tensor')
- prompt_key_grad: float32 [4096, 1152], P(('narrow', 'wide'), 'tensor')
- prompt_value_grad: float32 [4096, 1152], P(('narrow', 'wide'), 'tensor')
- cross_out_grad: float32 [1152, 1152], P(('narrow', 'wide'), 'tensor')
- feed_up_grad: float32 [1152, 4608], P(('narrow', 'wide'), 'tensor')
- feed_down_grad: float32 [1152, 4608], P(('narrow', 'wide'), 'tensor')
Inputs may be any that keep to these rules, and one draw needn't show every extreme that they name: `clip_lengths`: some clip has exactly 8 frames. `text_lengths`: some clip uses all 120 prompt tokens.
All inputs are finite; a program needn't handle non-finite values.
Results may differ from a plain program's by a relative error of at most 0.04.
Values may be sent and summed in bfloat16 or wider, within the bound.
A program may use at most 256 MiB of HBM per device.

v0:
```python
import math

import jax
import jax.numpy as jnp
from jax import lax
from jax.sharding import PartitionSpec as P

HEAD_DIM = 72


EPSILON = 1e-06
NEGATIVE = -1e30
CONTRACT_LAST = (((1,), (1,)), ((), ()))
CONTRACT_FIRST = (((0,), (0,)), ((), ()))


def matmul(left, right):
    return jnp.dot(left, right, preferred_element_type=jnp.float32)


def matmul_tr(left, right):
    return lax.dot_general(left, right, CONTRACT_LAST, preferred_element_type=jnp.float32)


def outer_sum(left, right):
    return lax.dot_general(left, right, CONTRACT_FIRST, preferred_element_type=jnp.float32)


def norm_rows(values):
    center = values - jnp.mean(values, -1, keepdims=True)
    inverse = lax.rsqrt(jnp.mean(center * center, -1, keepdims=True) + EPSILON)
    return (center * inverse, inverse)


def norm_back(normed, inverse, incoming):
    return inverse * (
        incoming
        - jnp.mean(incoming, -1, keepdims=True)
        - normed * jnp.mean(incoming * normed, -1, keepdims=True)
    )


def over_heads(partial_sum):
    return lax.psum(partial_sum.astype(jnp.bfloat16), "tensor").astype(jnp.float32)


def attend_forward(queries, key_rows, values, allowed, pattern, score_scale):
    scores = jnp.where(
        allowed,
        jnp.einsum(pattern[0], queries, key_rows, preferred_element_type=jnp.float32) * score_scale,
        NEGATIVE,
    )
    row_max = jnp.max(scores, -1, keepdims=True)
    exponent = jnp.exp(scores - row_max)
    row_total = jnp.sum(exponent, -1, keepdims=True)
    attend = (exponent / row_total).astype(jnp.bfloat16)
    context = jnp.einsum(pattern[1], attend, values, preferred_element_type=jnp.float32)
    return (context.astype(jnp.bfloat16), row_max + jnp.log(row_total))


def attend_back(queries, key_rows, values, allowed, log_total, context_grad, pattern, score_scale):
    scores = jnp.where(
        allowed,
        jnp.einsum(pattern[0], queries, key_rows, preferred_element_type=jnp.float32) * score_scale,
        NEGATIVE,
    )
    attend = jnp.exp(scores - log_total)
    attend_grad = jnp.einsum(pattern[0], context_grad, values, preferred_element_type=jnp.float32)
    score_grad = (attend * (attend_grad - jnp.sum(attend * attend_grad, -1, keepdims=True))).astype(
        jnp.bfloat16
    )
    query_grad = (
        jnp.einsum(pattern[1], score_grad, key_rows, preferred_element_type=jnp.float32)
        * score_scale
    )
    key_grad = (
        jnp.einsum(pattern[2], score_grad, queries, preferred_element_type=jnp.float32)
        * score_scale
    )
    value_grad = jnp.einsum(
        pattern[2], attend.astype(jnp.bfloat16), context_grad, preferred_element_type=jnp.float32
    )
    return (query_grad, key_grad, value_grad)


def on_device(
    frames,
    cotangent,
    prompt,
    timestep,
    clip_lengths,
    text_lengths,
    modulation_weight,
    modulation_bias,
    space_query,
    space_key,
    space_value,
    space_out,
    time_gain,
    time_query,
    time_key,
    time_value,
    time_out,
    time_gate,
    cross_gain,
    cross_query,
    prompt_key,
    prompt_value,
    cross_out,
    feed_up,
    feed_down,
):
    frame_count = frames.shape[1]
    patch_count = frames.shape[2] * frames.shape[3]
    model_width = frames.shape[4]
    token_count = frame_count * patch_count
    score_scale = 1.0 / math.sqrt(HEAD_DIM)
    residual = frames.reshape(token_count, model_width).astype(jnp.float32)
    frame_live = jnp.arange(frame_count) < clip_lengths[0]
    token_live = jnp.repeat(frame_live, patch_count)[:, None]
    prompt_rows = prompt[0]
    word_live = jnp.arange(prompt_rows.shape[0]) < text_lengths[0]
    (
        modulation_weight,
        space_query,
        space_key,
        space_value,
        space_out,
        time_query,
        time_key,
        time_value,
        time_out,
        cross_query,
        prompt_key,
        prompt_value,
        cross_out,
        feed_up,
        feed_down,
    ) = (
        lax.all_gather(modulation_weight, "wide", axis=0, tiled=True),
        lax.all_gather(space_query, "wide", axis=0, tiled=True),
        lax.all_gather(space_key, "wide", axis=0, tiled=True),
        lax.all_gather(space_value, "wide", axis=0, tiled=True),
        lax.all_gather(space_out, "wide", axis=0, tiled=True),
        lax.all_gather(time_query, "wide", axis=0, tiled=True),
        lax.all_gather(time_key, "wide", axis=0, tiled=True),
        lax.all_gather(time_value, "wide", axis=0, tiled=True),
        lax.all_gather(time_out, "wide", axis=0, tiled=True),
        lax.all_gather(cross_query, "wide", axis=0, tiled=True),
        lax.all_gather(prompt_key, "wide", axis=0, tiled=True),
        lax.all_gather(prompt_value, "wide", axis=0, tiled=True),
        lax.all_gather(cross_out, "wide", axis=0, tiled=True),
        lax.all_gather(feed_up, "wide", axis=0, tiled=True),
        lax.all_gather(feed_down, "wide", axis=0, tiled=True),
    )
    head_width = space_query.shape[1]
    head_count = head_width // HEAD_DIM
    split_heads = (frame_count, patch_count, head_count, HEAD_DIM)
    half_width = model_width // 2
    frequency = jnp.exp(-math.log(10000.0) * jnp.arange(half_width, dtype=jnp.float32) / half_width)
    angles = timestep[0].astype(jnp.float32) * frequency
    condition = jax.nn.silu(jnp.concatenate([jnp.cos(angles), jnp.sin(angles)])).astype(
        jnp.bfloat16
    )
    slice_width = modulation_weight.shape[1]
    slice_start = lax.axis_index("tensor") * slice_width
    own_modulation = matmul(condition[None, :], modulation_weight)[0] + lax.dynamic_slice_in_dim(
        modulation_bias, slice_start, slice_width
    )
    modulation = lax.all_gather(own_modulation, "tensor", axis=0, tiled=True)
    shift_one, scale_one, gate_one, shift_two, scale_two, gate_two = jnp.split(modulation, 6)
    normed_one, inverse_one = norm_rows(residual)
    input_one = (normed_one * (1.0 + scale_one) + shift_one).astype(jnp.bfloat16)
    query_one = matmul(input_one, space_query).astype(jnp.bfloat16).reshape(split_heads)
    key_one = matmul(input_one, space_key).astype(jnp.bfloat16).reshape(split_heads)
    value_one = matmul(input_one, space_value).astype(jnp.bfloat16).reshape(split_heads)
    key_frame, value_frame = (
        lax.all_gather(key_one, "wide", axis=1, tiled=True),
        lax.all_gather(value_one, "wide", axis=1, tiled=True),
    )
    space_pattern = ("fphe,fkhe->fhpk", "fhpk,fkhe->fphe", "fhpk,fphe->fkhe")
    every_patch = jnp.ones((key_frame.shape[1],), jnp.bool_)
    context_one, log_one = attend_forward(
        query_one, key_frame, value_frame, every_patch, space_pattern, score_scale
    )
    context_one = context_one.reshape(token_count, head_width)
    branch_one = over_heads(matmul_tr(context_one, space_out))
    after_one = residual + gate_one * branch_one
    normed_two, inverse_two = norm_rows(after_one)
    input_two = (normed_two * time_gain).astype(jnp.bfloat16)
    query_two = matmul(input_two, time_query).astype(jnp.bfloat16).reshape(split_heads)
    key_two = matmul(input_two, time_key).astype(jnp.bfloat16).reshape(split_heads)
    value_two = matmul(input_two, time_value).astype(jnp.bfloat16).reshape(split_heads)
    time_pattern = ("fphe,gphe->phfg", "phfg,gphe->fphe", "phfg,fphe->gphe")
    context_two, log_two = attend_forward(
        query_two, key_two, value_two, frame_live, time_pattern, score_scale
    )
    context_two = context_two.reshape(token_count, head_width)
    branch_two = over_heads(matmul_tr(context_two, time_out))
    gate_time = jnp.tanh(time_gate)
    after_two = after_one + gate_time * branch_two
    normed_three, inverse_three = norm_rows(after_two)
    input_three = (normed_three * cross_gain).astype(jnp.bfloat16)
    query_three = (
        matmul(input_three, cross_query)
        .astype(jnp.bfloat16)
        .reshape(token_count, head_count, HEAD_DIM)
    )
    word_keys = (
        matmul(prompt_rows, prompt_key).astype(jnp.bfloat16).reshape(-1, head_count, HEAD_DIM)
    )
    word_values = (
        matmul(prompt_rows, prompt_value).astype(jnp.bfloat16).reshape(-1, head_count, HEAD_DIM)
    )
    cross_pattern = ("nhe,jhe->nhj", "nhj,jhe->nhe", "nhj,nhe->jhe")
    context_three, log_three = attend_forward(
        query_three, word_keys, word_values, word_live, cross_pattern, score_scale
    )
    context_three = context_three.reshape(token_count, head_width)
    branch_three = over_heads(matmul_tr(context_three, cross_out))
    after_three = after_two + branch_three
    normed_four, inverse_four = norm_rows(after_three)
    input_four = (normed_four * (1.0 + scale_two) + shift_two).astype(jnp.bfloat16)
    pre_act = matmul(input_four, feed_up)
    hidden, gelu_pull = jax.vjp(lambda inner: jax.nn.gelu(inner, approximate=True), pre_act)
    hidden = hidden.astype(jnp.bfloat16)
    branch_four = over_heads(matmul_tr(hidden, feed_down))
    after_four = after_three + gate_two * branch_four
    output = jnp.where(token_live, after_four, 0.0).astype(jnp.bfloat16).reshape(frames.shape)
    upstream = jnp.where(
        token_live, cotangent.reshape(token_count, model_width).astype(jnp.float32), 0.0
    )
    feed_grad = (gate_two * upstream).astype(jnp.bfloat16)
    gate_two_grad = jnp.sum(upstream * branch_four, 0)
    feed_down_grad = outer_sum(feed_grad, hidden)
    pre_grad = gelu_pull(matmul(feed_grad, feed_down))[0].astype(jnp.bfloat16)
    feed_up_grad = outer_sum(input_four, pre_grad)
    input_four_grad = over_heads(matmul_tr(pre_grad, feed_up))
    shift_two_grad = jnp.sum(input_four_grad, 0)
    scale_two_grad = jnp.sum(input_four_grad * normed_four, 0)
    upstream = upstream + norm_back(normed_four, inverse_four, input_four_grad * (1.0 + scale_two))
    cross_grad = upstream.astype(jnp.bfloat16)
    cross_out_grad = outer_sum(cross_grad, context_three)
    context_grad = (
        matmul(cross_grad, cross_out)
        .astype(jnp.bfloat16)
        .reshape(token_count, head_count, HEAD_DIM)
    )
    query_grad, key_grad, value_grad = attend_back(
        query_three,
        word_keys,
        word_values,
        word_live,
        log_three,
        context_grad,
        cross_pattern,
        score_scale,
    )
    query_grad = query_grad.astype(jnp.bfloat16).reshape(token_count, head_width)
    cross_query_grad = outer_sum(input_three, query_grad)
    word_key_grad = key_grad.astype(jnp.bfloat16).reshape(-1, head_width)
    word_value_grad = value_grad.astype(jnp.bfloat16).reshape(-1, head_width)
    prompt_key_grad = outer_sum(prompt_rows, word_key_grad)
    prompt_value_grad = outer_sum(prompt_rows, word_value_grad)
    input_three_grad = over_heads(matmul_tr(query_grad, cross_query))
    cross_gain_grad = jnp.sum(input_three_grad * normed_three, 0)
    upstream = upstream + norm_back(normed_three, inverse_three, input_three_grad * cross_gain)
    time_grad = (gate_time * upstream).astype(jnp.bfloat16)
    time_gate_grad = jnp.sum(upstream * branch_two, 0) * (1.0 - gate_time * gate_time)
    time_out_grad = outer_sum(time_grad, context_two)
    context_grad = matmul(time_grad, time_out).astype(jnp.bfloat16).reshape(split_heads)
    query_grad, key_grad, value_grad = attend_back(
        query_two, key_two, value_two, frame_live, log_two, context_grad, time_pattern, score_scale
    )
    query_grad = query_grad.astype(jnp.bfloat16).reshape(token_count, head_width)
    key_grad = key_grad.astype(jnp.bfloat16).reshape(token_count, head_width)
    value_grad = value_grad.astype(jnp.bfloat16).reshape(token_count, head_width)
    time_query_grad = outer_sum(input_two, query_grad)
    time_key_grad = outer_sum(input_two, key_grad)
    time_value_grad = outer_sum(input_two, value_grad)
    input_two_grad = over_heads(
        matmul_tr(query_grad, time_query)
        + matmul_tr(key_grad, time_key)
        + matmul_tr(value_grad, time_value)
    )
    time_gain_grad = jnp.sum(input_two_grad * normed_two, 0)
    upstream = upstream + norm_back(normed_two, inverse_two, input_two_grad * time_gain)
    space_grad = (gate_one * upstream).astype(jnp.bfloat16)
    gate_one_grad = jnp.sum(upstream * branch_one, 0)
    space_out_grad = outer_sum(space_grad, context_one)
    context_grad = matmul(space_grad, space_out).astype(jnp.bfloat16).reshape(split_heads)
    key_frame, value_frame = (
        lax.all_gather(key_one, "wide", axis=1, tiled=True),
        lax.all_gather(value_one, "wide", axis=1, tiled=True),
    )
    query_grad, key_grad, value_grad = attend_back(
        query_one,
        key_frame,
        value_frame,
        every_patch,
        log_one,
        context_grad,
        space_pattern,
        score_scale,
    )
    key_grad, value_grad = (
        lax.psum_scatter(
            key_grad.astype(jnp.bfloat16), "wide", scatter_dimension=1, tiled=True
        ).astype(jnp.float32),
        lax.psum_scatter(
            value_grad.astype(jnp.bfloat16), "wide", scatter_dimension=1, tiled=True
        ).astype(jnp.float32),
    )
    query_grad = query_grad.astype(jnp.bfloat16).reshape(token_count, head_width)
    key_grad = key_grad.astype(jnp.bfloat16).reshape(token_count, head_width)
    value_grad = value_grad.astype(jnp.bfloat16).reshape(token_count, head_width)
    space_query_grad = outer_sum(input_one, query_grad)
    space_key_grad = outer_sum(input_one, key_grad)
    space_value_grad = outer_sum(input_one, value_grad)
    input_one_grad = over_heads(
        matmul_tr(query_grad, space_query)
        + matmul_tr(key_grad, space_key)
        + matmul_tr(value_grad, space_value)
    )
    shift_one_grad = jnp.sum(input_one_grad, 0)
    scale_one_grad = jnp.sum(input_one_grad * normed_one, 0)
    upstream = upstream + norm_back(normed_one, inverse_one, input_one_grad * (1.0 + scale_one))
    frames_grad = upstream.astype(jnp.bfloat16).reshape(frames.shape)
    modulation_bias_grad = jnp.concatenate(
        [
            shift_one_grad,
            scale_one_grad,
            gate_one_grad,
            shift_two_grad,
            scale_two_grad,
            gate_two_grad,
        ]
    )
    own_grad = lax.dynamic_slice_in_dim(modulation_bias_grad, slice_start, slice_width)
    modulation_weight_grad = condition.astype(jnp.float32)[:, None] * own_grad[None, :]
    (
        modulation_weight_grad,
        modulation_bias_grad,
        space_query_grad,
        space_key_grad,
        space_value_grad,
        space_out_grad,
        time_gain_grad,
        time_query_grad,
        time_key_grad,
        time_value_grad,
        time_out_grad,
        time_gate_grad,
        cross_gain_grad,
        cross_query_grad,
        prompt_key_grad,
        prompt_value_grad,
        cross_out_grad,
        feed_up_grad,
        feed_down_grad,
    ) = (
        lax.psum_scatter(
            modulation_weight_grad, ("narrow", "wide"), scatter_dimension=0, tiled=True
        ),
        lax.psum_scatter(modulation_bias_grad, ("narrow", "wide"), scatter_dimension=0, tiled=True),
        lax.psum_scatter(space_query_grad, ("narrow", "wide"), scatter_dimension=0, tiled=True),
        lax.psum_scatter(space_key_grad, ("narrow", "wide"), scatter_dimension=0, tiled=True),
        lax.psum_scatter(space_value_grad, ("narrow", "wide"), scatter_dimension=0, tiled=True),
        lax.psum_scatter(space_out_grad, ("narrow", "wide"), scatter_dimension=0, tiled=True),
        lax.psum_scatter(time_gain_grad, ("narrow", "wide"), scatter_dimension=0, tiled=True),
        lax.psum_scatter(time_query_grad, ("narrow", "wide"), scatter_dimension=0, tiled=True),
        lax.psum_scatter(time_key_grad, ("narrow", "wide"), scatter_dimension=0, tiled=True),
        lax.psum_scatter(time_value_grad, ("narrow", "wide"), scatter_dimension=0, tiled=True),
        lax.psum_scatter(time_out_grad, ("narrow", "wide"), scatter_dimension=0, tiled=True),
        lax.psum_scatter(time_gate_grad, ("narrow", "wide"), scatter_dimension=0, tiled=True),
        lax.psum_scatter(cross_gain_grad, ("narrow", "wide"), scatter_dimension=0, tiled=True),
        lax.psum_scatter(cross_query_grad, ("narrow", "wide"), scatter_dimension=0, tiled=True),
        lax.psum_scatter(prompt_key_grad, ("narrow", "wide"), scatter_dimension=0, tiled=True),
        lax.psum_scatter(prompt_value_grad, ("narrow", "wide"), scatter_dimension=0, tiled=True),
        lax.psum_scatter(cross_out_grad, ("narrow", "wide"), scatter_dimension=0, tiled=True),
        lax.psum_scatter(feed_up_grad, ("narrow", "wide"), scatter_dimension=0, tiled=True),
        lax.psum_scatter(feed_down_grad, ("narrow", "wide"), scatter_dimension=0, tiled=True),
    )
    return (
        output,
        frames_grad,
        modulation_weight_grad,
        modulation_bias_grad,
        space_query_grad,
        space_key_grad,
        space_value_grad,
        space_out_grad,
        time_gain_grad,
        time_query_grad,
        time_key_grad,
        time_value_grad,
        time_out_grad,
        time_gate_grad,
        cross_gain_grad,
        cross_query_grad,
        prompt_key_grad,
        prompt_value_grad,
        cross_out_grad,
        feed_up_grad,
        feed_down_grad,
    )


def solution(mesh):
    return jax.shard_map(
        on_device,
        mesh=mesh,
        in_specs=(
            P("narrow", None, "wide", None, None),
            P("narrow", None, "wide", None, None),
            P("narrow", None, None),
            P("narrow"),
            P("narrow"),
            P("narrow"),
            P("wide", "tensor"),
            P(),
            P("wide", "tensor"),
            P("wide", "tensor"),
            P("wide", "tensor"),
            P("wide", "tensor"),
            P(),
            P("wide", "tensor"),
            P("wide", "tensor"),
            P("wide", "tensor"),
            P("wide", "tensor"),
            P(),
            P(),
            P("wide", "tensor"),
            P("wide", "tensor"),
            P("wide", "tensor"),
            P("wide", "tensor"),
            P("wide", "tensor"),
            P("wide", "tensor"),
        ),
        out_specs=(
            P("narrow", None, "wide", None, None),
            P("narrow", None, "wide", None, None),
            P(("narrow", "wide"), "tensor"),
            P(("narrow", "wide")),
            P(("narrow", "wide"), "tensor"),
            P(("narrow", "wide"), "tensor"),
            P(("narrow", "wide"), "tensor"),
            P(("narrow", "wide"), "tensor"),
            P(("narrow", "wide")),
            P(("narrow", "wide"), "tensor"),
            P(("narrow", "wide"), "tensor"),
            P(("narrow", "wide"), "tensor"),
            P(("narrow", "wide"), "tensor"),
            P(("narrow", "wide")),
            P(("narrow", "wide")),
            P(("narrow", "wide"), "tensor"),
            P(("narrow", "wide"), "tensor"),
            P(("narrow", "wide"), "tensor"),
            P(("narrow", "wide"), "tensor"),
            P(("narrow", "wide"), "tensor"),
            P(("narrow", "wide"), "tensor"),
        ),
        check_vma=False,
    )
```

profile of v0, /device:TPU:0, one launch (start us, length us, event | category | flops | bytes accessed | tf_op | source)
XLA Modules:
  0.0 1471.8 jit_solution(17306719336269292527)
XLA Ops:
  29.5 2.9 convolution_reduce_fusion
  33.3 20.2 %all-reduce = f32[6912]{0:T(1024)S(1)} all-reduce(f32[6912]{0:T(1024)S(1)} %add_dynamic-update-slice_fusion), channel_id=1, replica_groups=mesh['narrow'=4,'wide'=2,'tensor'=4] {'tensor'}, use_global_device_ids=true, to_apply=%add | all-reduce | flops 6912 | bytes 55296
  59.7 4.3 all_gather.59
  70.2 2.8 convolution_convert_fusion.17
  75.5 3.1 all_gather.62
  86.2 2.9 convolution_convert_fusion.5
  108.8 34.6 %all-reduce.15.cloned.1.call-done = bf16[512,1152]{1,0:T(8,128)(2,1)} async-done(((bf16[512,1152]{1,0:T(8,128)(2,1)}), bf16[512,1152]{1,0:T(8,128)(2,1)}) %all-reduce.15.cloned.1.call-update) | async-done | bytes 1179664 | tf_op jit(solution)/shard_map/psum | solution.py:44
  151.0 2.8 copy.146
  158.7 2.8 copy.143
  166.4 2.8 copy.144
  183.4 3.1 convolution_convert_fusion.4
  191.9 2.8 reshape.426
  199.8 2.8 reshape.428
  202.6 3.1 convolution_convert_fusion.23
  208.1 34.2 %all-reduce.17.cloned.1.call-done = bf16[512,1152]{1,0:T(8,128)(2,1)} async-done(((bf16[512,1152]{1,0:T(8,128)(2,1)}), bf16[512,1152]{1,0:T(8,128)(2,1)}) %all-reduce.17.cloned.1.call-update) | async-done | bytes 1179664 | tf_op jit(solution)/shard_map/psum | solution.py:44
  257.0 5.4 fusion.123
  262.4 51.8 %all-reduce.19.cloned.1.call-done = bf16[512,1152]{1,0:T(8,128)(2,1)} async-done(((bf16[512,1152]{1,0:T(8,128)(2,1)}), bf16[512,1152]{1,0:T(8,128)(2,1)}) %all-reduce.19.cloned.1.call-update) | async-done | bytes 1179664 | tf_op jit(solution)/shard_map/psum | solution.py:44
  318.9 7.8 all-gather.22.cloned.1.call-done
  326.7 7.5 fusion.48
  335.2 2.9 convolution_convert_fusion.1
  339.5 55.9 %all-reduce.21.cloned.1.call-done = bf16[512,1152]{1,0:T(8,128)(2,1)} async-done(((bf16[512,1152]{1,0:T(8,128)(2,1)}), bf16[512,1152]{1,0:T(8,128)(2,1)}) %all-reduce.21.cloned.1.call-update) | async-done | bytes 1179664 | tf_op jit(solution)/shard_map/psum | solution.py:44
  395.4 3.8 fusion.49
  409.7 53.6 %all-reduce.23.cloned.1.call-done = bf16[512,1152]{1,0:T(8,128)(2,1)} async-done(((bf16[512,1152]{1,0:T(8,128)(2,1)}), bf16[512,1152]{1,0:T(8,128)(2,1)}) %all-reduce.23.cloned.1.call-update) | async-done | bytes 1179664 | tf_op jit(solution)/shard_map/psum | solution.py:44
  463.4 3.7 fusion.27
  467.1 3.7 fusion.18
  475.8 2.8 copy.152
  496.1 3.5 fusion.125
  511.6 3.1 convolution_add_fusion.3
  516.9 55.5 %all-reduce.25.cloned.1.call-done = bf16[512,1152]{1,0:T(8,128)(2,1)} async-done(((bf16[512,1152]{1,0:T(8,128)(2,1)}), bf16[512,1152]{1,0:T(8,128)(2,1)}) %all-reduce.25.cloned.1.call-update) | async-done | bytes 1179664 | tf_op jit(solution)/shard_map/psum | solution.py:44
  572.4 3.3 fusion.32
  596.7 5.9 convolution_convert_fusion.2
  623.4 3.0 fusion.133
  626.5 3.8 fusion.92
  630.3 3.0 fusion.130
  633.4 3.0 fusion.131
  636.5 3.0 fusion.132
  639.9 3.7 fusion.101
  644.2 3.0 fusion.127
  647.4 3.7 fusion.102
  651.1 3.1 fusion.128
  654.3 3.0 fusion.129
  657.4 6.3 fusion.111
  664.9 5.8 fusion.110
  672.2 2.9 convolution_bitcast_fusion.1
  676.7 2.9 convolution_bitcast_fusion
  680.1 39.3 %all-reduce.27.cloned.1.call-done = (bf16[512,1152]{1,0:T(8,128)(2,1)}, bf16[512,1152]{1,0:T(8,128)(2,1)}) async-done(((bf16[512,1152]{1,0:T(8,128)(2,1)}, bf16[512,1152]{1,0:T(8,128)(2,1)}), (bf16[512,1152]{1,0:T(8,128)(2,1)}, bf16[512,1152]{1,0:T(8,128)(2,1)})) %all-reduce.27.cloned.1.call-update) | async-done | bytes 2359312 | tf_op jit(solution)/shard_map/psum | solution.py:44
  722.0 3.0 fusion.22
  725.1 3.9 broadcast_multiply_fusion
  731.6 24.8 %all-reduce.5 = (f32[6912]{0:T(1024)S(1)}, f32[1152]{0:T(1024)S(1)}, f32[1152]{0:T(1024)S(1)}, f32[1152]{0:T(1024)S(1)}) all-reduce(f32[6912]{0:T(1024)S(1)} %constant_dynamic-update-slice_fusion, f32[1152]{0:T(1024)S(1)} %copy-done.112, ...), channel_id=5, replica_groups=mesh['narrow'=4,'wide'=2,'tensor'=4] {'narrow','wide'}, use_global_device_ids=true, to_apply=%region_42.43.clone | all-reduce | flops 10368 | bytes 82944
  759.0 3.6 fusion.36
  762.6 42.6 %reduce-scatter.46.cloned.1.call-done = f32[144,288]{1,0:T(8,128)} async-done(((f32[1152,288]{1,0:T(8,128)}), f32[144,288]{1,0:T(8,128)}) %reduce-scatter.46.cloned.1.call-update) | async-done | bytes 165904 | tf_op jit(solution)/shard_map/reduce_scatter | solution.py:380
  805.2 43.2 %reduce-scatter.32.cloned.1.call-done = f32[144,288]{1,0:T(8,128)} async-done(((f32[1152,288]{1,0:T(8,128)}), f32[144,288]{1,0:T(8,128)}) %reduce-scatter.32.cloned.1.call-update) | async-done | bytes 165904 | tf_op jit(solution)/shard_map/reduce_scatter | solution.py:371
  848.4 43.2 %reduce-scatter.34.cloned.1.call-done = f32[144,288]{1,0:T(8,128)} async-done(((f32[1152,288]{1,0:T(8,128)}), f32[144,288]{1,0:T(8,128)}) %reduce-scatter.34.cloned.1.call-update) | async-done | bytes 165904 | tf_op jit(solution)/shard_map/reduce_scatter | solution.py:372
  891.6 43.4 %reduce-scatter.36.cloned.1.call-done = f32[144,288]{1,0:T(8,128)} async-done(((f32[1152,288]{1,0:T(8,128)}), f32[144,288]{1,0:T(8,128)}) %reduce-scatter.36.cloned.1.call-update) | async-done | bytes 165904 | tf_op jit(solution)/shard_map/reduce_scatter | solution.py:373
  935.0 43.2 %reduce-scatter.38.cloned.1.call-done = f32[144,288]{1,0:T(8,128)} async-done(((f32[1152,288]{1,0:T(8,128)}), f32[144,288]{1,0:T(8,128)}) %reduce-scatter.38.cloned.1.call-update) | async-done | bytes 165904 | tf_op jit(solution)/shard_map/reduce_scatter | solution.py:374
  978.3 43.4 %reduce-scatter.24.cloned.1.call-done = f32[144,288]{1,0:T(8,128)} async-done(((f32[1152,288]{1,0:T(8,128)}), f32[144,288]{1,0:T(8,128)}) %reduce-scatter.24.cloned.1.call-update) | async-done | bytes 165904 | tf_op jit(solution)/shard_map/reduce_scatter | solution.py:366
  1021.6 43.4 %reduce-scatter.30.cloned.1.call-done = f32[144,288]{1,0:T(8,128)} async-done(((f32[1152,288]{1,0:T(8,128)}), f32[144,288]{1,0:T(8,128)}) %reduce-scatter.30.cloned.1.call-update) | async-done | bytes 165904 | tf_op jit(solution)/shard_map/reduce_scatter | solution.py:369
  1065.0 43.4 %reduce-scatter.26.cloned.1.call-done = f32[144,288]{1,0:T(8,128)} async-done(((f32[1152,288]{1,0:T(8,128)}), f32[144,288]{1,0:T(8,128)}) %reduce-scatter.26.cloned.1.call-update) | async-done | bytes 165904 | tf_op jit(solution)/shard_map/reduce_scatter | solution.py:367
  1108.4 43.2 %reduce-scatter.28.cloned.1.call-done = f32[144,288]{1,0:T(8,128)} async-done(((f32[1152,288]{1,0:T(8,128)}), f32[144,288]{1,0:T(8,128)}) %reduce-scatter.28.cloned.1.call-update) | async-done | bytes 165904 | tf_op jit(solution)/shard_map/reduce_scatter | solution.py:368
  1151.6 60.9 %reduce-scatter.48.cloned.1.call-done = f32[144,1152]{1,0:T(8,128)} async-done(((f32[1152,1152]{1,0:T(8,128)}), f32[144,1152]{1,0:T(8,128)}) %reduce-scatter.48.cloned.1.call-update) | async-done | bytes 663568 | tf_op jit(solution)/shard_map/reduce_scatter | solution.py:381
  1212.6 61.2 %reduce-scatter.50.cloned.1.call-done = f32[144,1152]{1,0:T(8,128)} async-done(((f32[1152,1152]{1,0:T(8,128)}), f32[144,1152]{1,0:T(8,128)}) %reduce-scatter.50.cloned.1.call-update) | async-done | bytes 663568 | tf_op jit(solution)/shard_map/reduce_scatter | solution.py:382
  1273.7 57.8 %reduce-scatter.42.cloned.1.call-done = f32[512,288]{0,1:T(8,128)} async-done(((f32[4096,288]{0,1:T(8,128)}), f32[512,288]{0,1:T(8,128)}) %reduce-scatter.42.cloned.1.call-update) | async-done | bytes 589840 | tf_op jit(solution)/shard_map/reduce_scatter | solution.py:378
  1331.5 58.3 %reduce-scatter.44.cloned.1.call-done = f32[512,288]{0,1:T(8,128)} async-done(((f32[4096,288]{0,1:T(8,128)}), f32[512,288]{0,1:T(8,128)}) %reduce-scatter.44.cloned.1.call-update) | async-done | bytes 589840 | tf_op jit(solution)/shard_map/reduce_scatter | solution.py:379
  1389.8 74.9 %reduce-scatter.22.cloned.1.call-done = f32[144,1728]{1,0:T(8,128)} async-done(((f32[1152,1728]{1,0:T(8,128)}), f32[144,1728]{1,0:T(8,128)}) %reduce-scatter.22.cloned.1.call-update) | async-done | bytes 995344 | tf_op jit(solution)/shard_map/reduce_scatter | solution.py:362
  (499 shorter events, 229.3 us)
Async XLA Ops:
  7.2 195.4 %copy-start = (bf16[1,120,4096]{2,1,0:T(8,128)(2,1)S(1)}, bf16[1,120,4096]{2,1,0:T(8,128)(2,1)}, u32[]{:S(2)}) copy-start(bf16[1,120,4096]{2,1,0:T(8,128)(2,1)} %param.27) | copy-start | bytes 2949124
  7.2 22.2 %all-gather.16.cloned.1.call-start = ((), (), s32[]{:S(2)}) async-start(), calls=%async_computation.17 | async-start | bytes 6193152 | tf_op jit(solution)/shard_map/all_gather | solution.py:140
  8.0 135.5 %all-reduce.15.cloned.1.call-start = ((), (), s32[]{:S(2)}) async-start(), calls=%async_computation.18 | async-start | bytes 2359296 | tf_op jit(solution)/shard_map/psum | solution.py:44
  9.8 44.4 %copy-start.104 = (f32[512]{0:T(512)}, f32[512]{0:T(512)S(1)}, u32[]{:S(2)}) copy-start(f32[512]{0:T(512)S(1)} %div.94) | copy-start | bytes 6148
  9.8 5.4 copy-start.62
  10.3 43.8 %copy-start.106 = (f32[512]{0:T(512)}, f32[512]{0:T(512)S(1)}, u32[]{:S(2)}) copy-start(f32[512]{0:T(512)S(1)} %rsqrt.37) | copy-start | bytes 6148
  22.3 5.9 copy-start.131
  29.4 26.3 %copy-start.41 = (bf16[1152,288]{0,1:T(8,128)(2,1)S(1)}, bf16[1152,288]{0,1:T(8,128)(2,1)}, u32[]{:S(2)}) copy-start(bf16[1152,288]{0,1:T(8,128)(2,1)} %reshape.410) | copy-start | bytes 1990660
  57.1 6.9 copy-start.43
  64.0 6.2 copy-start.52
  70.2 8.4 copy-start.23
  75.5 6.6 copy-start.34
  86.2 4.9 copy-start.65
  89.1 113.5 %all-gather.18.cloned.1.call-start = ((), (), s32[]{:S(2)}) async-start(), calls=%async_computation.20 | async-start | bytes 3538944 | tf_op jit(solution)/shard_map/all_gather | solution.py:151
  89.8 115.8 %all-gather.20.cloned.1.call-start = ((), (), s32[]{:S(2)}) async-start(), calls=%async_computation.21 | async-start | bytes 3538944 | tf_op jit(solution)/shard_map/all_gather | solution.py:150
  90.4 151.9 %all-reduce.17.cloned.1.call-start = ((), (), s32[]{:S(2)}) async-start(), calls=%async_computation.19 | async-start | bytes 2359296 | tf_op jit(solution)/shard_map/psum | solution.py:44
  91.1 82.8 %copy-start.125 = (pred[8]{0:T(512)(128)(4,1)}, pred[8]{0:T(512)(128)(4,1)S(1)}, u32[]{:S(2)}) copy-start(pred[8]{0:T(512)(128)(4,1)S(1)} %iota_compare_fusion.1) | copy-start | bytes 28
  94.0 5.8 copy-start.66
  186.5 70.5 %all-gather.24.cloned.1.call-start = ((), (), s32[]{:S(2)}) async-start(), calls=%async_computation.24 | async-start | bytes 3981312 | tf_op jit(solution)/shard_map/all_gather | solution.py:154
  187.1 127.1 %all-reduce.19.cloned.1.call-start = ((), (), s32[]{:S(2)}) async-start(), calls=%async_computation.22 | async-start | bytes 2359296 | tf_op jit(solution)/shard_map/psum | solution.py:44
  250.8 75.9 %all-gather.22.cloned.1.call-start = ((), (), s32[]{:S(2)}) async-start(), calls=%async_computation.23 | async-start | bytes 3981312 | tf_op jit(solution)/shard_map/all_gather | solution.py:153
  251.5 143.8 %all-reduce.21.cloned.1.call-start = ((), (), s32[]{:S(2)}) async-start(), calls=%async_computation.25 | async-start | bytes 2359296 | tf_op jit(solution)/shard_map/psum | solution.py:44
  326.7 8.5 copy-start.129
  338.1 125.2 %all-reduce.23.cloned.1.call-start = ((), (), s32[]{:S(2)}) async-start(), calls=%async_computation.26 | async-start | bytes 2359296 | tf_op jit(solution)/shard_map/psum | solution.py:44
  405.1 58.2 %copy-start.90 = (f32[1152]{0:T(1024)S(1)}, f32[1152]{0:T(1024)}, u32[]{:S(2)}) copy-start(f32[1152]{0:T(1024)} %param.43) | copy-start | bytes 13828
  407.7 164.7 %all-reduce.25.cloned.1.call-start = ((), (), s32[]{:S(2)}) async-start(), calls=%async_computation.27 | async-start | bytes 2359296 | tf_op jit(solution)/shard_map/psum | solution.py:44
  409.7 57.4 %copy-start.91 = (f32[1152]{0:T(1024)S(1)}, f32[1152]{0:T(1024)}, u32[]{:S(2)}) copy-start(f32[1152]{0:T(1024)} %param.43) | copy-start | bytes 13828
  409.7 57.4 %copy-start.100 = (f32[512]{0:T(512)S(1)}, f32[512]{0:T(512)}, u32[]{:S(2)}) copy-start(f32[512]{0:T(512)} %copy-done.99) | copy-start | bytes 6148
  409.7 57.4 %copy-start.118 = (f32[512]{0:T(512)S(1)}, f32[512]{0:T(512)}, u32[]{:S(2)}) copy-start(f32[512]{0:T(512)} %copy-done.117) | copy-start | bytes 6148
  467.1 5.2 copy-start.49
  467.1 5.2 copy-start.78
  514.8 57.6 %copy-start.93 = (f32[1152]{0:T(1024)S(1)}, f32[1152]{0:T(1024)}, u32[]{:S(2)}) copy-start(f32[1152]{0:T(1024)} %param.37) | copy-start | bytes 13828
  514.8 57.6 %copy-start.98 = (f32[512]{0:T(512)S(1)}, f32[512]{0:T(512)}, u32[]{:S(2)}) copy-start(f32[512]{0:T(512)} %copy-done.97) | copy-start | bytes 6148
  514.8 57.6 %copy-start.116 = (f32[512]{0:T(512)S(1)}, f32[512]{0:T(512)}, u32[]{:S(2)}) copy-start(f32[512]{0:T(512)} %copy-done.115) | copy-start | bytes 6148
  516.8 92.8 %reduce-scatter.18.cloned.1.call-start = ((), (), s32[]{:S(2)}) async-start(), calls=%async_computation.28 | async-start | bytes 1572864 | tf_op jit(solution)/shard_map/reduce_scatter | solution.py:307
  591.1 22.7 %reduce-scatter.20.cloned.1.call-start = ((), (), s32[]{:S(2)}) async-start(), calls=%async_computation.29 | async-start | bytes 1572864 | tf_op jit(solution)/shard_map/reduce_scatter | solution.py:310
  596.4 123.0 %all-reduce.27.cloned.1.call-start = ((), (), s32[]{:S(2)}) async-start(), calls=%async_computation.45 | async-start | bytes 4718592 | tf_op jit(solution)/shard_map/psum | solution.py:44
  596.6 5.9 copy-start.22
  596.6 5.9 copy-start.31
  609.6 9.1 copy-start.53
  623.4 139.2 %reduce-scatter.40.cloned.1.call-start = ((), (), s32[]{:S(2)}) async-start(), calls=%async_computation.39 | async-start | bytes 1990656 | tf_op jit(solution)/shard_map/reduce_scatter | solution.py:377
  626.4 178.8 %reduce-scatter.46.cloned.1.call-start = ((), (), s32[]{:S(2)}) async-start(), calls=%async_computation.42 | async-start | bytes 1990656 | tf_op jit(solution)/shard_map/reduce_scatter | solution.py:380
  630.3 218.1 %reduce-scatter.32.cloned.1.call-start = ((), (), s32[]{:S(2)}) async-start(), calls=%async_computation.35 | async-start | bytes 1990656 | tf_op jit(solution)/shard_map/reduce_scatter | solution.py:371
  633.3 258.3 %reduce-scatter.34.cloned.1.call-start = ((), (), s32[]{:S(2)}) async-start(), calls=%async_computation.36 | async-start | bytes 1990656 | tf_op jit(solution)/shard_map/reduce_scatter | solution.py:372
  636.5 298.6 %reduce-scatter.36.cloned.1.call-start = ((), (), s32[]{:S(2)}) async-start(), calls=%async_computation.37 | async-start | bytes 1990656 | tf_op jit(solution)/shard_map/reduce_scatter | solution.py:373
  639.6 338.7 %reduce-scatter.38.cloned.1.call-start = ((), (), s32[]{:S(2)}) async-start(), calls=%async_computation.38 | async-start | bytes 1990656 | tf_op jit(solution)/shard_map/reduce_scatter | solution.py:374
  643.6 378.0 %reduce-scatter.24.cloned.1.call-start = ((), (), s32[]{:S(2)}) async-start(), calls=%async_computation.31 | async-start | bytes 1990656 | tf_op jit(solution)/shard_map/reduce_scatter | solution.py:366
  647.3 417.7 %reduce-scatter.30.cloned.1.call-start = ((), (), s32[]{:S(2)}) async-start(), calls=%async_computation.34 | async-start | bytes 1990656 | tf_op jit(solution)/shard_map/reduce_scatter | solution.py:369
  651.1 457.3 %reduce-scatter.26.cloned.1.call-start = ((), (), s32[]{:S(2)}) async-start(), calls=%async_computation.32 | async-start | bytes 1990656 | tf_op jit(solution)/shard_map/reduce_scatter | solution.py:367
  654.2 497.4 %reduce-scatter.28.cloned.1.call-start = ((), (), s32[]{:S(2)}) async-start(), calls=%async_computation.33 | async-start | bytes 1990656 | tf_op jit(solution)/shard_map/reduce_scatter | solution.py:368
  657.3 555.2 %reduce-scatter.48.cloned.1.call-start = ((), (), s32[]{:S(2)}) async-start(), calls=%async_computation.43 | async-start | bytes 5971968 | tf_op jit(solution)/shard_map/reduce_scatter | solution.py:381
  663.7 610.0 %reduce-scatter.50.cloned.1.call-start = ((), (), s32[]{:S(2)}) async-start(), calls=%async_computation.44 | async-start | bytes 5971968 | tf_op jit(solution)/shard_map/reduce_scatter | solution.py:382
  670.8 660.7 %reduce-scatter.42.cloned.1.call-start = ((), (), s32[]{:S(2)}) async-start(), calls=%async_computation.40 | async-start | bytes 5308416 | tf_op jit(solution)/shard_map/reduce_scatter | solution.py:378
  675.2 714.7 %reduce-scatter.44.cloned.1.call-start = ((), (), s32[]{:S(2)}) async-start(), calls=%async_computation.41 | async-start | bytes 5308416 | tf_op jit(solution)/shard_map/reduce_scatter | solution.py:379
  679.6 39.7 %copy-start.105 = (f32[512]{0:T(512)S(1)}, f32[512]{0:T(512)}, u32[]{:S(2)}) copy-start(f32[512]{0:T(512)} %copy-done.104) | copy-start | bytes 6148
  679.6 39.7 %copy-start.107 = (f32[512]{0:T(512)S(1)}, f32[512]{0:T(512)}, u32[]{:S(2)}) copy-start(f32[512]{0:T(512)} %copy-done.106) | copy-start | bytes 6148
  679.6 42.4 %copy-start.20 = (bf16[1,8,2,32,1152]{4,3,2,1,0:T(8,128)(2,1)S(1)}, bf16[1,8,2,32,1152]{4,3,2,1,0:T(8,128)(2,1)}, u32[]{:S(2)}) copy-start(bf16[1,8,2,32,1152]{4,3,2,1,0:T(8,128)(2,1)} %param.26) | copy-start | bytes 3538948
  679.7 42.3 %copy-start.121 = (f32[1152]{0:T(1024)S(1)}, f32[1152]{0:T(1024)}, u32[]{:S(2)}) copy-start(f32[1152]{0:T(1024)} %get-tuple-element.45) | copy-start | bytes 13828
  679.7 42.3 %copy-start.110 = (f32[1152]{0:T(1024)S(1)}, f32[1152]{0:T(1024)}, u32[]{:S(2)}) copy-start(f32[1152]{0:T(1024)} %get-tuple-element.33) | copy-start | bytes 13828
  679.7 42.3 %copy-start.109 = (f32[1152]{0:T(1024)S(1)}, f32[1152]{0:T(1024)}, u32[]{:S(2)}) copy-start(f32[1152]{0:T(1024)} %get-tuple-element.25) | copy-start | bytes 13828
  679.7 42.3 %copy-start.88 = (f32[1152]{0:T(1024)S(1)}, f32[1152]{0:T(1024)}, u32[]{:S(2)}) copy-start(f32[1152]{0:T(1024)} %get-tuple-element.55) | copy-start | bytes 13828
  679.7 42.3 %copy-start.127 = (pred[512]{0:T(512)(128)(4,1)S(1)}, pred[512]{0:T(512)(128)(4,1)}, u32[]{:S(2)}) copy-start(pred[512]{0:T(512)(128)(4,1)} %broadcast_in_dim.47) | copy-start | bytes 1540
  679.7 785.0 %reduce-scatter.22.cloned.1.call-start = ((), (), s32[]{:S(2)}) async-start(), calls=%async_computation.30 | async-start | bytes 9289728 | tf_op jit(solution)/shard_map/reduce_scatter | solution.py:362
  729.0 30.0 %copy-start.29 = (bf16[512,1152]{1,0:T(8,128)(2,1)S(1)}, bf16[512,1152]{1,0:T(8,128)(2,1)}, u32[]{:S(2)}) copy-start(bf16[512,1152]{1,0:T(8,128)(2,1)} %get-tuple-element.40) | copy-start | bytes 3538948
  (98 other events, 216.8 us)
Sparse Core Ops, SparseCore 0:
  9.6 16.5 all-gather.15
  89.2 54.1 all-reduce.14
  145.0 10.4 all-gather.17
  156.9 12.1 all-gather.19
  186.6 55.6 all-reduce.16
  243.7 10.9 all-gather.23
  257.1 57.0 all-reduce.18
  315.7 10.9 all-gather.21
  338.2 57.0 all-reduce.20
  407.9 55.4 all-reduce.22
  516.9 55.4 all-reduce.24
  591.3 8.0 reduce-scatter.17
  601.7 9.6 reduce-scatter.19
  623.5 95.8 all-reduce.26
  723.1 38.7 reduce-scatter.39
  765.7 39.3 reduce-scatter.45
  809.0 39.4 reduce-scatter.31
  852.2 39.3 reduce-scatter.33
  895.6 39.3 reduce-scatter.35
  938.8 39.4 reduce-scatter.37
  982.2 39.3 reduce-scatter.23
  1025.6 39.3 reduce-scatter.29
  1068.9 39.3 reduce-scatter.25
  1112.2 39.4 reduce-scatter.27
  1155.6 56.9 reduce-scatter.47
  1216.8 56.9 reduce-scatter.49
  1277.6 53.8 reduce-scatter.41
  1335.9 53.8 reduce-scatter.43
  1394.1 70.6 reduce-scatter.21
where the time goes:
time: 1480 us; the launch traced here: 1470 us
  waiting for transfers between devices  1040 us (70%)
  matrix products  149 us (10%)
  local copies, waits for them, and re-layouts  131 us (9%)
  blocking collectives  77.3 us (5%)
  other arithmetic  53.4 us (4%)
  between operations  20.1 us (1%)
    psum x7, waiting for transfers between devices, over_heads(): lax.psum(partial_sum.astype(jnp.bfloat16), 'tensor').astype(jnp.float32)  325 us
    reduce_scatter x1, waiting for transfers between devices, on_device(): lax.psum_scatter(modulation_weight_grad, ('narrow', 'wide'), scatter_dime...  74.9 us
    reduce_scatter x1, waiting for transfers between devices, on_device(): lax.psum_scatter(feed_down_grad, ('narrow', 'wide'), scatter_dimension=0,...  61.2 us
    reduce_scatter x1, waiting for transfers between devices, on_device(): lax.psum_scatter(feed_up_grad, ('narrow', 'wide'), scatter_dimension=0, t...  60.9 us
    reduce_scatter x1, waiting for transfers between devices, on_device(): lax.psum_scatter(prompt_value_grad, ('narrow', 'wide'), scatter_dimension...  58.3 us
    reduce_scatter x1, waiting for transfers between devices, on_device(): lax.psum_scatter(prompt_key_grad, ('narrow', 'wide'), scatter_dimension=0...  57.8 us
    dot_general x14, matrix products, outer_sum(): lax.dot_general(left, right, CONTRACT_FIRST, preferred_element_type=jnp.f...  50.2 us
    unnamed x2, blocking collectives  45 us
  transfers between devices with their start and end apart: 29, of which 22 were waited for; matrix products, arithmetic and copies ran while one was open for 13% of the time, Pallas kernels for 0%

commit v1 on v0

--- a/solution.py
+++ b/solution.py
@@ -1,15 +1,1313 @@
+import functools
 import math
 
 import jax
 import jax.numpy as jnp
 from jax import lax
+from jax.experimental import pallas as pl
+from jax.experimental.pallas import tpu as pltpu
 from jax.sharding import PartitionSpec as P
 
 HEAD_DIM = 72
-
-
+LANES = 128
 EPSILON = 1e-06
 NEGATIVE = -1e30
+NARROW, WIDE, TENSOR = "narrow", "wide", "tensor"
+COLS = "cols"
+MESH_ID = pl.DeviceIdType.MESH
+F32 = jnp.float32
+BF16 = jnp.bfloat16
+VMEM = pltpu.VMEM
+VM = pl.BlockSpec(memory_space=pltpu.VMEM)
+ANY = pl.BlockSpec(memory_space=pl.ANY)
+DMA = pltpu.SemaphoreType.DMA
+
+
+def dot(left, right):
+    return jnp.dot(left, right, preferred_element_type=F32)
+
+
+def dot_tr(left, right):
+    return lax.dot_general(left, right, (((1,), (1,)), ((), ())), preferred_element_type=F32)
+
+
+def dot_outer(left, right):
+    return lax.dot_general(left, right, (((0,), (0,)), ((), ())), preferred_element_type=F32)
+
+
+def norm_tile(values):
+    center = values - jnp.mean(values, -1, keepdims=True)
+    inverse = lax.rsqrt(jnp.mean(center * center, -1, keepdims=True) + EPSILON)
+    return center * inverse, inverse
+
+
+def norm_pull(normed, inverse, incoming):
+    return inverse * (
+        incoming
+        - jnp.mean(incoming, -1, keepdims=True)
+        - normed * jnp.mean(incoming * normed, -1, keepdims=True)
+    )
+
+
+def softmax_tile(scores):
+    exponent = jnp.exp(scores - jnp.max(scores, -1, keepdims=True))
+    return exponent / jnp.sum(exponent, -1, keepdims=True)
+
+
+class Place:
+    def __init__(self, sizes):
+        self.sizes = sizes
+        self.n = lax.axis_index(NARROW)
+        self.w = lax.axis_index(WIDE)
+        self.t = lax.axis_index(TENSOR)
+
+    def tensor_peer(self, step):
+        return lax.rem(self.t + step, self.sizes[TENSOR])
+
+    def over_tensor(self, step):
+        return (self.n, self.w, self.tensor_peer(step))
+
+    def sibling(self):
+        return (self.n, 1 - self.w, self.t)
+
+    def over_narrow(self, peer):
+        return (peer, self.w, self.t)
+
+
+def greet(partners):
+    barrier = pltpu.get_barrier_semaphore()
+    for partner in partners:
+        pl.semaphore_signal(barrier, inc=1, device_id=partner, device_id_type=MESH_ID)
+    pl.semaphore_wait(barrier, len(partners))
+
+
+def send(source, target, send_sem, recv_sem, partner):
+    copy = pltpu.make_async_remote_copy(
+        src_ref=source,
+        dst_ref=target,
+        send_sem=send_sem,
+        recv_sem=recv_sem,
+        device_id=partner,
+        device_id_type=MESH_ID,
+    )
+    copy.start()
+    return copy
+
+
+class Ring:
+    def __init__(self, place, quarter, send_sems, recv_sems):
+        self.place, self.quarter = place, quarter
+        self.send_sems, self.recv_sems = send_sems, recv_sems
+        self.peers = place.sizes[TENSOR] - 1
+        self.used = 0
+
+    def take(self):
+        self.used += 1
+        return self.used - 1
+
+    def scatter(self, partial, landing):
+        slot = self.take()
+        copies = []
+        for step in (2, 1, 3) if self.peers == 3 else range(1, self.peers + 1):
+            rows = pl.ds(
+                pl.multiple_of(self.place.tensor_peer(step) * self.quarter, self.quarter),
+                self.quarter,
+            )
+            copies.append(
+                send(
+                    partial.at[rows],
+                    landing.at[step - 1],
+                    self.send_sems.at[slot, step - 1],
+                    self.recv_sems.at[slot, step - 1],
+                    self.place.over_tensor(step),
+                )
+            )
+        return copies
+
+    def gather(self, own):
+        slot = self.take()
+        return [
+            send(
+                own,
+                own,
+                self.send_sems.at[slot, step - 1],
+                self.recv_sems.at[slot, step - 1],
+                self.place.over_tensor(step),
+            )
+            for step in ((2, 1, 3) if self.peers == 3 else range(1, self.peers + 1))
+        ]
+
+
+def wait_all(copies):
+    for copy in copies:
+        copy.wait()
+
+
+def summed(partial, landing, rows, peers):
+    total = partial[rows].astype(F32)
+    for peer in range(peers):
+        total = total + landing[peer].astype(F32)
+    return total
+
+
+def modulation_kernel(sizes, condition, weight, shared, mine, landing, send_sems, recv_sems):
+    place = Place(sizes)
+    partners = []
+    for dw in range(sizes[WIDE]):
+        for dt in range(sizes[TENSOR]):
+            if dw or dt:
+                partners.append(
+                    (
+                        place.n,
+                        lax.rem(place.w + dw, sizes[WIDE]),
+                        lax.rem(place.t + dt, sizes[TENSOR]),
+                    )
+                )
+    greet(partners)
+    mine[0] = dot(condition[...], weight[...])[0:1]
+    slot = place.w * sizes[TENSOR] + place.t
+    copies = [
+        send(mine.at[0], landing.at[slot], send_sems.at[i], recv_sems.at[i], partner)
+        for i, partner in enumerate(partners)
+    ]
+    landing[slot] = mine[0]
+    wait_all(copies)
+    shared[...] = landing[...]
+
+
+def modulation_call(sizes, condition, weight):
+    group = sizes[WIDE] * sizes[TENSOR]
+    width = weight.shape[1]
+    return pl.pallas_call(
+        functools.partial(modulation_kernel, sizes),
+        name="modulation",
+        out_shape=jax.ShapeDtypeStruct((group, 1, width), F32),
+        in_specs=[VM, VM],
+        out_specs=VM,
+        scratch_shapes=[
+            VMEM((1, 1, width), F32),
+            VMEM((group, 1, width), F32),
+            DMA((group - 1,)),
+            DMA((group - 1,)),
+        ],
+        compiler_params=pltpu.CompilerParams(collective_id=0, has_side_effects=True),
+    )(condition, weight)
+
+
+def forward_kernel(
+    sizes,
+    frames,
+    vectors,
+    key_live,
+    word_live,
+    spread,
+    prompt,
+    *refs,
+):
+    weights = refs[:12]
+    (
+        h1, q1, side, o1, h2, q2, o2, h3, q3, kv3, o3, h4,
+        a1_own, a2_own, x3_own, n2_own, n3_own, n4_own, inverses,
+    ) = refs[12:31]
+    (
+        full, full_prompt, wide_context, partial, landing, residual, group_mask,
+        local_sems, side_send, side_recv, kv_send, kv_recv, ring_send, ring_recv,
+    ) = refs[31:]
+    place = Place(sizes)
+    peers = sizes[TENSOR] - 1
+    frame_count, chunks, cols, width = frames.shape
+    rows = frame_count * cols
+    quarter = rows // sizes[TENSOR]
+    own_frames = frame_count // sizes[TENSOR]
+    heads = spread.shape[1] // LANES
+    scale = 1.0 / math.sqrt(HEAD_DIM)
+    ring = Ring(place, quarter, ring_send, ring_recv)
+    greet([place.sibling()] + [place.over_tensor(step) for step in range(1, peers + 1)])
+
+    def fetch(i):
+        half = weights[i].shape[0]
+        spot = pl.ds(pl.multiple_of(place.w * half, half), half)
+        target = full.at[i, spot] if i < 10 else full_prompt.at[i - 10, spot]
+        local = pltpu.make_async_copy(weights[i], target, local_sems.at[i])
+        local.start()
+        return [local, send(weights[i], target, side_send.at[i], side_recv.at[i], place.sibling())]
+
+    pending = {i: fetch(i) for i in (0, 1, 2, 3)}
+
+    def ready(*which):
+        for i in which:
+            wait_all(pending.pop(i))
+
+    @pl.loop(0, frame_count)
+    def _(f):
+        for r in range(chunks):
+            normed, _ = norm_tile(frames[f, r].astype(F32))
+            h1[pl.ds(pl.multiple_of(r * rows + f * cols, cols), cols)] = (
+                normed * vectors[1:2] + vectors[0:1]
+            ).astype(BF16)
+
+    row_id = lax.broadcasted_iota(jnp.int32, (rows, rows), 0)
+    col_id = lax.broadcasted_iota(jnp.int32, (rows, rows), 1)
+    group_mask[...] = jnp.where(
+        lax.rem(row_id, cols) == lax.rem(col_id, cols),
+        jnp.broadcast_to(key_live[0:1], (rows, rows)),
+        0.0,
+    )
+
+    def project(source, spot, weight, out, index):
+        narrow = dot(source[spot], full[weight]).astype(BF16)
+        out[index, spot] = dot(narrow, spread[...]).astype(BF16)
+
+    def chunk_rows(r):
+        return pl.ds(r * rows, rows)
+
+    ready(0, 1, 2)
+
+    @pl.loop(0, 3)
+    def _(i):
+        for r in range(chunks):
+            project(h1, chunk_rows(r), i, q1, i)
+
+    kv_copies = [
+        send(q1.at[1 + j], side.at[j], kv_send.at[j], kv_recv.at[j], place.sibling())
+        for j in range(2)
+    ]
+    for i in (4, 5, 6, 7, 10, 11, 8, 9):
+        pending[i] = fetch(i)
+    wait_all(kv_copies)
+
+    @pl.loop(0, frame_count)
+    def _(f):
+        spots = [
+            pl.ds(pl.multiple_of(r * rows + f * cols, cols), cols) for r in range(chunks)
+        ]
+        queries = jnp.concatenate([q1[0, spot] for spot in spots], 0)
+        keys = jnp.concatenate(
+            [q1[1, spot] for spot in spots] + [side[0, spot] for spot in spots], 0
+        )
+        values = jnp.concatenate(
+            [q1[2, spot] for spot in spots] + [side[1, spot] for spot in spots], 0
+        )
+        for h in range(heads):
+            lanes = slice(h * LANES, (h + 1) * LANES)
+            attend = softmax_tile(dot_tr(queries[:, lanes], keys[:, lanes]) * scale)
+            context = dot(attend.astype(BF16), values[:, lanes]).astype(BF16)
+            for r in range(chunks):
+                wide_context[spots[r], lanes] = context[r * cols : (r + 1) * cols]
+
+    def emit(r, out, weight):
+        spot = chunk_rows(r)
+        out[spot] = dot_tr(wide_context[spot], spread[...]).astype(BF16)
+        partial[r] = dot_tr(out[spot], full[weight]).astype(BF16)
+        return ring.scatter(partial.at[r], landing.at[ring.used])
+
+    own = pl.ds(pl.multiple_of(place.t * quarter, quarter), quarter)
+
+    def own_rows(r):
+        return pl.ds(pl.multiple_of(r * rows + place.t * quarter, quarter), quarter)
+
+    def kept(r):
+        return pl.ds(r * quarter, quarter)
+
+    def branch(r, stage):
+        return summed(partial.at[r], landing.at[stage], own, peers)
+
+    ready(3)
+    scatters = []
+    for r in range(chunks):
+        scatters.append((ring.used, emit(r, o1, 3)))
+
+    ready(10, 11)
+    kv3[...] = jnp.zeros_like(kv3)
+    for j in range(2):
+        narrow = dot(prompt[...], full_prompt[j]).astype(BF16)
+        kv3[j, 0 : prompt.shape[0]] = dot(narrow, spread[...]).astype(BF16)
+
+    gathers = []
+    for r in range(chunks):
+        stage, copies = scatters[r]
+        wait_all(copies)
+        branch_one = branch(r, stage)
+        a1_own[kept(r)] = branch_one
+        x_own = frames[pl.ds(place.t * own_frames, own_frames), r].reshape(quarter, width)
+        after = x_own.astype(F32) + vectors[2:3] * branch_one
+        normed, inverse = norm_tile(after)
+        residual[kept(r)] = after
+        n2_own[kept(r)] = normed
+        inverses[0, kept(r)] = jnp.broadcast_to(inverse, (quarter, LANES))
+        h2[own_rows(r)] = (normed * vectors[6:7]).astype(BF16)
+        gathers.append(ring.gather(h2.at[own_rows(r)]))
+
+    ready(4, 5, 6, 7)
+    scatters = []
+    for r in range(chunks):
+        wait_all(gathers[r])
+        spot = chunk_rows(r)
+
+        @pl.loop(0, 3)
+        def _(i):
+            project(h2, spot, 4 + i, q2, i)
+
+        @pl.loop(0, heads)
+        def _(h):
+            lanes = pl.ds(pl.multiple_of(h * LANES, LANES), LANES)
+            scores = dot_tr(q2[0, spot, lanes], q2[1, spot, lanes]) * scale
+            attend = softmax_tile(jnp.where(group_mask[...] > 0.5, scores, NEGATIVE))
+            wide_context[spot, lanes] = dot(attend.astype(BF16), q2[2, spot, lanes]).astype(BF16)
+
+        scatters.append((ring.used, emit(r, o2, 7)))
+
+    gathers = []
+    for r in range(chunks):
+        stage, copies = scatters[r]
+        wait_all(copies)
+        branch_two = branch(r, stage)
+        a2_own[kept(r)] = branch_two
+        after = residual[kept(r)] + vectors[7:8] * branch_two
+        normed, inverse = norm_tile(after)
+        residual[kept(r)] = after
+        n3_own[kept(r)] = normed
+        inverses[1, kept(r)] = jnp.broadcast_to(inverse, (quarter, LANES))
+        h3[own_rows(r)] = (normed * vectors[8:9]).astype(BF16)
+        gathers.append(ring.gather(h3.at[own_rows(r)]))
+
+    ready(8, 9)
+    scatters = []
+    for r in range(chunks):
+        wait_all(gathers[r])
+        spot = chunk_rows(r)
+        narrow = dot(h3[spot], full[8]).astype(BF16)
+        q3[spot] = dot(narrow, spread[...]).astype(BF16)
+
+        @pl.loop(0, heads)
+        def _(h):
+            lanes = pl.ds(pl.multiple_of(h * LANES, LANES), LANES)
+            scores = dot_tr(q3[spot, lanes], kv3[0, :, lanes]) * scale
+            attend = softmax_tile(jnp.where(word_live[0:1] > 0.5, scores, NEGATIVE))
+            wide_context[spot, lanes] = dot(attend.astype(BF16), kv3[1, :, lanes]).astype(BF16)
+
+        scatters.append((ring.used, emit(r, o3, 9)))
+
+    gathers = []
+    for r in range(chunks):
+        stage, copies = scatters[r]
+        wait_all(copies)
+        after = residual[kept(r)] + branch(r, stage)
+        normed, inverse = norm_tile(after)
+        x3_own[kept(r)] = after
+        n4_own[kept(r)] = normed
+        inverses[2, kept(r)] = jnp.broadcast_to(inverse, (quarter, LANES))
+        h4[own_rows(r)] = (normed * vectors[4:5] + vectors[3:4]).astype(BF16)
+        gathers.append(ring.gather(h4.at[own_rows(r)]))
+    for copies in gathers:
+        wait_all(copies)
+
+
+def forward_call(sizes, frames, vectors, key_live, word_live, spread, prompt, weights):
+    frame_count, chunks, cols, width = frames.shape
+    rows = frame_count * cols
+    tokens = rows * chunks
+    head_width, padded = spread.shape
+    quarter = rows // sizes[TENSOR]
+    peers = sizes[TENSOR] - 1
+    kept = quarter * chunks
+    full_rows = weights[0].shape[0] * sizes[WIDE]
+    prompt_width = weights[10].shape[0] * sizes[WIDE]
+    stages = 6 * chunks
+    s = jax.ShapeDtypeStruct
+    wide_act, heads_act = s((tokens, width), BF16), s((tokens, head_width), BF16)
+    triple, own = s((3, tokens, padded), BF16), s((kept, width), F32)
+    outs = [
+        wide_act, triple, s((2, tokens, padded), BF16), heads_act,
+        wide_act, triple, heads_act,
+        wide_act, s((tokens, padded), BF16), s((2, LANES, padded), BF16), heads_act,
+        wide_act, own, own, own, own, own, own, s((3, kept, LANES), F32),
+    ]
+    return pl.pallas_call(
+        functools.partial(forward_kernel, sizes),
+        name="forward",
+        out_shape=outs,
+        in_specs=[VM] * 6 + [ANY] * 12,
+        out_specs=[VM] * len(outs),
+        scratch_shapes=[
+            VMEM((10, full_rows, head_width), BF16),
+            VMEM((2, prompt_width, head_width), BF16),
+            VMEM((tokens, padded), BF16),
+            VMEM((chunks, rows, width), BF16),
+            VMEM((stages, peers, quarter, width), BF16),
+            VMEM((kept, width), F32),
+            VMEM((rows, rows), F32),
+            DMA((12,)), DMA((12,)), DMA((12,)), DMA((2,)), DMA((2,)),
+            DMA((stages, peers)), DMA((stages, peers)),
+        ],
+        compiler_params=pltpu.CompilerParams(
+            collective_id=1, has_side_effects=True, vmem_limit_bytes=60 << 20
+        ),
+    )(frames, vectors, key_live, word_live, spread, prompt, *weights)
+
+
+def prepare(sizes, frames, timestep, clip_lengths, text_lengths, modulation_weight,
+            modulation_bias, time_gain, time_gate, cross_gain, head_width):
+    frame_count, width = frames.shape[1], frames.shape[4]
+    cols = frames.shape[3]
+    half_width = width // 2
+    frequency = jnp.exp(-math.log(10000.0) * jnp.arange(half_width, dtype=F32) / half_width)
+    angles = timestep[0].astype(F32) * frequency
+    condition = jax.nn.silu(jnp.concatenate([jnp.cos(angles), jnp.sin(angles)])).astype(BF16)
+    mine = lax.dynamic_slice_in_dim(
+        condition, lax.axis_index(WIDE) * modulation_weight.shape[0], modulation_weight.shape[0]
+    )
+    parts = modulation_call(
+        sizes, jnp.broadcast_to(mine[None], (16, mine.shape[0])), modulation_weight
+    )
+    parts = parts.reshape(sizes[WIDE], -1)
+    modulation = (jnp.sum(parts, 0) + modulation_bias).reshape(6, width)
+    vectors = jnp.stack(
+        [
+            modulation[0], 1.0 + modulation[1], modulation[2],
+            modulation[3], 1.0 + modulation[4], modulation[5],
+            time_gain, jnp.tanh(time_gate), cross_gain,
+        ]
+    )
+    live = jnp.arange(frame_count) < clip_lengths[0]
+    key_live = jnp.repeat(live, cols).astype(F32)[None]
+    word_live = (jnp.arange(LANES) < text_lengths[0]).astype(F32)[None]
+    heads = head_width // HEAD_DIM
+    padded = jnp.arange(heads * LANES)
+    source = jnp.where(
+        padded % LANES < HEAD_DIM, padded // LANES * HEAD_DIM + padded % LANES, -1
+    )
+    spread = (jnp.arange(head_width)[:, None] == source[None]).astype(BF16)
+    return condition, vectors, live, key_live, word_live, spread
+
+
+def over_columns(width, tile, body):
+    whole = width // tile
+
+    @pl.loop(0, whole)
+    def _(j):
+        body(pl.ds(pl.multiple_of(j * tile, tile), tile))
+
+    if width % tile:
+        body(pl.ds(whole * tile, width % tile))
+
+
+GELU_C = math.sqrt(2.0 / math.pi)
+
+
+def mlp_kernel(
+    sizes,
+    h4, cotangent, vectors, live, n4_own, inverses, x3_own, up_half, down_half,
+    output, e3, g3_own, up_grad, down_grad, sums,
+    up, down, e4, hidden, pre_grad, partial, landing,
+    local_sems, side_send, side_recv, ring_send, ring_recv,
+):
+    place = Place(sizes)
+    peers = sizes[TENSOR] - 1
+    frame_count, chunks, cols, width = cotangent.shape
+    rows = frame_count * cols
+    quarter = rows // sizes[TENSOR]
+    own_frames = frame_count // sizes[TENSOR]
+    ring = Ring(place, quarter, ring_send, ring_recv)
+    greet([place.sibling()] + [place.over_tensor(step) for step in range(1, peers + 1)])
+    copies = []
+    for i, (source, target) in enumerate(((up_half, up), (down_half, down))):
+        half = source.shape[0]
+        spot = pl.ds(pl.multiple_of(place.w * half, half), half)
+        local = pltpu.make_async_copy(source, target.at[spot], local_sems.at[i])
+        local.start()
+        copies += [
+            local,
+            send(source, target.at[spot], side_send.at[i], side_recv.at[i], place.sibling()),
+        ]
+
+    @pl.loop(0, frame_count)
+    def _(f):
+        for r in range(chunks):
+            e4[pl.ds(pl.multiple_of(r * rows + f * cols, cols), cols)] = (
+                vectors[5:6] * (cotangent[f, r].astype(F32) * live[f, 0:1, 0:1])
+            ).astype(BF16)
+
+    wait_all(copies)
+    scatters = []
+    for r in range(chunks):
+        spot = pl.ds(r * rows, rows)
+
+        def act(lanes):
+            pre = dot(h4[spot], up[:, lanes])
+            grad = dot(e4[spot], down[:, lanes])
+            inner = jnp.tanh(GELU_C * (pre + 0.044715 * pre * pre * pre))
+            gate = 0.5 * (1.0 + inner)
+            hidden[spot, lanes] = (pre * gate).astype(BF16)
+            slope = gate + 0.5 * pre * (1.0 - inner * inner) * (
+                GELU_C * (1.0 + 3.0 * 0.044715 * pre * pre)
+            )
+            pre_grad[spot, lanes] = (grad * slope).astype(BF16)
+
+        over_columns(up.shape[1], 256, act)
+        partial[r] = dot_tr(pre_grad[spot], up[...]).astype(BF16)
+        scatters.append((ring.used, ring.scatter(partial.at[r], landing.at[ring.used])))
+
+    for r in range(chunks):
+        spot = pl.ds(r * rows, rows)
+        partial[chunks + r] = dot_tr(hidden[spot], down[...]).astype(BF16)
+
+    def down_tile(lanes):
+        down_grad[:, lanes] = dot_outer(e4[...], hidden[:, lanes]).astype(BF16)
+
+    def up_tile(lanes):
+        up_grad[:, lanes] = dot_outer(h4[...], pre_grad[:, lanes]).astype(BF16)
+
+    over_columns(up.shape[1], 256, down_tile)
+
+    own = pl.ds(pl.multiple_of(place.t * quarter, quarter), quarter)
+    own_spot = pl.ds(place.t * own_frames, own_frames)
+    shift_sum = jnp.zeros((1, width), F32)
+    scale_sum = jnp.zeros((1, width), F32)
+    gate_sum = jnp.zeros((1, width), F32)
+
+    def own_live(r):
+        pieces = []
+        for f in range(own_frames):
+            pieces.append(
+                jnp.broadcast_to(live[place.t * own_frames + f, 0:1, 0:1], (cols, 1))
+            )
+        return jnp.concatenate(pieces, 0)
+
+    def own_upstream(r):
+        return cotangent[own_spot, r].reshape(quarter, width).astype(F32) * own_live(r)
+
+    gathers = []
+    for r in range(chunks):
+        kept = pl.ds(r * quarter, quarter)
+        stage, copies = scatters[r]
+        wait_all(copies)
+        grad = summed(partial.at[r], landing.at[stage], own, peers)
+        normed = n4_own[kept]
+        shift_sum = shift_sum + jnp.sum(grad, 0, keepdims=True)
+        scale_sum = scale_sum + jnp.sum(grad * normed, 0, keepdims=True)
+        upstream = own_upstream(r) + norm_pull(
+            normed, inverses[2, kept][:, 0:1], grad * vectors[4:5]
+        )
+        g3_own[kept] = upstream
+        rows_own = pl.ds(pl.multiple_of(r * rows + place.t * quarter, quarter), quarter)
+        e3[rows_own] = upstream.astype(BF16)
+        gathers.append(ring.gather(e3.at[rows_own]))
+    scatters = []
+    for r in range(chunks):
+        scatters.append((ring.used, ring.scatter(partial.at[chunks + r], landing.at[ring.used])))
+
+    over_columns(up.shape[1], 256, up_tile)
+
+    for r in range(chunks):
+        kept = pl.ds(r * quarter, quarter)
+        stage, copies = scatters[r]
+        wait_all(copies)
+        branch = summed(partial.at[chunks + r], landing.at[stage], own, peers)
+        gate_sum = gate_sum + jnp.sum(own_upstream(r) * branch, 0, keepdims=True)
+        after = (x3_own[kept] + vectors[5:6] * branch) * own_live(r)
+        output[own_spot, r] = after.astype(BF16).reshape(own_frames, cols, width)
+        gathers.append(ring.gather(output.at[own_spot, r]))
+    sums[...] = jnp.concatenate(
+        [shift_sum, scale_sum, gate_sum, jnp.zeros((5, width), F32)], 0
+    )
+    for copies in gathers:
+        wait_all(copies)
+
+
+def mlp_call(sizes, h4, cotangent, vectors, live, n4_own, inverses, x3_own, up_half, down_half):
+    frame_count, chunks, cols, width = cotangent.shape
+    rows = frame_count * cols
+    tokens = rows * chunks
+    quarter = rows // sizes[TENSOR]
+    peers = sizes[TENSOR] - 1
+    hidden = up_half.shape[1]
+    s = jax.ShapeDtypeStruct
+    stages = 4 * chunks
+    live = jnp.broadcast_to(live.astype(F32)[:, None, None], (frame_count, 8, LANES))
+    outs = [
+        s(cotangent.shape, BF16), s((tokens, width), BF16), s((quarter * chunks, width), F32),
+        s((width, hidden), BF16), s((width, hidden), BF16), s((8, width), F32),
+    ]
+    return pl.pallas_call(
+        functools.partial(mlp_kernel, sizes),
+        name="mlp",
+        out_shape=outs,
+        in_specs=[VM] * 7 + [ANY] * 2,
+        out_specs=[VM] * len(outs),
+        scratch_shapes=[
+            VMEM((width, hidden), BF16), VMEM((width, hidden), BF16),
+            VMEM((tokens, width), BF16), VMEM((tokens, hidden), BF16),
+            VMEM((tokens, hidden), BF16),
+            VMEM((2 * chunks, rows, width), BF16),
+            VMEM((stages, peers, quarter, width), BF16),
+            DMA((2,)), DMA((2,)), DMA((2,)), DMA((stages, peers)), DMA((stages, peers)),
+        ],
+        compiler_params=pltpu.CompilerParams(
+            collective_id=2, has_side_effects=True, vmem_limit_bytes=60 << 20
+        ),
+    )(h4, cotangent, vectors, live, n4_own, inverses, x3_own, up_half, down_half)
+
+
+class Reducer:
+    def __init__(self, place, source, mine, merged, received, sems):
+        self.place, self.source = place, source
+        self.mine, self.merged, self.received = mine, merged, received
+        self.local, self.side_send, self.side_recv, self.far_send, self.far_recv = sems
+        self.clips = place.sizes[NARROW]
+        self.block = mine.shape[1]
+
+    def rows(self, clip, core):
+        start = (clip * self.place.sizes[WIDE] + core) * self.block
+        return pl.ds(pl.multiple_of(start, self.block), self.block)
+
+    def split(self):
+        self.copies = []
+        for clip in range(self.clips):
+            local = pltpu.make_async_copy(
+                self.source.at[self.rows(clip, self.place.w)],
+                self.mine.at[clip],
+                self.local.at[clip],
+            )
+            local.start()
+            self.copies += [
+                local,
+                send(
+                    self.source.at[self.rows(clip, 1 - self.place.w)],
+                    self.merged.at[clip],
+                    self.side_send.at[clip],
+                    self.side_recv.at[clip],
+                    self.place.sibling(),
+                ),
+            ]
+
+    def spread(self):
+        wait_all(self.copies)
+        self.copies = []
+
+        @pl.loop(0, self.clips)
+        def _(clip):
+            self.merged[clip] = (
+                self.merged[clip].astype(F32) + self.mine[clip].astype(F32)
+            ).astype(BF16)
+
+        for step in (3, 1, 2) if self.clips == 4 else range(1, self.clips):
+            peer = lax.rem(self.place.n + step, self.clips)
+            self.copies.append(
+                send(
+                    self.merged.at[peer],
+                    self.received.at[step - 1],
+                    self.far_send.at[step - 1],
+                    self.far_recv.at[step - 1],
+                    self.place.over_narrow(peer),
+                )
+            )
+
+    def finish(self, out):
+        wait_all(self.copies)
+        total = self.merged[self.place.n].astype(F32)
+        for step in range(self.clips - 1):
+            total = total + self.received[step].astype(F32)
+        out[...] = total
+
+
+def reducer_scratch(sizes, jobs, block, width):
+    clips = sizes[NARROW]
+    return [
+        VMEM((jobs, clips, block, width), BF16),
+        VMEM((jobs, clips, block, width), BF16),
+        VMEM((jobs, clips - 1, block, width), BF16),
+        DMA((jobs, clips)), DMA((jobs, clips)), DMA((jobs, clips)),
+        DMA((jobs, clips - 1)), DMA((jobs, clips - 1)),
+    ]
+
+
+def reducers(place, sources, scratch):
+    mine, merged, received, *sems = scratch
+    return [
+        Reducer(
+            place, source, mine.at[i], merged.at[i], received.at[i], [sem.at[i] for sem in sems]
+        )
+        for i, source in enumerate(sources)
+    ]
+
+
+def all_partners(place):
+    sizes = place.sizes
+    return (
+        [place.sibling()]
+        + [place.over_tensor(step) for step in range(1, sizes[TENSOR])]
+        + [
+            place.over_narrow(lax.rem(place.n + step, sizes[NARROW]))
+            for step in range(1, sizes[NARROW])
+        ]
+    )
+
+
+def fetch_weights(place, halves, full, local_sems, side_send, side_recv):
+    pending = []
+    for i, half_ref in enumerate(halves):
+        half = half_ref.shape[0]
+        spot = pl.ds(pl.multiple_of(place.w * half, half), half)
+        local = pltpu.make_async_copy(half_ref, full.at[i, spot], local_sems.at[i])
+        local.start()
+        pending.append(
+            [
+                local,
+                send(half_ref, full.at[i, spot], side_send.at[i], side_recv.at[i], place.sibling()),
+            ]
+        )
+    return pending
+
+
+def attention_pull(queries, keys, values, context_grad, mask, scale):
+    scores = dot_tr(queries, keys) * scale
+    if mask is not None:
+        scores = jnp.where(mask, scores, NEGATIVE)
+    attend = softmax_tile(scores)
+    attend_grad = dot_tr(context_grad, values)
+    score_grad = (
+        attend * (attend_grad - jnp.sum(attend * attend_grad, -1, keepdims=True))
+    ).astype(BF16)
+    return (
+        dot(score_grad, keys) * scale,
+        dot_outer(score_grad, queries) * scale,
+        dot_outer(attend.astype(BF16), context_grad),
+    )
+
+
+def back_kernel(
+    sizes,
+    e3, g3_own, n3_own, n2_own, inverses, a2_own, vectors, key_live, word_live, spread,
+    h3, q3, kv3, o3, h2, q2, o2,
+    *refs,
+):
+    halves, gradients = refs[:6], refs[6:8]
+    g1_own, e1, query_out, value_out, word_grads, up_out, down_out, sums = refs[8:16]
+    (
+        full, wide_grad, wide_parts, narrow_parts, word_sums, word_side, e2, partial, landing,
+        group_mask, local_sems, side_send, side_recv, word_send, word_recv, ring_send, ring_recv,
+    ) = refs[16:33]
+    place = Place(sizes)
+    peers = sizes[TENSOR] - 1
+    tokens, width = e3.shape
+    chunks = tokens // group_mask.shape[0]
+    rows = tokens // chunks
+    cols = sizes[COLS]
+    quarter = rows // sizes[TENSOR]
+    heads = spread.shape[1] // LANES
+    scale = 1.0 / math.sqrt(HEAD_DIM)
+    ring = Ring(place, quarter, ring_send, ring_recv)
+    greet(all_partners(place))
+    pending = fetch_weights(place, halves, full, local_sems, side_send, side_recv)
+    feed = reducers(place, gradients, refs[33:])
+    for job in feed:
+        job.split()
+
+    row_id = lax.broadcasted_iota(jnp.int32, (rows, rows), 0)
+    col_id = lax.broadcasted_iota(jnp.int32, (rows, rows), 1)
+    group_mask[...] = jnp.where(
+        lax.rem(row_id, cols) == lax.rem(col_id, cols),
+        jnp.broadcast_to(key_live[0:1], (rows, rows)),
+        0.0,
+    )
+    own = pl.ds(pl.multiple_of(place.t * quarter, quarter), quarter)
+
+    def chunk_rows(r):
+        return pl.ds(r * rows, rows)
+
+    def own_rows(r):
+        return pl.ds(pl.multiple_of(r * rows + place.t * quarter, quarter), quarter)
+
+    def kept(r):
+        return pl.ds(r * quarter, quarter)
+
+    def head_lanes(h):
+        return pl.ds(pl.multiple_of(h * LANES, LANES), LANES)
+
+    def context_grad(source, spot, weight):
+        narrow = dot(source[spot], full[weight]).astype(BF16)
+        wide_grad[spot] = dot(narrow, spread[...]).astype(BF16)
+
+    word_sums[...] = jnp.zeros_like(word_sums)
+    wait_all(pending[0])
+    wait_all(pending[1])
+    scatters = []
+    for r in range(chunks):
+        spot = chunk_rows(r)
+        context_grad(e3, spot, 0)
+
+        @pl.loop(0, heads)
+        def _(h):
+            lanes = head_lanes(h)
+            query_grad, key_grad, value_grad = attention_pull(
+                q3[spot, lanes], kv3[0, :, lanes], kv3[1, :, lanes], wide_grad[spot, lanes],
+                word_live[0:1] > 0.5, scale,
+            )
+            wide_parts[0, spot, lanes] = query_grad.astype(BF16)
+            word_sums[0, :, lanes] += key_grad
+            word_sums[1, :, lanes] += value_grad
+
+        narrow_parts[0, spot] = dot_tr(wide_parts[0, spot], spread[...]).astype(BF16)
+        partial[r] = dot_tr(narrow_parts[0, spot], full[1]).astype(BF16)
+        scatters.append((ring.used, ring.scatter(partial.at[r], landing.at[ring.used])))
+    word_copy = send(word_sums, word_side, word_send, word_recv, place.sibling())
+    value_out[0] = dot_outer(e3[...], o3[...]).astype(BF16)
+    query_out[0] = dot_outer(h3[...], narrow_parts[0]).astype(BF16)
+    for job in feed:
+        job.spread()
+
+    gain_sum = jnp.zeros((1, width), F32)
+    gate_sum = jnp.zeros((1, width), F32)
+    time_sum = jnp.zeros((1, width), F32)
+    gathers = []
+    for r in range(chunks):
+        stage, copies = scatters[r]
+        wait_all(copies)
+        grad = summed(partial.at[r], landing.at[stage], own, peers)
+        normed = n3_own[kept(r)]
+        gain_sum = gain_sum + jnp.sum(grad * normed, 0, keepdims=True)
+        upstream = g3_own[kept(r)] + norm_pull(
+            normed, inverses[1, kept(r)][:, 0:1], grad * vectors[8:9]
+        )
+        g1_own[kept(r)] = upstream
+        gate_sum = gate_sum + jnp.sum(upstream * a2_own[kept(r)], 0, keepdims=True)
+        e2[own_rows(r)] = (vectors[7:8] * upstream).astype(BF16)
+        gathers.append(ring.gather(e2.at[own_rows(r)]))
+    word_copy.wait()
+    for j in range(2):
+        word_grads[j] = dot_tr(
+            (word_sums[j] + word_side[j]).astype(BF16), spread[...]
+        ).astype(BF16)
+
+    for copies in pending[2:]:
+        wait_all(copies)
+    scatters = []
+    for r in range(chunks):
+        spot = chunk_rows(r)
+        wait_all(gathers[r])
+        context_grad(e2, spot, 2)
+
+        @pl.loop(0, heads)
+        def _(h):
+            lanes = head_lanes(h)
+            parts = attention_pull(
+                q2[0, spot, lanes], q2[1, spot, lanes], q2[2, spot, lanes],
+                wide_grad[spot, lanes], group_mask[...] > 0.5, scale,
+            )
+            for i in range(3):
+                wide_parts[i, spot, lanes] = parts[i].astype(BF16)
+
+        @pl.loop(0, 3)
+        def _(i):
+            narrow_parts[i, spot] = dot_tr(wide_parts[i, spot], spread[...]).astype(BF16)
+
+        total = dot_tr(narrow_parts[0, spot], full[3])
+        for i in (1, 2):
+            total = total + dot_tr(narrow_parts[i, spot], full[3 + i])
+        partial[r] = total.astype(BF16)
+        scatters.append((ring.used, ring.scatter(partial.at[r], landing.at[ring.used])))
+    value_out[1] = dot_outer(e2[...], o2[...]).astype(BF16)
+
+    @pl.loop(0, 3)
+    def _(i):
+        query_out[1 + i] = dot_outer(h2[...], narrow_parts[i]).astype(BF16)
+
+    gathers = []
+    for r in range(chunks):
+        stage, copies = scatters[r]
+        wait_all(copies)
+        grad = summed(partial.at[r], landing.at[stage], own, peers)
+        normed = n2_own[kept(r)]
+        time_sum = time_sum + jnp.sum(grad * normed, 0, keepdims=True)
+        upstream = g1_own[kept(r)] + norm_pull(
+            normed, inverses[0, kept(r)][:, 0:1], grad * vectors[6:7]
+        )
+        g1_own[kept(r)] = upstream
+        e1[own_rows(r)] = (vectors[2:3] * upstream).astype(BF16)
+        gathers.append(ring.gather(e1.at[own_rows(r)]))
+    feed[0].finish(up_out)
+    feed[1].finish(down_out)
+    sums[...] = jnp.concatenate([gain_sum, gate_sum, time_sum, jnp.zeros((5, width), F32)], 0)
+    for copies in gathers:
+        wait_all(copies)
+
+
+def back_call(sizes, cols, acts, halves, gradients):
+    e3, spread = acts[0], acts[9]
+    tokens, width = e3.shape
+    key_live = acts[7]
+    rows = key_live.shape[1]
+    chunks = tokens // rows
+    quarter = rows // sizes[TENSOR]
+    peers = sizes[TENSOR] - 1
+    head_width, padded = spread.shape
+    full_rows = halves[0].shape[0] * sizes[WIDE]
+    hidden = gradients[0].shape[1]
+    block = width // (sizes[NARROW] * sizes[WIDE])
+    s = jax.ShapeDtypeStruct
+    stages = 4 * chunks
+    outs = [
+        s((quarter * chunks, width), F32), s((tokens, width), BF16),
+        s((4, width, head_width), BF16), s((2, width, head_width), BF16),
+        s((2, LANES, head_width), BF16),
+        s((block, hidden), F32), s((block, hidden), F32), s((8, width), F32),
+    ]
+    return pl.pallas_call(
+        functools.partial(back_kernel, {**sizes, COLS: cols}),
+        name="back",
+        out_shape=outs,
+        in_specs=[VM] * len(acts) + [ANY] * 8,
+        out_specs=[VM] * len(outs),
+        scratch_shapes=[
+            VMEM((6, full_rows, head_width), BF16),
+            VMEM((tokens, padded), BF16),
+            VMEM((3, tokens, padded), BF16),
+            VMEM((3, tokens, head_width), BF16),
+            VMEM((2, LANES, padded), F32), VMEM((2, LANES, padded), F32),
+            VMEM((tokens, width), BF16),
+            VMEM((chunks, rows, width), BF16),
+            VMEM((stages, peers, quarter, width), BF16),
+            VMEM((rows, rows), F32),
+            DMA((6,)), DMA((6,)), DMA((6,)), DMA(()), DMA(()),
+            DMA((stages, peers)), DMA((stages, peers)),
+        ]
+        + reducer_scratch(sizes, 2, block, hidden),
+        compiler_params=pltpu.CompilerParams(
+            collective_id=3, has_side_effects=True, vmem_limit_bytes=60 << 20
+        ),
+    )(*acts, *halves, *gradients)
+
+
+def space_kernel(
+    sizes,
+    e1, g1_own, frames, a1_own, vectors, spread, h1, q1, side, o1, prompt, word_grads,
+    *refs,
+):
+    halves, early_value, early_query = refs[:4], refs[4], refs[5]
+    frames_grad, early_out, space_out, prompt_out, sums = refs[6:11]
+    (
+        full, wide_grad, wide_parts, narrow_parts, key_sums, side_out, side_in, space_grads,
+        words, word_parts, partial, landing,
+        local_sems, side_send, side_recv, key_send, key_recv, word_send, word_recv,
+        ring_send, ring_recv,
+    ) = refs[11:32]
+    place = Place(sizes)
+    peers = sizes[TENSOR] - 1
+    clips = sizes[NARROW]
+    frame_count, chunks, cols, width = frames.shape
+    rows = frame_count * cols
+    tokens = rows * chunks
+    quarter = rows // sizes[TENSOR]
+    own_frames = frame_count // sizes[TENSOR]
+    heads = spread.shape[1] // LANES
+    half = chunks * cols
+    scale = 1.0 / math.sqrt(HEAD_DIM)
+    ring = Ring(place, quarter, ring_send, ring_recv)
+    greet(all_partners(place))
+    pending = fetch_weights(place, halves, full, local_sems, side_send, side_recv)
+    early_scratch, late_scratch = refs[32:40], refs[40:48]
+    sources = [early_value.at[0], early_query.at[0], early_value.at[1]] + [
+        early_query.at[1 + i] for i in range(3)
+    ]
+    early = reducers(place, sources, early_scratch)
+    late = reducers(place, [space_grads.at[i] for i in range(4)], late_scratch)
+    block = words.shape[2]
+    word_copies = []
+    for step in range(1, clips):
+        peer = lax.rem(place.n + step, clips)
+        lanes = pl.ds(
+            pl.multiple_of((peer * sizes[WIDE] + place.w) * block, block), block
+        )
+        for j, (source, target) in enumerate(
+            ((prompt.at[:, lanes], words.at[step]), (word_grads, word_parts.at[step]))
+        ):
+            word_copies.append(
+                send(
+                    source, target, word_send.at[step - 1, j], word_recv.at[step - 1, j],
+                    place.over_narrow(peer),
+                )
+            )
+    for job in early:
+        job.split()
+    mine = pl.ds(pl.multiple_of((place.n * sizes[WIDE] + place.w) * block, block), block)
+    words[0] = prompt[:, mine]
+    word_parts[0] = word_grads[...]
+    own = pl.ds(pl.multiple_of(place.t * quarter, quarter), quarter)
+    own_spot = pl.ds(place.t * own_frames, own_frames)
+
+    for copies in pending:
+        wait_all(copies)
+    for r in range(chunks):
+        spot = pl.ds(r * rows, rows)
+        narrow = dot(e1[spot], full[0]).astype(BF16)
+        wide_grad[spot] = dot(narrow, spread[...]).astype(BF16)
+
+    @pl.loop(0, frame_count)
+    def _(f):
+        spots = [
+            pl.ds(pl.multiple_of(r * rows + f * cols, cols), cols) for r in range(chunks)
+        ]
+        queries = jnp.concatenate([q1[0, spot] for spot in spots], 0)
+        grads = jnp.concatenate([wide_grad[spot] for spot in spots], 0)
+        keys = jnp.concatenate(
+            [q1[1, spot] for spot in spots] + [side[0, spot] for spot in spots], 0
+        )
+        values = jnp.concatenate(
+            [q1[2, spot] for spot in spots] + [side[1, spot] for spot in spots], 0
+        )
+        for h in range(heads):
+            lanes = slice(h * LANES, (h + 1) * LANES)
+            parts = attention_pull(
+                queries[:, lanes], keys[:, lanes], values[:, lanes], grads[:, lanes], None, scale
+            )
+            for r in range(chunks):
+                here = slice(r * cols, (r + 1) * cols)
+                there = slice(half + r * cols, half + (r + 1) * cols)
+                wide_parts[0, spots[r], lanes] = parts[0][here].astype(BF16)
+                for j in range(2):
+                    key_sums[j, spots[r], lanes] = parts[1 + j][here]
+                    side_out[j, spots[r], lanes] = parts[1 + j][there].astype(BF16)
+
+    key_copy = send(side_out, side_in, key_send, key_recv, place.sibling())
+    for job in early:
+        job.spread()
+    space_grads[0] = dot_outer(e1[...], o1[...]).astype(BF16)
+    narrow_parts[0] = dot_tr(wide_parts[0], spread[...]).astype(BF16)
+    key_copy.wait()
+    for j in range(2):
+        wide_parts[1 + j] = (key_sums[j] + side_in[j].astype(F32)).astype(BF16)
+        narrow_parts[1 + j] = dot_tr(wide_parts[1 + j], spread[...]).astype(BF16)
+    scatters = []
+    for r in range(chunks):
+        spot = pl.ds(r * rows, rows)
+        total = dot_tr(narrow_parts[0, spot], full[1])
+        for i in (1, 2):
+            total = total + dot_tr(narrow_parts[i, spot], full[1 + i])
+        partial[r] = total.astype(BF16)
+        scatters.append((ring.used, ring.scatter(partial.at[r], landing.at[ring.used])))
+
+    @pl.loop(0, 3)
+    def _(i):
+        space_grads[1 + i] = dot_outer(h1[...], narrow_parts[i]).astype(BF16)
+
+    for job in late:
+        job.split()
+    wait_all(word_copies)
+    for j in range(2):
+        total = dot_outer(words[0], word_parts[0, j, 0 : prompt.shape[0]])
+        for step in range(1, clips):
+            total = total + dot_outer(words[step], word_parts[step, j, 0 : prompt.shape[0]])
+        prompt_out[j] = total
+    for job in late:
+        job.spread()
+
+    gate_sum = jnp.zeros((1, width), F32)
+    shift_sum = jnp.zeros((1, width), F32)
+    scale_sum = jnp.zeros((1, width), F32)
+    gathers = []
+    for r in range(chunks):
+        kept = pl.ds(r * quarter, quarter)
+        stage, copies = scatters[r]
+        wait_all(copies)
+        grad = summed(partial.at[r], landing.at[stage], own, peers)
+        x_own = frames[own_spot, r].reshape(quarter, width).astype(F32)
+        normed, inverse = norm_tile(x_own)
+        gate_sum = gate_sum + jnp.sum(g1_own[kept] * a1_own[kept], 0, keepdims=True)
+        shift_sum = shift_sum + jnp.sum(grad, 0, keepdims=True)
+        scale_sum = scale_sum + jnp.sum(grad * normed, 0, keepdims=True)
+        upstream = g1_own[kept] + norm_pull(normed, inverse, grad * vectors[1:2])
+        frames_grad[own_spot, r] = upstream.astype(BF16).reshape(own_frames, cols, width)
+        gathers.append(ring.gather(frames_grad.at[own_spot, r]))
+    sums[...] = jnp.concatenate(
+        [shift_sum, scale_sum, gate_sum, jnp.zeros((5, width), F32)], 0
+    )
+    for i, job in enumerate(early):
+        job.finish(early_out.at[i])
+    for i, job in enumerate(late):
+        job.finish(space_out.at[i])
+    for copies in gathers:
+        wait_all(copies)
+
+
+def space_call(sizes, acts, halves, gradients):
+    frames, spread, prompt = acts[2], acts[5], acts[10]
+    frame_count, chunks, cols, width = frames.shape
+    rows = frame_count * cols
+    tokens = rows * chunks
+    quarter = rows // sizes[TENSOR]
+    peers = sizes[TENSOR] - 1
+    head_width, padded = spread.shape
+    full_rows = halves[0].shape[0] * sizes[WIDE]
+    parts = sizes[NARROW] * sizes[WIDE]
+    block, word_block = width // parts, prompt.shape[1] // parts
+    clips = sizes[NARROW]
+    s = jax.ShapeDtypeStruct
+    stages = 2 * chunks
+    outs = [
+        s(frames.shape, BF16), s((6, block, head_width), F32), s((4, block, head_width), F32),
+        s((2, word_block, head_width), F32), s((8, width), F32),
+    ]
+    return pl.pallas_call(
+        functools.partial(space_kernel, sizes),
+        name="space",
+        out_shape=outs,
+        in_specs=[VM] * len(acts) + [ANY] * 6,
+        out_specs=[VM] * len(outs),
+        scratch_shapes=[
+            VMEM((4, full_rows, head_width), BF16),
+            VMEM((tokens, padded), BF16),
+            VMEM((3, tokens, padded), BF16),
+            VMEM((3, tokens, head_width), BF16),
+            VMEM((2, tokens, padded), F32),
+            VMEM((2, tokens, padded), BF16), VMEM((2, tokens, padded), BF16),
+            VMEM((4, width, head_width), BF16),
+            VMEM((clips, prompt.shape[0], word_block), BF16),
+            VMEM((clips, 2, LANES, head_width), BF16),
+            VMEM((chunks, rows, width), BF16),
+            VMEM((stages, peers, quarter, width), BF16),
+            DMA((4,)), DMA((4,)), DMA((4,)), DMA(()), DMA(()),
+            DMA((clips - 1, 2)), DMA((clips - 1, 2)),
+            DMA((stages, peers)), DMA((stages, peers)),
+        ]
+        + reducer_scratch(sizes, 6, block, head_width)
+        + reducer_scratch(sizes, 4, block, head_width),
+        compiler_params=pltpu.CompilerParams(
+            collective_id=4, has_side_effects=True, vmem_limit_bytes=61 << 20
+        ),
+    )(*acts, *halves, *gradients)
+
+
+def tail_kernel(sizes, rows, condition, merged, conditions, landing, total, send_sems, recv_sems,
+                far_send, far_recv):
+    place = Place(sizes)
+    partners = []
+    for dw in range(sizes[WIDE]):
+        for dt in range(sizes[TENSOR]):
+            if dw or dt:
+                partners.append(
+                    (
+                        place.n,
+                        lax.rem(place.w + dw, sizes[WIDE]),
+                        lax.rem(place.t + dt, sizes[TENSOR]),
+                    )
+                )
+    far = [
+        place.over_narrow(lax.rem(place.n + step, sizes[NARROW]))
+        for step in range(1, sizes[NARROW])
+    ]
+    greet(partners + far)
+    copies = [
+        send(rows, landing.at[i], send_sems.at[i], recv_sems.at[i], partner)
+        for i, partner in enumerate(partners)
+    ]
+    cond_copies = [
+        send(condition, conditions.at[place.n], far_send.at[i, 1], far_recv.at[i, 1], partner)
+        for i, partner in enumerate(far)
+    ]
+    conditions[place.n] = condition[...]
+    wait_all(copies)
+    value = rows[...]
+    for i in range(len(partners)):
+        value = value + landing[i]
+    total[...] = value
+    far_copies = [
+        send(total, merged.at[place.n], far_send.at[i, 0], far_recv.at[i, 0], partner)
+        for i, partner in enumerate(far)
+    ]
+    merged[place.n] = value
+    wait_all(cond_copies + far_copies)
+
+
+def tail_call(sizes, rows, condition):
+    clips = sizes[NARROW]
+    group = sizes[WIDE] * sizes[TENSOR] - 1
+    s = jax.ShapeDtypeStruct
+    return pl.pallas_call(
+        functools.partial(tail_kernel, sizes),
+        name="tail",
+        out_shape=[s((clips,) + rows.shape, F32), s((clips,) + condition.shape, F32)],
+        in_specs=[VM, VM],
+        out_specs=[VM, VM],
+        scratch_shapes=[
+            VMEM((group,) + rows.shape, F32), VMEM(rows.shape, F32),
+            DMA((group,)), DMA((group,)), DMA((clips - 1, 2)), DMA((clips - 1, 2)),
+        ],
+        compiler_params=pltpu.CompilerParams(collective_id=5, has_side_effects=True),
+    )(rows, condition)
+
+
+def fused_on_device(
+    sizes,
+    frames, cotangent, prompt, timestep, clip_lengths, text_lengths,
+    modulation_weight, modulation_bias, space_query, space_key, space_value, space_out,
+    time_gain, time_query, time_key, time_value, time_out, time_gate, cross_gain, cross_query,
+    prompt_key, prompt_value, cross_out, feed_up, feed_down,
+):
+    width = frames.shape[4]
+    cols = frames.shape[3]
+    head_width = space_query.shape[1]
+    condition, vectors, live, key_live, word_live, spread = prepare(
+        sizes, frames, timestep, clip_lengths, text_lengths, modulation_weight, modulation_bias,
+        time_gain, time_gate, cross_gain, head_width,
+    )
+    (
+        h1, q1, side, o1, h2, q2, o2, h3, q3, kv3, o3, h4,
+        a1_own, a2_own, x3_own, n2_own, n3_own, n4_own, inverses,
+    ) = forward_call(
+        sizes, frames[0], vectors, key_live, word_live, spread, prompt[0],
+        [space_query, space_key, space_value, space_out, time_query, time_key, time_value,
+         time_out, cross_query, cross_out, prompt_key, prompt_value],
+    )
+    output, e3, g3_own, up_grad, down_grad, sums_four = mlp_call(
+        sizes, h4, cotangent[0], vectors, live, n4_own, inverses, x3_own, feed_up, feed_down
+    )
+    g1_own, e1, query_out, value_out, word_grads, up_out, down_out, sums_two = back_call(
+        sizes, cols,
+        [e3, g3_own, n3_own, n2_own, inverses, a2_own, vectors, key_live, word_live, spread,
+         h3, q3, kv3, o3, h2, q2, o2],
+        [cross_out, cross_query, time_out, time_query, time_key, time_value],
+        [up_grad, down_grad],
+    )
+    frames_grad, early_out, late_out, prompt_out, sums_one = space_call(
+        sizes,
+        [e1, g1_own, frames[0], a1_own, vectors, spread, h1, q1, side, o1, prompt[0], word_grads],
+        [space_out, space_query, space_key, space_value],
+        [value_out, query_out],
+    )
+    merged, conditions = tail_call(
+        sizes,
+        jnp.concatenate([sums_one[:3], sums_four[:3], sums_two[:3], jnp.zeros((7, width), F32)]),
+        condition.astype(F32)[None],
+    )
+    part = lax.axis_index(NARROW) * sizes[WIDE] + lax.axis_index(WIDE)
+    block = width // (sizes[NARROW] * sizes[WIDE])
+    slice_width = modulation_weight.shape[1]
+    pulled = merged[:, :6].reshape(sizes[NARROW], 6 * width)
+    own_pulled = lax.dynamic_slice_in_dim(
+        pulled, lax.axis_index(TENSOR) * slice_width, slice_width, 1
+    )
+    own_condition = lax.dynamic_slice_in_dim(conditions[:, 0], part * block, block, 1)
+    modulation_weight_grad = jnp.sum(own_condition[:, :, None] * own_pulled[:, None], 0)
+    summed_rows = jnp.sum(merged, 0)
+    bias_block = 6 * block
+    modulation_bias_grad = lax.dynamic_slice_in_dim(
+        summed_rows[:6].reshape(6 * width), part * bias_block, bias_block
+    )
+    cross_gain_grad, gate_rows, time_gain_grad = (
+        lax.dynamic_slice_in_dim(summed_rows[i], part * block, block) for i in (6, 7, 8)
+    )
+    own_gate = jnp.tanh(lax.dynamic_slice_in_dim(time_gate, part * block, block))
+    time_gate_grad = gate_rows * (1.0 - own_gate * own_gate)
+    return (
+        output[None], frames_grad[None], modulation_weight_grad, modulation_bias_grad,
+        late_out[1], late_out[2], late_out[3], late_out[0],
+        time_gain_grad, early_out[3], early_out[4], early_out[5], early_out[2], time_gate_grad,
+        cross_gain_grad, early_out[1], prompt_out[0], prompt_out[1], early_out[0],
+        up_out, down_out,
+    )
+
+
 CONTRACT_LAST = (((1,), (1,)), ((), ()))
 CONTRACT_FIRST = (((0,), (0,)), ((), ()))
 
@@ -41,7 +1339,7 @@
 
 
 def over_heads(partial_sum):
-    return lax.psum(partial_sum.astype(jnp.bfloat16), "tensor").astype(jnp.float32)
+    return lax.psum(partial_sum.astype(jnp.bfloat16), TENSOR).astype(jnp.float32)
 
 
 def attend_forward(queries, key_rows, values, allowed, pattern, score_scale):
@@ -137,21 +1435,21 @@
         feed_up,
         feed_down,
     ) = (
-        lax.all_gather(modulation_weight, "wide", axis=0, tiled=True),
-        lax.all_gather(space_query, "wide", axis=0, tiled=True),
-        lax.all_gather(space_key, "wide", axis=0, tiled=True),
-        lax.all_gather(space_value, "wide", axis=0, tiled=True),
-        lax.all_gather(space_out, "wide", axis=0, tiled=True),
-        lax.all_gather(time_query, "wide", axis=0, tiled=True),
-        lax.all_gather(time_key, "wide", axis=0, tiled=True),
-        lax.all_gather(time_value, "wide", axis=0, tiled=True),
-        lax.all_gather(time_out, "wide", axis=0, tiled=True),
-        lax.all_gather(cross_query, "wide", axis=0, tiled=True),
-        lax.all_gather(prompt_key, "wide", axis=0, tiled=True),
-        lax.all_gather(prompt_value, "wide", axis=0, tiled=True),
-        lax.all_gather(cross_out, "wide", axis=0, tiled=True),
-        lax.all_gather(feed_up, "wide", axis=0, tiled=True),
-        lax.all_gather(feed_down, "wide", axis=0, tiled=True),
+        lax.all_gather(modulation_weight, WIDE, axis=0, tiled=True),
+        lax.all_gather(space_query, WIDE, axis=0, tiled=True),
+        lax.all_gather(space_key, WIDE, axis=0, tiled=True),
+        lax.all_gather(space_value, WIDE, axis=0, tiled=True),
+        lax.all_gather(space_out, WIDE, axis=0, tiled=True),
+        lax.all_gather(time_query, WIDE, axis=0, tiled=True),
+        lax.all_gather(time_key, WIDE, axis=0, tiled=True),
+        lax.all_gather(time_value, WIDE, axis=0, tiled=True),
+        lax.all_gather(time_out, WIDE, axis=0, tiled=True),
+        lax.all_gather(cross_query, WIDE, axis=0, tiled=True),
+        lax.all_gather(prompt_key, WIDE, axis=0, tiled=True),
+        lax.all_gather(prompt_value, WIDE, axis=0, tiled=True),
+        lax.all_gather(cross_out, WIDE, axis=0, tiled=True),
+        lax.all_gather(feed_up, WIDE, axis=0, tiled=True),
+        lax.all_gather(feed_down, WIDE, axis=0, tiled=True),
     )
     head_width = space_query.shape[1]
     head_count = head_width // HEAD_DIM
@@ -163,11 +1461,11 @@
         jnp.bfloat16
     )
     slice_width = modulation_weight.shape[1]
-    slice_start = lax.axis_index("tensor") * slice_width
+    slice_start = lax.axis_index(TENSOR) * slice_width
     own_modulation = matmul(condition[None, :], modulation_weight)[0] + lax.dynamic_slice_in_dim(
         modulation_bias, slice_start, slice_width
     )
-    modulation = lax.all_gather(own_modulation, "tensor", axis=0, tiled=True)
+    modulation = lax.all_gather(own_modulation, TENSOR, axis=0, tiled=True)
     shift_one, scale_one, gate_one, shift_two, scale_two, gate_two = jnp.split(modulation, 6)
     normed_one, inverse_one = norm_rows(residual)
     input_one = (normed_one * (1.0 + scale_one) + shift_one).astype(jnp.bfloat16)
@@ -175,8 +1473,8 @@
     key_one = matmul(input_one, space_key).astype(jnp.bfloat16).reshape(split_heads)
     value_one = matmul(input_one, space_value).astype(jnp.bfloat16).reshape(split_heads)
     key_frame, value_frame = (
-        lax.all_gather(key_one, "wide", axis=1, tiled=True),
-        lax.all_gather(value_one, "wide", axis=1, tiled=True),
+        lax.all_gather(key_one, WIDE, axis=1, tiled=True),
+        lax.all_gather(value_one, WIDE, axis=1, tiled=True),
     )
     space_pattern = ("fphe,fkhe->fhpk", "fhpk,fkhe->fphe", "fhpk,fphe->fkhe")
     every_patch = jnp.ones((key_frame.shape[1],), jnp.bool_)
@@ -290,8 +1588,8 @@
     space_out_grad = outer_sum(space_grad, context_one)
     context_grad = matmul(space_grad, space_out).astype(jnp.bfloat16).reshape(split_heads)
     key_frame, value_frame = (
-        lax.all_gather(key_one, "wide", axis=1, tiled=True),
-        lax.all_gather(value_one, "wide", axis=1, tiled=True),
+        lax.all_gather(key_one, WIDE, axis=1, tiled=True),
+        lax.all_gather(value_one, WIDE, axis=1, tiled=True),
     )
     query_grad, key_grad, value_grad = attend_back(
         query_one,
@@ -305,10 +1603,10 @@
     )
     key_grad, value_grad = (
         lax.psum_scatter(
-            key_grad.astype(jnp.bfloat16), "wide", scatter_dimension=1, tiled=True
+            key_grad.astype(jnp.bfloat16), WIDE, scatter_dimension=1, tiled=True
         ).astype(jnp.float32),
         lax.psum_scatter(
-            value_grad.astype(jnp.bfloat16), "wide", scatter_dimension=1, tiled=True
+            value_grad.astype(jnp.bfloat16), WIDE, scatter_dimension=1, tiled=True
         ).astype(jnp.float32),
     )
     query_grad = query_grad.astype(jnp.bfloat16).reshape(token_count, head_width)
@@ -360,26 +1658,26 @@
         feed_down_grad,
     ) = (
         lax.psum_scatter(
-            modulation_weight_grad, ("narrow", "wide"), scatter_dimension=0, tiled=True
+            modulation_weight_grad, (NARROW, WIDE), scatter_dimension=0, tiled=True
         ),
-        lax.psum_scatter(modulation_bias_grad, ("narrow", "wide"), scatter_dimension=0, tiled=True),
-        lax.psum_scatter(space_query_grad, ("narrow", "wide"), scatter_dimension=0, tiled=True),
-        lax.psum_scatter(space_key_grad, ("narrow", "wide"), scatter_dimension=0, tiled=True),
-        lax.psum_scatter(space_value_grad, ("narrow", "wide"), scatter_dimension=0, tiled=True),
-        lax.psum_scatter(space_out_grad, ("narrow", "wide"), scatter_dimension=0, tiled=True),
-        lax.psum_scatter(time_gain_grad, ("narrow", "wide"), scatter_dimension=0, tiled=True),
-        lax.psum_scatter(time_query_grad, ("narrow", "wide"), scatter_dimension=0, tiled=True),
-        lax.psum_scatter(time_key_grad, ("narrow", "wide"), scatter_dimension=0, tiled=True),
-        lax.psum_scatter(time_value_grad, ("narrow", "wide"), scatter_dimension=0, tiled=True),
-        lax.psum_scatter(time_out_grad, ("narrow", "wide"), scatter_dimension=0, tiled=True),
-        lax.psum_scatter(time_gate_grad, ("narrow", "wide"), scatter_dimension=0, tiled=True),
-        lax.psum_scatter(cross_gain_grad, ("narrow", "wide"), scatter_dimension=0, tiled=True),
-        lax.psum_scatter(cross_query_grad, ("narrow", "wide"), scatter_dimension=0, tiled=True),
-        lax.psum_scatter(prompt_key_grad, ("narrow", "wide"), scatter_dimension=0, tiled=True),
-        lax.psum_scatter(prompt_value_grad, ("narrow", "wide"), scatter_dimension=0, tiled=True),
-        lax.psum_scatter(cross_out_grad, ("narrow", "wide"), scatter_dimension=0, tiled=True),
-        lax.psum_scatter(feed_up_grad, ("narrow", "wide"), scatter_dimension=0, tiled=True),
-        lax.psum_scatter(feed_down_grad, ("narrow", "wide"), scatter_dimension=0, tiled=True),
+        lax.psum_scatter(modulation_bias_grad, (NARROW, WIDE), scatter_dimension=0, tiled=True),
+        lax.psum_scatter(space_query_grad, (NARROW, WIDE), scatter_dimension=0, tiled=True),
+        lax.psum_scatter(space_key_grad, (NARROW, WIDE), scatter_dimension=0, tiled=True),
+        lax.psum_scatter(space_value_grad, (NARROW, WIDE), scatter_dimension=0, tiled=True),
+        lax.psum_scatter(space_out_grad, (NARROW, WIDE), scatter_dimension=0, tiled=True),
+        lax.psum_scatter(time_gain_grad, (NARROW, WIDE), scatter_dimension=0, tiled=True),
+        lax.psum_scatter(time_query_grad, (NARROW, WIDE), scatter_dimension=0, tiled=True),
+        lax.psum_scatter(time_key_grad, (NARROW, WIDE), scatter_dimension=0, tiled=True),
+        lax.psum_scatter(time_value_grad, (NARROW, WIDE), scatter_dimension=0, tiled=True),
+        lax.psum_scatter(time_out_grad, (NARROW, WIDE), scatter_dimension=0, tiled=True),
+        lax.psum_scatter(time_gate_grad, (NARROW, WIDE), scatter_dimension=0, tiled=True),
+        lax.psum_scatter(cross_gain_grad, (NARROW, WIDE), scatter_dimension=0, tiled=True),
+        lax.psum_scatter(cross_query_grad, (NARROW, WIDE), scatter_dimension=0, tiled=True),
+        lax.psum_scatter(prompt_key_grad, (NARROW, WIDE), scatter_dimension=0, tiled=True),
+        lax.psum_scatter(prompt_value_grad, (NARROW, WIDE), scatter_dimension=0, tiled=True),
+        lax.psum_scatter(cross_out_grad, (NARROW, WIDE), scatter_dimension=0, tiled=True),
+        lax.psum_scatter(feed_up_grad, (NARROW, WIDE), scatter_dimension=0, tiled=True),
+        lax.psum_scatter(feed_down_grad, (NARROW, WIDE), scatter_dimension=0, tiled=True),
     )
     return (
         output,
@@ -406,59 +1704,33 @@
     )
 
 
+WEIGHT = P(WIDE, TENSOR)
+OWNED = P((NARROW, WIDE), TENSOR)
+ROWS = P((NARROW, WIDE))
+PATCHES = P(NARROW, None, WIDE, None, None)
+CLIP = P(NARROW)
+COPIED = P()
+
+
+def fits(sizes):
+    return sizes[WIDE] == 2 and sizes[TENSOR] == 4 and sizes[NARROW] == 4
+
+
 def solution(mesh):
+    sizes = {name: mesh.shape[name] for name in mesh.axis_names}
     return jax.shard_map(
-        on_device,
+        functools.partial(fused_on_device, sizes) if fits(sizes) else on_device,
         mesh=mesh,
         in_specs=(
-            P("narrow", None, "wide", None, None),
-            P("narrow", None, "wide", None, None),
-            P("narrow", None, None),
-            P("narrow"),
-            P("narrow"),
-            P("narrow"),
-            P("wide", "tensor"),
-            P(),
-            P("wide", "tensor"),
-            P("wide", "tensor"),
-            P("wide", "tensor"),
-            P("wide", "tensor"),
-            P(),
-            P("wide", "tensor"),
-            P("wide", "tensor"),
-            P("wide", "tensor"),
-            P("wide", "tensor"),
-            P(),
-            P(),
-            P("wide", "tensor"),
-            P("wide", "tensor"),
-            P("wide", "tensor"),
-            P("wide", "tensor"),
-            P("wide", "tensor"),
-            P("wide", "tensor"),
+            (PATCHES, PATCHES, P(NARROW, None, None), CLIP, CLIP, CLIP)
+            + (WEIGHT, COPIED, WEIGHT, WEIGHT, WEIGHT, WEIGHT)
+            + (COPIED, WEIGHT, WEIGHT, WEIGHT, WEIGHT, COPIED)
+            + (COPIED, WEIGHT, WEIGHT, WEIGHT, WEIGHT, WEIGHT, WEIGHT)
         ),
         out_specs=(
-            P("narrow", None, "wide", None, None),
-            P("narrow", None, "wide", None, None),
-            P(("narrow", "wide"), "tensor"),
-            P(("narrow", "wide")),
-            P(("narrow", "wide"), "tensor"),
-            P(("narrow", "wide"), "tensor"),
-            P(("narrow", "wide"), "tensor"),
-            P(("narrow", "wide"), "tensor"),
-            P(("narrow", "wide")),
-            P(("narrow", "wide"), "tensor"),
-            P(("narrow", "wide"), "tensor"),
-            P(("narrow", "wide"), "tensor"),
-            P(("narrow", "wide"), "tensor"),
-            P(("narrow", "wide")),
-            P(("narrow", "wide")),
-            P(("narrow", "wide"), "tensor"),
-            P(("narrow", "wide"), "tensor"),
-            P(("narrow", "wide"), "tensor"),
-            P(("narrow", "wide"), "tensor"),
-            P(("narrow", "wide"), "tensor"),
-            P(("narrow", "wide"), "tensor"),
+            (PATCHES, PATCHES, OWNED, ROWS, OWNED, OWNED, OWNED, OWNED)
+            + (ROWS, OWNED, OWNED, OWNED, OWNED, ROWS)
+            + (ROWS, OWNED, OWNED, OWNED, OWNED, OWNED, OWNED)
         ),
         check_vma=False,
     )

time: 1480 us -> 595 us (0.40)
  waiting for transfers between devices: 1040 us -> 0 us
  Pallas kernels: 0 us -> 547 us
  matrix products: 149 us -> 0 us
  local copies, waits for them, and re-layouts: 131 us -> 33.3 us
  blocking collectives: 77.3 us -> 0 us
  other arithmetic: 53.4 us -> 7.6 us
  between operations: 20.1 us -> 3.11 us
    reduce_scatter x17 -> x0, waiting for transfers between devices: 702 us -> none  [the longest x1 74.9 us: on_device(): lax.psum_scatter(modulation_weight_grad, ('narrow', 'wide'), scatter_dime...]
    pallas_call x0 -> x6, Pallas kernels: none -> 547 us  [the longest x1 184 us: forward_call(): pl.pallas_call(functools.partial(forward_kernel, sizes), name='forward',...]
    psum x7 -> x0, waiting for transfers between devices: 325 us -> none  [over_heads(): lax.psum(partial_sum.astype(jnp.bfloat16), 'tensor').astype(jnp.float32)]
    dot_general x59 -> x0, matrix products: 149 us -> none  [the longest x14 50.2 us: outer_sum(): lax.dot_general(left, right, CONTRACT_FIRST, preferred_element_type=jnp.f...]
    reshape x24 -> x2, local copies, waits for them, and re-layouts: 46.6 us -> 0.11 us  [the longest x1 0.1 us: prepare(): parts = parts.reshape(sizes[WIDE], -1)]
    unnamed x2 -> x0, blocking collectives: 45 us -> none
    all_gather x12 -> x0, blocking collectives: 32.2 us -> none  [the longest x1 4.3 us: on_device(): lax.all_gather(value_one, 'wide', axis=1, tiled=True)]
    reduce_sum x18 -> x3, other arithmetic: 31.3 us -> 2.4 us  [the longest x1 1.34 us: fused_on_device(): jnp.sum(own_condition[:, :, None] * own_pulled[:, None], 0)]
  transfers between devices with their start and end apart: 29 -> 0, of which waited for: 22 -> 0; matrix products, arithmetic and copies ran while one was open for 13% -> 0% of each run, Pallas kernels for 0% -> 0%
where the time goes in v1:
time: 595 us; the launch traced here: 591 us
  Pallas kernels  547 us (92%)
  local copies, waits for them, and re-layouts  33.3 us (6%)
  other arithmetic  7.6 us (1%)
    pallas_call x1, Pallas kernels, forward_call(): pl.pallas_call(functools.partial(forward_kernel, sizes), name='forward',...  184 us
    pallas_call x1, Pallas kernels, back_call(): pl.pallas_call(functools.partial(back_kernel, {**sizes, COLS: cols}), nam...  120 us
    pallas_call x1, Pallas kernels, mlp_call(): pl.pallas_call(functools.partial(mlp_kernel, sizes), name='mlp', out_shap...  119 us
    pallas_call x1, Pallas kernels, space_call(): pl.pallas_call(functools.partial(space_kernel, sizes), name='space', out_...  87.1 us
    pallas_call x1, Pallas kernels, tail_call(): pl.pallas_call(functools.partial(tail_kernel, sizes), name='tail', out_sh...  26.5 us
    unnamed x65, local copies, waits for them, and re-layouts  21.8 us

profile of v1, /device:TPU:0, one launch (start us, length us, event | category | flops | bytes accessed | tf_op | source)
XLA Modules:
  0.0 591.0 jit_solution(6547018356180563893)
XLA Ops:
  2.6 0.5 compare_convert_fusion.word_live
  3.2 0.1 pad.5.clone
  3.2 0.1 broadcast_in_dim.15
  3.3 0.6 convert_element_type.68.key_live
  3.9 0.7 stack.14
  4.6 0.7 stack.16
  5.4 0.1 multiply_convert_fusion
  5.5 0.7 convert_convert_fusion.condition
  6.2 0.7 tanh.6
  6.9 0.6 broadcast_in_dim.14.condition
  7.5 0.7 broadcast_in_dim.16.live
  8.2 10.3 %modulation.1 = f32[8,1,1728]{2,1,0:T(1,128)} custom-call(bf16[16,576]{1,0:T(8,128)(2,1)} %broadcast_in_dim.14.condition, bf16[576,1728]{1,0:T(8,128)(2,1)} %weight.1), custom_call_target="tpu_custom_call" | custom-call | tf_op jit(solution)/shard_map/modulation/pallas_call | solution.py:181
  18.5 0.0 copy-start.10
  18.5 0.0 copy-start.11
  18.5 1.0 reduce
  19.6 0.1 reshape.177
  19.7 0.1 reduce_sum.27
  19.8 1.3 stack.17.vectors
  21.2 0.8 fusion.spread
  21.9 1.0 copy.94.refs_0_.refs_1_
  22.9 0.0 copy-done.10
  22.9 1.0 copy.95.refs_1_.refs_2_
  23.9 1.0 copy.96.refs_2_.refs_3_
  24.8 1.0 copy.97.refs_3_.refs_0_
  25.8 1.0 copy.98.refs_4_.refs_3_
  26.8 1.0 copy.99.refs_5_.refs_4_
  27.7 1.0 copy.100.refs_6_.refs_5_
  28.7 1.0 copy.101.refs_7_.refs_2_
  29.7 1.0 copy.102.refs_8_.refs_1_
  30.6 1.0 copy.103.refs_9_.refs_0_
  31.6 0.0 copy-done.4
  31.6 1.7 copy.104.refs_10_
  33.3 1.5 copy.105.refs_11_
  34.9 184.1 %forward.1 = (bf16[512,1152]{1,0:T(8,128)(2,1)}, bf16[3,512,512]{2,1,0:T(8,128)(2,1)}, bf16[2,512,512]{2,1,0:T(8,128)(2,1)}, bf16[512,288]{1,0:T(8,128)(2,1)}, b...) custom-call(bf16[8,2,32,1152]{3,2,1,0:T(8,128)(2,1)} %bitcast.43, ...), custom_call_target="tpu_custom_call" | custom-call | tf_op jit(solution)/shard_map/forward/pallas_call | solution.py:426
  219.0 119.4 %mlp.1 = (bf16[8,2,32,1152]{3,2,1,0:T(8,128)(2,1)}, bf16[512,1152]{1,0:T(8,128)(2,1)}, f32[128,1152]{1,0:T(8,128)}, bf16[1152,1152]{1,0:T(8,128)(2,1)}, bf16[1152,1152]{1,0:T(8,128)(2,1)}, /*index=5*/f32[8,1152]{1,0:T(8,128)}) custom-call(bf16[512,1152]{1,0:T(8,128)(2,1)} %get-tuple-element.61.h4, bf16[8,2,32,1152]{3,2,1,0:T(8,128)(2,1)} %bitcast.47, ...), custom_call_target="tpu_custom_call" | custom-call | tf_op jit(solution)/shard_map/mlp/pallas_call | solution.py:632
  338.3 119.7 %back.1 = (f32[128,1152]{1,0:T(8,128)}, bf16[512,1152]{1,0:T(8,128)(2,1)}, bf16[4,1152,288]{2,1,0:T(8,128)(2,1)}, bf16[2,1152,288]{2,1,0:T(8,128)(2,1)}, bf16[2,...) custom-call(bf16[512,1152]{1,0:T(8,128)(2,1)} %get-tuple-element.66.e3, ...), custom_call_target="tpu_custom_call" | custom-call | tf_op jit(solution)/shard_map/back/pallas_call | solution.py:956
  458.0 0.0 copy-start.21
  458.0 0.0 copy-start.20
  458.0 87.1 %space.1 = (bf16[8,2,32,1152]{3,2,1,0:T(8,128)(2,1)}, f32[6,144,288]{2,1,0:T(8,128)}, f32[4,144,288]{2,1,0:T(8,128)}, f32[2,512,288]{2,1,0:T(8,128)}, f32[8,1152]{1,0:T(8,128)}) custom-call(bf16[512,1152]{1,0:T(8,128)(2,1)} %get-tuple-element.80.e1, f32[128,1152]{1,0:T(8,128)} %get-tuple-element.81.g1_own, bf16[8,2,32,1152]{3,2,1,0:T(8,128)(2,1)} %bitcast.44, ...), custom_call_target="tpu_custom_call" | custom-call | tf_op jit(solution)/shard_map/space/pallas_call | solution.py:1151
  545.2 0.8 slice.102
  546.1 0.7 maximum_maximum_fusion.rows
  546.8 26.5 %tail.1 = (f32[4,16,1152]{2,1,0:T(8,128)}, f32[4,1,1152]{2,1,0:T(1,128)}) custom-call(f32[16,1152]{1,0:T(8,128)} %maximum_maximum_fusion.rows, f32[1,1152]{1,0:T(1,128)} %convert_convert_fusion.condition), custom_call_target="tpu_custom_call" | custom-call | tf_op jit(solution)/shard_map/tail/pallas_call | solution.py:1226
  573.3 0.8 constant_dynamic-slice_fusion.4
  574.1 1.0 reduce_sum.29
  575.1 0.9 slice_bitcast_fusion.12
  576.1 0.1 constant_dynamic-slice_fusion.3
  576.2 0.7 dynamic_slice.33
  576.9 0.6 constant_dynamic-slice_fusion
  577.5 0.1 constant_dynamic-slice_fusion.1
  577.6 1.3 subtract_multiply_fusion
  578.9 0.6 constant_dynamic-slice_fusion.2
  579.6 0.9 slice_bitcast_fusion.8
  580.5 1.3 multiply_reduce_fusion
  581.8 1.1 slice_bitcast_fusion.2
  582.9 0.8 copy-done
  583.7 0.1 slice_bitcast_fusion
  583.8 1.1 copy.117
  584.9 1.1 copy.116
  586.0 1.0 copy.129
  587.0 0.7 copy-done.3
  587.7 1.0 copy.130
  588.7 0.5 copy-done.8
  589.2 0.8 copy.131
  590.0 0.8 copy.132
  (57 shorter events, 0.3 us)
Async XLA Ops:
  0.7 19.1 %copy-start.19 = (f32[6912]{0:T(1024)S(1)}, f32[6912]{0:T(1024)}, u32[]{:S(2)}) copy-start(f32[6912]{0:T(1024)} %param.32) | copy-start | bytes 82948
  8.2 13.7 %copy-start.9 = (bf16[576,288]{0,1:T(8,128)(2,1)S(1)}, bf16[576,288]{0,1:T(8,128)(2,1)}, u32[]{:S(2)}) copy-start(bf16[576,288]{0,1:T(8,128)(2,1)} %param.33) | copy-start | bytes 995332
  18.5 4.4 copy-start.10
  18.5 5.3 copy-start.11
  21.2 3.7 copy-start.12
  22.9 2.9 copy-start.13
  23.9 2.9 copy-start.14
  24.8 2.9 copy-start.15
  25.8 2.9 copy-start.16
  26.8 2.9 copy-start.17
  27.7 2.9 copy-start.18
  28.7 2.9 copy-start.4
  31.6 1.7 copy-start.5
  458.0 88.0 %copy-start.21 = (f32[8,1152]{1,0:T(8,128)S(1)}, f32[8,1152]{1,0:T(8,128)}, u32[]{:S(2)}) copy-start(f32[8,1152]{1,0:T(8,128)} %get-tuple-element.93) | copy-start | bytes 110596
  458.0 88.0 %copy-start.20 = (f32[8,1152]{1,0:T(8,128)S(1)}, f32[8,1152]{1,0:T(8,128)}, u32[]{:S(2)}) copy-start(f32[8,1152]{1,0:T(8,128)} %get-tuple-element.92) | copy-start | bytes 110596
  545.2 34.4 %copy-start.6 = (f32[4,144,288]{2,1,0:T(8,128)S(1)}, f32[4,144,288]{2,1,0:T(8,128)}, u32[]{:S(2)}) copy-start(f32[4,144,288]{2,1,0:T(8,128)} %get-tuple-element.96) | copy-start | bytes 1990660
  579.6 2.3 copy-start.1
  581.8 1.9 copy-start
  583.8 2.1 copy-start.2
  586.0 1.7 copy-start.3
  587.7 1.5 copy-start.8
  587.7 2.4 copy-start.7

commit v2 on v1

--- a/solution.py
+++ b/solution.py
@@ -10,6 +10,9 @@
 
 HEAD_DIM = 72
 LANES = 128
+GRANULES = 2
+WHOLE = 256
+CHUNKS = 2
 EPSILON = 1e-06
 NEGATIVE = -1e30
 NARROW, WIDE, TENSOR = "narrow", "wide", "tensor"
@@ -94,60 +97,154 @@
     return copy
 
 
-class Ring:
-    def __init__(self, place, quarter, send_sems, recv_sems):
-        self.place, self.quarter = place, quarter
-        self.send_sems, self.recv_sems = send_sems, recv_sems
-        self.peers = place.sizes[TENSOR] - 1
-        self.used = 0
-
-    def take(self):
-        self.used += 1
-        return self.used - 1
-
-    def scatter(self, partial, landing):
-        slot = self.take()
-        copies = []
-        for step in (2, 1, 3) if self.peers == 3 else range(1, self.peers + 1):
-            rows = pl.ds(
-                pl.multiple_of(self.place.tensor_peer(step) * self.quarter, self.quarter),
-                self.quarter,
+class Transfer:
+    def __init__(self, slot, scatter, view, landing, born):
+        self.slot, self.scatter, self.view, self.landing = slot, scatter, view, landing
+        self.step, self.born = 0, born
+
+
+class Line:
+    def __init__(self, place, send_sems, recv_sems):
+        self.place, self.send_sems, self.recv_sems = place, send_sems, recv_sems
+        self.open, self.slots, self.clock = [], 0, 0
+
+    def at(self, index, body):
+        pl.when(self.place.t == index)(body)
+
+    def hop(self, move, source, target, sent, received, g, peer):
+        return pltpu.make_async_remote_copy(
+            src_ref=source,
+            dst_ref=target,
+            send_sem=self.send_sems.at[move.slot, sent, g],
+            recv_sem=self.recv_sems.at[move.slot, received, g],
+            device_id=(self.place.n, self.place.w, peer),
+            device_id_type=MESH_ID,
+        )
+
+    def reduce_hop(self, move, owner, lands, g, peer):
+        return self.hop(
+            move, move.view(owner, g), move.landing(lands, g), owner, lands, g, peer
+        )
+
+    def copy_hop(self, move, owner, sent, g, peer):
+        block = move.view(owner, g)
+        return self.hop(move, block, block, sent, owner, g, peer)
+
+    def start(self, scatter, view, landing=None):
+        move = Transfer(self.slots, scatter, view, landing, self.clock)
+        self.slots += 1
+        if scatter:
+            plan = {
+                0: [(3, 3, 1), (2, 2, 1), (1, 1, 1)],
+                1: [(0, 0, 0)],
+                2: [(3, 3, 3)],
+                3: [(0, 0, 2), (1, 1, 2), (2, 2, 2)],
+            }
+            make = self.reduce_hop
+        else:
+            plan = {
+                0: [(0, 0, 2), (0, 1, 1)],
+                1: [(1, 0, 2), (1, 1, 0)],
+                2: [(2, 0, 1), (2, 1, 3)],
+                3: [(3, 0, 1), (3, 1, 2)],
+            }
+            make = self.copy_hop
+        for device, hops in plan.items():
+
+            def begin(hops=hops):
+                for owner, index, peer in hops:
+                    for g in range(GRANULES):
+                        make(move, owner, index, g, peer).start()
+
+            self.at(device, begin)
+        self.open.append(move)
+        return move
+
+    def pending_block(self, move, index, g):
+        block = move.landing(index, g) if move.scatter else move.view(index, g)
+        return self.hop(move, block, block, 0, index, g, 0)
+
+    def relay(self, move, index, g, lands, sent, peer):
+        self.pending_block(move, index, g).wait_recv()
+        if move.scatter:
+            block = move.landing(index, g)
+            block[...] = (block[...].astype(F32) + move.view(index, g)[...].astype(F32)).astype(
+                BF16
             )
-            copies.append(
-                send(
-                    partial.at[rows],
-                    landing.at[step - 1],
-                    self.send_sems.at[slot, step - 1],
-                    self.recv_sems.at[slot, step - 1],
-                    self.place.over_tensor(step),
-                )
-            )
-        return copies
-
-    def gather(self, own):
-        slot = self.take()
-        return [
-            send(
-                own,
-                own,
-                self.send_sems.at[slot, step - 1],
-                self.recv_sems.at[slot, step - 1],
-                self.place.over_tensor(step),
-            )
-            for step in ((2, 1, 3) if self.peers == 3 else range(1, self.peers + 1))
-        ]
+            self.hop(move, block, move.landing(lands, g), index, lands, g, peer).start()
+        else:
+            self.copy_hop(move, index, sent, g, peer).start()
+
+    def steps(self):
+        return 2 * GRANULES
+
+    def advance(self, move):
+        late, g = divmod(move.step, GRANULES)
+        move.step += 1
+        if move.scatter:
+            plan = {1: ((3, 2, 0, 3), (2, 3, 0, 2)), 2: ((0, 1, 0, 0), (1, 0, 0, 1))}
+        else:
+            plan = {1: ((2, 0, 2, 0), (3, 0, 3, 0)), 2: ((1, 0, 2, 3), (0, 0, 3, 3))}
+        for device, pair in plan.items():
+            index, lands, sent, peer = pair[late]
+
+            def body(index=index, lands=lands, sent=sent, peer=peer):
+                self.relay(move, index, g, lands, sent, peer)
+
+            self.at(device, body)
+
+    def tick(self, count=1, lag=2):
+        self.clock += 1
+        for _ in range(count):
+            for move in self.open:
+                if move.step < self.steps() and move.born + lag <= self.clock:
+                    self.advance(move)
+                    break
+
+    def drain(self, move):
+        while move.step < self.steps():
+            self.advance(move)
+
+    def finish(self, move):
+        while move.step < self.steps():
+            self.advance(move)
+            for other in self.open:
+                if other is not move and other.step < self.steps() and not other.scatter:
+                    self.advance(other)
+                    break
+        self.open.remove(move)
+        if move.scatter:
+            plan = {0: (0, 1), 1: (1, 0), 2: (2, 3), 3: (3, 2)}
+        else:
+            plan = {0: (1, 2, 3), 1: (0,), 2: (3,), 3: (2, 1, 0)}
+        for device, blocks in plan.items():
+
+            def body(blocks=blocks):
+                for index in blocks:
+                    for g in range(GRANULES):
+                        self.pending_block(move, index, g).wait_recv()
+
+            self.at(device, body)
+
+    def release(self, move):
+        for device in range(4):
+            if move.scatter:
+                sent = [d for d in range(4) if d != device]
+            else:
+                sent = range(4) if device in (1, 2) else range(2)
+
+            def body(sent=sent):
+                for index in sent:
+                    for g in range(GRANULES):
+                        block = move.view(0, g)
+                        self.hop(move, block, block, index, 0, g, 0).wait_send()
+
+            self.at(device, body)
 
 
 def wait_all(copies):
     for copy in copies:
         copy.wait()
-
-
-def summed(partial, landing, rows, peers):
-    total = partial[rows].astype(F32)
-    for peer in range(peers):
-        total = total + landing[peer].astype(F32)
-    return total
 
 
 def modulation_kernel(sizes, condition, weight, shared, mine, landing, send_sems, recv_sems):
@@ -194,6 +291,84 @@
     )(condition, weight)
 
 
+class Split:
+    def __init__(self, place, frame_count, chunks, cols):
+        parts = place.sizes[TENSOR]
+        self.frame_count, self.chunks, self.cols = frame_count, chunks, cols
+        self.rows = frame_count * cols
+        self.quarter = self.rows // parts
+        self.place = place
+        self.frames = frame_count // parts
+
+    def chunk(self, r):
+        return pl.ds(r * self.rows, self.rows)
+
+    def kept(self, r):
+        return pl.ds(r * self.quarter, self.quarter)
+
+    def own(self, r):
+        start = r * self.rows + self.place.t * self.quarter
+        return pl.ds(pl.multiple_of(start, self.quarter), self.quarter)
+
+    def own_frames(self):
+        return pl.ds(self.place.t * self.frames, self.frames)
+
+    def rows_view(self, ref, r):
+        size = self.quarter // GRANULES
+
+        def view(s, g):
+            return ref.at[pl.ds(r * self.rows + s * self.quarter + g * size, size)]
+
+        return view
+
+    def frames_view(self, ref, r):
+        size = self.frames // GRANULES
+
+        def view(s, g):
+            return ref.at[pl.ds(s * self.frames + g * size, size), r]
+
+        return view
+
+    def landing_view(self, ref):
+        size = self.quarter // GRANULES
+
+        def view(s, g):
+            return ref.at[s, pl.ds(g * size, size)]
+
+        return view
+
+    def total(self, partial, landing, r):
+        t = self.place.t
+        beside = t + 1 - 2 * lax.rem(t, 2)
+        return (
+            partial[self.own(r)].astype(F32)
+            + landing[t].astype(F32)
+            + landing[beside].astype(F32)
+        )
+
+    def spots(self, f):
+        return [
+            pl.ds(pl.multiple_of(r * self.rows + f * self.cols, self.cols), self.cols)
+            for r in range(self.chunks)
+        ]
+
+
+def neighbours(place):
+    steps = range(1, place.sizes[TENSOR])
+    return [place.sibling()] + [place.over_tensor(step) for step in steps]
+
+
+def write_group_mask(group_mask, key_live, cols):
+    shape = group_mask.shape
+    row_id = lax.broadcasted_iota(jnp.int32, shape, 0)
+    col_id = lax.broadcasted_iota(jnp.int32, shape, 1)
+    group_mask[...] = jnp.where(
+        lax.rem(row_id, cols) == lax.rem(col_id, cols),
+        jnp.broadcast_to(key_live[0:1], shape),
+        0.0,
+    )
+
+
 def forward_kernel(
     sizes,
     frames,
@@ -214,19 +389,17 @@
         local_sems, side_send, side_recv, kv_send, kv_recv, ring_send, ring_recv,
     ) = refs[31:]
     place = Place(sizes)
-    peers = sizes[TENSOR] - 1
     frame_count, chunks, cols, width = frames.shape
-    rows = frame_count * cols
-    quarter = rows // sizes[TENSOR]
-    own_frames = frame_count // sizes[TENSOR]
+    split = Split(place, frame_count, chunks, cols)
+    rows, half = split.rows, split.quarter
     heads = spread.shape[1] // LANES
     scale = 1.0 / math.sqrt(HEAD_DIM)
-    ring = Ring(place, quarter, ring_send, ring_recv)
-    greet([place.sibling()] + [place.over_tensor(step) for step in range(1, peers + 1)])
+    chain = Line(place, ring_send, ring_recv)
+    greet(neighbours(place))
 
     def fetch(i):
-        half = weights[i].shape[0]
-        spot = pl.ds(pl.multiple_of(place.w * half, half), half)
+        weight_half = weights[i].shape[0]
+        spot = pl.ds(pl.multiple_of(place.w * weight_half, weight_half), weight_half)
         target = full.at[i, spot] if i < 10 else full_prompt.at[i - 10, spot]
         local = pltpu.make_async_copy(weights[i], target, local_sems.at[i])
         local.start()
@@ -246,27 +419,18 @@
                 normed * vectors[1:2] + vectors[0:1]
             ).astype(BF16)
 
-    row_id = lax.broadcasted_iota(jnp.int32, (rows, rows), 0)
-    col_id = lax.broadcasted_iota(jnp.int32, (rows, rows), 1)
-    group_mask[...] = jnp.where(
-        lax.rem(row_id, cols) == lax.rem(col_id, cols),
-        jnp.broadcast_to(key_live[0:1], (rows, rows)),
-        0.0,
-    )
+    write_group_mask(group_mask, key_live, cols)
 
     def project(source, spot, weight, out, index):
         narrow = dot(source[spot], full[weight]).astype(BF16)
         out[index, spot] = dot(narrow, spread[...]).astype(BF16)
 
-    def chunk_rows(r):
-        return pl.ds(r * rows, rows)
-
     ready(0, 1, 2)
 
     @pl.loop(0, 3)
     def _(i):
-        for r in range(chunks):
-            project(h1, chunk_rows(r), i, q1, i)
+        for r in range(0, chunks * rows, WHOLE):
+            project(h1, pl.ds(r, WHOLE), i, q1, i)
 
     kv_copies = [
         send(q1.at[1 + j], side.at[j], kv_send.at[j], kv_recv.at[j], place.sibling())
@@ -278,9 +442,7 @@
 
     @pl.loop(0, frame_count)
     def _(f):
-        spots = [
-            pl.ds(pl.multiple_of(r * rows + f * cols, cols), cols) for r in range(chunks)
-        ]
+        spots = split.spots(f)
         queries = jnp.concatenate([q1[0, spot] for spot in spots], 0)
         keys = jnp.concatenate(
             [q1[1, spot] for spot in spots] + [side[0, spot] for spot in spots], 0
@@ -295,112 +457,116 @@
             for r in range(chunks):
                 wide_context[spots[r], lanes] = context[r * cols : (r + 1) * cols]
 
-    def emit(r, out, weight):
-        spot = chunk_rows(r)
+    sent = [None] * chunks
+
+    def emit(r, out, weight, stage):
+        spot = split.chunk(r)
         out[spot] = dot_tr(wide_context[spot], spread[...]).astype(BF16)
-        partial[r] = dot_tr(out[spot], full[weight]).astype(BF16)
-        return ring.scatter(partial.at[r], landing.at[ring.used])
-
-    own = pl.ds(pl.multiple_of(place.t * quarter, quarter), quarter)
-
-    def own_rows(r):
-        return pl.ds(pl.multiple_of(r * rows + place.t * quarter, quarter), quarter)
-
-    def kept(r):
-        return pl.ds(r * quarter, quarter)
+        if sent[r] is not None:
+            chain.release(sent[r])
+        partial[spot] = dot_tr(out[spot], full[weight]).astype(BF16)
+        sent[r] = chain.start(
+            True, split.rows_view(partial, r), split.landing_view(landing.at[stage * chunks + r])
+        )
+        return sent[r]
 
     def branch(r, stage):
-        return summed(partial.at[r], landing.at[stage], own, peers)
+        return split.total(partial, landing.at[stage * chunks + r], r)
+
+    def settle(scatters, body, target):
+        gathers = []
+        for r in range(chunks):
+            chain.finish(scatters[r])
+            body(r)
+            gathers.append(chain.start(False, split.rows_view(target, r)))
+        return gathers
 
     ready(3)
     scatters = []
     for r in range(chunks):
-        scatters.append((ring.used, emit(r, o1, 3)))
+        scatters.append(emit(r, o1, 3, 0))
+        chain.tick(0)
 
     ready(10, 11)
     kv3[...] = jnp.zeros_like(kv3)
     for j in range(2):
         narrow = dot(prompt[...], full_prompt[j]).astype(BF16)
         kv3[j, 0 : prompt.shape[0]] = dot(narrow, spread[...]).astype(BF16)
-
-    gathers = []
-    for r in range(chunks):
-        stage, copies = scatters[r]
-        wait_all(copies)
-        branch_one = branch(r, stage)
-        a1_own[kept(r)] = branch_one
-        x_own = frames[pl.ds(place.t * own_frames, own_frames), r].reshape(quarter, width)
+        chain.tick(4)
+
+    def body_one(r):
+        kept = split.kept(r)
+        branch_one = branch(r, 0)
+        a1_own[kept] = branch_one
+        x_own = frames[split.own_frames(), r].reshape(half, width)
         after = x_own.astype(F32) + vectors[2:3] * branch_one
         normed, inverse = norm_tile(after)
-        residual[kept(r)] = after
-        n2_own[kept(r)] = normed
-        inverses[0, kept(r)] = jnp.broadcast_to(inverse, (quarter, LANES))
-        h2[own_rows(r)] = (normed * vectors[6:7]).astype(BF16)
-        gathers.append(ring.gather(h2.at[own_rows(r)]))
-
+        residual[kept] = after
+        n2_own[kept] = normed
+        inverses[0, kept] = jnp.broadcast_to(inverse, (half, LANES))
+        h2[split.own(r)] = (normed * vectors[6:7]).astype(BF16)
+
+    gathers = settle(scatters, body_one, h2)
+    released = list(gathers)
     ready(4, 5, 6, 7)
     scatters = []
     for r in range(chunks):
-        wait_all(gathers[r])
-        spot = chunk_rows(r)
-
-        @pl.loop(0, 3)
-        def _(i):
+        chain.finish(gathers[r])
+        spot = split.chunk(r)
+        for i in range(3):
             project(h2, spot, 4 + i, q2, i)
-
-        @pl.loop(0, heads)
-        def _(h):
-            lanes = pl.ds(pl.multiple_of(h * LANES, LANES), LANES)
+            chain.tick()
+        for h in range(heads):
+            lanes = slice(h * LANES, (h + 1) * LANES)
             scores = dot_tr(q2[0, spot, lanes], q2[1, spot, lanes]) * scale
             attend = softmax_tile(jnp.where(group_mask[...] > 0.5, scores, NEGATIVE))
             wide_context[spot, lanes] = dot(attend.astype(BF16), q2[2, spot, lanes]).astype(BF16)
-
-        scatters.append((ring.used, emit(r, o2, 7)))
-
-    gathers = []
-    for r in range(chunks):
-        stage, copies = scatters[r]
-        wait_all(copies)
-        branch_two = branch(r, stage)
-        a2_own[kept(r)] = branch_two
-        after = residual[kept(r)] + vectors[7:8] * branch_two
+        chain.tick()
+        scatters.append(emit(r, o2, 7, 1))
+
+    def body_two(r):
+        kept = split.kept(r)
+        branch_two = branch(r, 1)
+        a2_own[kept] = branch_two
+        after = residual[kept] + vectors[7:8] * branch_two
         normed, inverse = norm_tile(after)
-        residual[kept(r)] = after
-        n3_own[kept(r)] = normed
-        inverses[1, kept(r)] = jnp.broadcast_to(inverse, (quarter, LANES))
-        h3[own_rows(r)] = (normed * vectors[8:9]).astype(BF16)
-        gathers.append(ring.gather(h3.at[own_rows(r)]))
-
+        residual[kept] = after
+        n3_own[kept] = normed
+        inverses[1, kept] = jnp.broadcast_to(inverse, (half, LANES))
+        h3[split.own(r)] = (normed * vectors[8:9]).astype(BF16)
+
+    gathers = settle(scatters, body_two, h3)
+    released += gathers
     ready(8, 9)
     scatters = []
     for r in range(chunks):
-        wait_all(gathers[r])
-        spot = chunk_rows(r)
+        chain.finish(gathers[r])
+        spot = split.chunk(r)
         narrow = dot(h3[spot], full[8]).astype(BF16)
         q3[spot] = dot(narrow, spread[...]).astype(BF16)
-
-        @pl.loop(0, heads)
-        def _(h):
-            lanes = pl.ds(pl.multiple_of(h * LANES, LANES), LANES)
+        chain.tick()
+        for h in range(heads):
+            lanes = slice(h * LANES, (h + 1) * LANES)
             scores = dot_tr(q3[spot, lanes], kv3[0, :, lanes]) * scale
             attend = softmax_tile(jnp.where(word_live[0:1] > 0.5, scores, NEGATIVE))
             wide_context[spot, lanes] = dot(attend.astype(BF16), kv3[1, :, lanes]).astype(BF16)
-
-        scatters.append((ring.used, emit(r, o3, 9)))
-
-    gathers = []
-    for r in range(chunks):
-        stage, copies = scatters[r]
-        wait_all(copies)
-        after = residual[kept(r)] + branch(r, stage)
+        chain.tick()
+        scatters.append(emit(r, o3, 9, 2))
+
+    def body_three(r):
+        kept = split.kept(r)
+        after = residual[kept] + branch(r, 2)
         normed, inverse = norm_tile(after)
-        x3_own[kept(r)] = after
-        n4_own[kept(r)] = normed
-        inverses[2, kept(r)] = jnp.broadcast_to(inverse, (quarter, LANES))
-        h4[own_rows(r)] = (normed * vectors[4:5] + vectors[3:4]).astype(BF16)
-        gathers.append(ring.gather(h4.at[own_rows(r)]))
-    for copies in gathers:
-        wait_all(copies)
+        x3_own[kept] = after
+        n4_own[kept] = normed
+        inverses[2, kept] = jnp.broadcast_to(inverse, (half, LANES))
+        h4[split.own(r)] = (normed * vectors[4:5] + vectors[3:4]).astype(BF16)
+
+    gathers = settle(scatters, body_three, h4)
+    for move in gathers:
+        chain.finish(move)
+    for move in sent + released + gathers:
+        chain.release(move)
 
 
 def forward_call(sizes, frames, vectors, key_live, word_live, spread, prompt, weights):
@@ -408,12 +574,11 @@
     rows = frame_count * cols
     tokens = rows * chunks
     head_width, padded = spread.shape
-    quarter = rows // sizes[TENSOR]
-    peers = sizes[TENSOR] - 1
-    kept = quarter * chunks
+    half = rows // sizes[TENSOR]
+    kept = half * chunks
     full_rows = weights[0].shape[0] * sizes[WIDE]
     prompt_width = weights[10].shape[0] * sizes[WIDE]
-    stages = 6 * chunks
+    moves = 6 * chunks
     s = jax.ShapeDtypeStruct
     wide_act, heads_act = s((tokens, width), BF16), s((tokens, head_width), BF16)
     triple, own = s((3, tokens, padded), BF16), s((kept, width), F32)
@@ -433,12 +598,12 @@
             VMEM((10, full_rows, head_width), BF16),
             VMEM((2, prompt_width, head_width), BF16),
             VMEM((tokens, padded), BF16),
-            VMEM((chunks, rows, width), BF16),
-            VMEM((stages, peers, quarter, width), BF16),
+            VMEM((tokens, width), BF16),
+            VMEM((3 * chunks, 4, half, width), BF16),
             VMEM((kept, width), F32),
             VMEM((rows, rows), F32),
             DMA((12,)), DMA((12,)), DMA((12,)), DMA((2,)), DMA((2,)),
-            DMA((stages, peers)), DMA((stages, peers)),
+            DMA((moves, 4, GRANULES)), DMA((moves, 4, GRANULES)),
         ],
         compiler_params=pltpu.CompilerParams(
             collective_id=1, has_side_effects=True, vmem_limit_bytes=60 << 20
@@ -449,7 +614,7 @@
 def prepare(sizes, frames, timestep, clip_lengths, text_lengths, modulation_weight,
             modulation_bias, time_gain, time_gate, cross_gain, head_width):
     frame_count, width = frames.shape[1], frames.shape[4]
-    cols = frames.shape[3]
+    cols = frames.shape[2] * frames.shape[3] // CHUNKS
     half_width = width // 2
     frequency = jnp.exp(-math.log(10000.0) * jnp.arange(half_width, dtype=F32) / half_width)
     angles = timestep[0].astype(F32) * frequency
@@ -495,21 +660,34 @@
 GELU_C = math.sqrt(2.0 / math.pi)
 
 
+def live_rows(live, split):
+    pieces = [
+        jnp.broadcast_to(
+            live[split.place.t * split.frames + f, 0:1, 0:1], (split.cols, 1)
+        )
+        for f in range(split.frames)
+    ]
+    return jnp.concatenate(pieces, 0)
+
+
+def own_cotangent(cotangent, live, split, r):
+    width = cotangent.shape[3]
+    rows = cotangent[split.own_frames(), r].reshape(split.quarter, width)
+    return rows.astype(F32) * live_rows(live, split)
+
+
 def mlp_kernel(
     sizes,
-    h4, cotangent, vectors, live, n4_own, inverses, x3_own, up_half, down_half,
-    output, e3, g3_own, up_grad, down_grad, sums,
+    h4, cotangent, vectors, live, n4_own, inverses, up_half, down_half,
+    branch_part, e3, g3_own, up_grad, down_grad, sums,
     up, down, e4, hidden, pre_grad, partial, landing,
     local_sems, side_send, side_recv, ring_send, ring_recv,
 ):
     place = Place(sizes)
-    peers = sizes[TENSOR] - 1
     frame_count, chunks, cols, width = cotangent.shape
-    rows = frame_count * cols
-    quarter = rows // sizes[TENSOR]
-    own_frames = frame_count // sizes[TENSOR]
-    ring = Ring(place, quarter, ring_send, ring_recv)
-    greet([place.sibling()] + [place.over_tensor(step) for step in range(1, peers + 1)])
+    split = Split(place, frame_count, chunks, cols)
+    line = Line(place, ring_send, ring_recv)
+    greet(neighbours(place))
     copies = []
     for i, (source, target) in enumerate(((up_half, up), (down_half, down))):
         half = source.shape[0]
@@ -523,15 +701,16 @@
 
     @pl.loop(0, frame_count)
     def _(f):
-        for r in range(chunks):
-            e4[pl.ds(pl.multiple_of(r * rows + f * cols, cols), cols)] = (
+        for r, spot in enumerate(split.spots(f)):
+            e4[spot] = (
                 vectors[5:6] * (cotangent[f, r].astype(F32) * live[f, 0:1, 0:1])
             ).astype(BF16)
 
+    sums[...] = jnp.zeros_like(sums)
     wait_all(copies)
     scatters = []
     for r in range(chunks):
-        spot = pl.ds(r * rows, rows)
+        spot = split.chunk(r)
 
         def act(lanes):
             pre = dot(h4[spot], up[:, lanes])
@@ -545,12 +724,17 @@
             pre_grad[spot, lanes] = (grad * slope).astype(BF16)
 
         over_columns(up.shape[1], 256, act)
-        partial[r] = dot_tr(pre_grad[spot], up[...]).astype(BF16)
-        scatters.append((ring.used, ring.scatter(partial.at[r], landing.at[ring.used])))
+        line.tick(1, 1)
+        partial[spot] = dot_tr(pre_grad[spot], up[...]).astype(BF16)
+        line.tick(1, 1)
+        scatters.append(
+            line.start(True, split.rows_view(partial, r), split.landing_view(landing.at[r]))
+        )
 
     for r in range(chunks):
-        spot = pl.ds(r * rows, rows)
-        partial[chunks + r] = dot_tr(hidden[spot], down[...]).astype(BF16)
+        spot = split.chunk(r)
+        branch_part[spot] = dot_tr(hidden[spot], down[...]).astype(BF16)
+        line.tick(1, 1)
 
     def down_tile(lanes):
         down_grad[:, lanes] = dot_outer(e4[...], hidden[:, lanes]).astype(BF16)
@@ -558,95 +742,62 @@
     def up_tile(lanes):
         up_grad[:, lanes] = dot_outer(h4[...], pre_grad[:, lanes]).astype(BF16)
 
-    over_columns(up.shape[1], 256, down_tile)
-
-    own = pl.ds(pl.multiple_of(place.t * quarter, quarter), quarter)
-    own_spot = pl.ds(place.t * own_frames, own_frames)
-    shift_sum = jnp.zeros((1, width), F32)
-    scale_sum = jnp.zeros((1, width), F32)
-    gate_sum = jnp.zeros((1, width), F32)
-
-    def own_live(r):
-        pieces = []
-        for f in range(own_frames):
-            pieces.append(
-                jnp.broadcast_to(live[place.t * own_frames + f, 0:1, 0:1], (cols, 1))
-            )
-        return jnp.concatenate(pieces, 0)
-
-    def own_upstream(r):
-        return cotangent[own_spot, r].reshape(quarter, width).astype(F32) * own_live(r)
-
     gathers = []
     for r in range(chunks):
-        kept = pl.ds(r * quarter, quarter)
-        stage, copies = scatters[r]
-        wait_all(copies)
-        grad = summed(partial.at[r], landing.at[stage], own, peers)
+        kept = split.kept(r)
+        line.finish(scatters[r])
+        grad = split.total(partial, landing.at[r], r)
         normed = n4_own[kept]
-        shift_sum = shift_sum + jnp.sum(grad, 0, keepdims=True)
-        scale_sum = scale_sum + jnp.sum(grad * normed, 0, keepdims=True)
-        upstream = own_upstream(r) + norm_pull(
+        sums[0:1] += jnp.sum(grad, 0, keepdims=True)
+        sums[1:2] += jnp.sum(grad * normed, 0, keepdims=True)
+        upstream = own_cotangent(cotangent, live, split, r) + norm_pull(
             normed, inverses[2, kept][:, 0:1], grad * vectors[4:5]
         )
         g3_own[kept] = upstream
-        rows_own = pl.ds(pl.multiple_of(r * rows + place.t * quarter, quarter), quarter)
-        e3[rows_own] = upstream.astype(BF16)
-        gathers.append(ring.gather(e3.at[rows_own]))
-    scatters = []
-    for r in range(chunks):
-        scatters.append((ring.used, ring.scatter(partial.at[chunks + r], landing.at[ring.used])))
+        e3[split.own(r)] = upstream.astype(BF16)
+        gathers.append(line.start(False, split.rows_view(e3, r)))
+        if r == 0:
+            over_columns(up.shape[1], 256, down_tile)
+            line.tick(2, 1)
 
     over_columns(up.shape[1], 256, up_tile)
-
-    for r in range(chunks):
-        kept = pl.ds(r * quarter, quarter)
-        stage, copies = scatters[r]
-        wait_all(copies)
-        branch = summed(partial.at[chunks + r], landing.at[stage], own, peers)
-        gate_sum = gate_sum + jnp.sum(own_upstream(r) * branch, 0, keepdims=True)
-        after = (x3_own[kept] + vectors[5:6] * branch) * own_live(r)
-        output[own_spot, r] = after.astype(BF16).reshape(own_frames, cols, width)
-        gathers.append(ring.gather(output.at[own_spot, r]))
-    sums[...] = jnp.concatenate(
-        [shift_sum, scale_sum, gate_sum, jnp.zeros((5, width), F32)], 0
-    )
-    for copies in gathers:
-        wait_all(copies)
-
-
-def mlp_call(sizes, h4, cotangent, vectors, live, n4_own, inverses, x3_own, up_half, down_half):
+    for move in gathers:
+        line.finish(move)
+    for move in scatters + gathers:
+        line.release(move)
+
+
+def mlp_call(sizes, h4, cotangent, vectors, live, n4_own, inverses, up_half, down_half):
     frame_count, chunks, cols, width = cotangent.shape
     rows = frame_count * cols
     tokens = rows * chunks
     quarter = rows // sizes[TENSOR]
-    peers = sizes[TENSOR] - 1
     hidden = up_half.shape[1]
     s = jax.ShapeDtypeStruct
-    stages = 4 * chunks
-    live = jnp.broadcast_to(live.astype(F32)[:, None, None], (frame_count, 8, LANES))
+    moves = 2 * chunks
     outs = [
-        s(cotangent.shape, BF16), s((tokens, width), BF16), s((quarter * chunks, width), F32),
+        s((tokens, width), BF16), s((tokens, width), BF16), s((quarter * chunks, width), F32),
         s((width, hidden), BF16), s((width, hidden), BF16), s((8, width), F32),
     ]
     return pl.pallas_call(
         functools.partial(mlp_kernel, sizes),
         name="mlp",
         out_shape=outs,
-        in_specs=[VM] * 7 + [ANY] * 2,
+        in_specs=[VM] * 6 + [ANY] * 2,
         out_specs=[VM] * len(outs),
         scratch_shapes=[
             VMEM((width, hidden), BF16), VMEM((width, hidden), BF16),
             VMEM((tokens, width), BF16), VMEM((tokens, hidden), BF16),
             VMEM((tokens, hidden), BF16),
-            VMEM((2 * chunks, rows, width), BF16),
-            VMEM((stages, peers, quarter, width), BF16),
-            DMA((2,)), DMA((2,)), DMA((2,)), DMA((stages, peers)), DMA((stages, peers)),
+            VMEM((tokens, width), BF16),
+            VMEM((chunks, 4, quarter, width), BF16),
+            DMA((2,)), DMA((2,)), DMA((2,)),
+            DMA((moves, 4, GRANULES)), DMA((moves, 4, GRANULES)),
         ],
         compiler_params=pltpu.CompilerParams(
             collective_id=2, has_side_effects=True, vmem_limit_bytes=60 << 20
         ),
-    )(h4, cotangent, vectors, live, n4_own, inverses, x3_own, up_half, down_half)
+    )(h4, cotangent, vectors, live, n4_own, inverses, up_half, down_half)
 
 
 class Reducer:
@@ -783,63 +934,50 @@
     *refs,
 ):
     halves, gradients = refs[:6], refs[6:8]
-    g1_own, e1, query_out, value_out, word_grads, up_out, down_out, sums = refs[8:16]
+    g1_own, e1, time_grads, word_grads, up_out, down_out, cross_out, sums = refs[8:16]
     (
         full, wide_grad, wide_parts, narrow_parts, word_sums, word_side, e2, partial, landing,
-        group_mask, local_sems, side_send, side_recv, word_send, word_recv, ring_send, ring_recv,
-    ) = refs[16:33]
+        group_mask, cross_grads,
+        local_sems, side_send, side_recv, word_send, word_recv, ring_send, ring_recv,
+    ) = refs[16:34]
     place = Place(sizes)
-    peers = sizes[TENSOR] - 1
     tokens, width = e3.shape
-    chunks = tokens // group_mask.shape[0]
-    rows = tokens // chunks
-    cols = sizes[COLS]
-    quarter = rows // sizes[TENSOR]
+    rows, cols = group_mask.shape[0], sizes[COLS]
+    chunks = tokens // rows
+    split = Split(place, rows // cols, chunks, cols)
     heads = spread.shape[1] // LANES
     scale = 1.0 / math.sqrt(HEAD_DIM)
-    ring = Ring(place, quarter, ring_send, ring_recv)
+    line = Line(place, ring_send, ring_recv)
     greet(all_partners(place))
     pending = fetch_weights(place, halves, full, local_sems, side_send, side_recv)
-    feed = reducers(place, gradients, refs[33:])
+    feed = reducers(place, gradients, refs[34:42])
+    cross = reducers(place, [cross_grads.at[0], cross_grads.at[1]], refs[42:50])
     for job in feed:
         job.split()
-
-    row_id = lax.broadcasted_iota(jnp.int32, (rows, rows), 0)
-    col_id = lax.broadcasted_iota(jnp.int32, (rows, rows), 1)
-    group_mask[...] = jnp.where(
-        lax.rem(row_id, cols) == lax.rem(col_id, cols),
-        jnp.broadcast_to(key_live[0:1], (rows, rows)),
-        0.0,
-    )
-    own = pl.ds(pl.multiple_of(place.t * quarter, quarter), quarter)
-
-    def chunk_rows(r):
-        return pl.ds(r * rows, rows)
-
-    def own_rows(r):
-        return pl.ds(pl.multiple_of(r * rows + place.t * quarter, quarter), quarter)
-
-    def kept(r):
-        return pl.ds(r * quarter, quarter)
-
-    def head_lanes(h):
-        return pl.ds(pl.multiple_of(h * LANES, LANES), LANES)
+    write_group_mask(group_mask, key_live, cols)
+    sums[...] = jnp.zeros_like(sums)
+    word_sums[...] = jnp.zeros_like(word_sums)
 
     def context_grad(source, spot, weight):
         narrow = dot(source[spot], full[weight]).astype(BF16)
         wide_grad[spot] = dot(narrow, spread[...]).astype(BF16)
 
-    word_sums[...] = jnp.zeros_like(word_sums)
+    def scatter(r, stage):
+        return line.start(
+            True,
+            split.rows_view(partial, r),
+            split.landing_view(landing.at[stage * chunks + r]),
+        )
+
     wait_all(pending[0])
     wait_all(pending[1])
     scatters = []
     for r in range(chunks):
-        spot = chunk_rows(r)
+        spot = split.chunk(r)
         context_grad(e3, spot, 0)
-
-        @pl.loop(0, heads)
-        def _(h):
-            lanes = head_lanes(h)
+        line.tick()
+        for h in range(heads):
+            lanes = slice(h * LANES, (h + 1) * LANES)
             query_grad, key_grad, value_grad = attention_pull(
                 q3[spot, lanes], kv3[0, :, lanes], kv3[1, :, lanes], wide_grad[spot, lanes],
                 word_live[0:1] > 0.5, scale,
@@ -847,111 +985,120 @@
             wide_parts[0, spot, lanes] = query_grad.astype(BF16)
             word_sums[0, :, lanes] += key_grad
             word_sums[1, :, lanes] += value_grad
-
+        line.tick()
         narrow_parts[0, spot] = dot_tr(wide_parts[0, spot], spread[...]).astype(BF16)
-        partial[r] = dot_tr(narrow_parts[0, spot], full[1]).astype(BF16)
-        scatters.append((ring.used, ring.scatter(partial.at[r], landing.at[ring.used])))
+        partial[spot] = dot_tr(narrow_parts[0, spot], full[1]).astype(BF16)
+        scatters.append(scatter(r, 0))
     word_copy = send(word_sums, word_side, word_send, word_recv, place.sibling())
-    value_out[0] = dot_outer(e3[...], o3[...]).astype(BF16)
-    query_out[0] = dot_outer(h3[...], narrow_parts[0]).astype(BF16)
-    for job in feed:
-        job.spread()
-
-    gain_sum = jnp.zeros((1, width), F32)
-    gate_sum = jnp.zeros((1, width), F32)
-    time_sum = jnp.zeros((1, width), F32)
+    cross_grads[0] = dot_outer(e3[...], o3[...]).astype(BF16)
+    line.tick(2)
+    cross_grads[1] = dot_outer(h3[...], narrow_parts[0]).astype(BF16)
+    line.tick(2)
+    for job in cross:
+        job.split()
     gathers = []
     for r in range(chunks):
-        stage, copies = scatters[r]
-        wait_all(copies)
-        grad = summed(partial.at[r], landing.at[stage], own, peers)
-        normed = n3_own[kept(r)]
-        gain_sum = gain_sum + jnp.sum(grad * normed, 0, keepdims=True)
-        upstream = g3_own[kept(r)] + norm_pull(
-            normed, inverses[1, kept(r)][:, 0:1], grad * vectors[8:9]
+        kept = split.kept(r)
+        line.finish(scatters[r])
+        grad = split.total(partial, landing.at[r], r)
+        normed = n3_own[kept]
+        sums[0:1] += jnp.sum(grad * normed, 0, keepdims=True)
+        upstream = g3_own[kept] + norm_pull(
+            normed, inverses[1, kept][:, 0:1], grad * vectors[8:9]
         )
-        g1_own[kept(r)] = upstream
-        gate_sum = gate_sum + jnp.sum(upstream * a2_own[kept(r)], 0, keepdims=True)
-        e2[own_rows(r)] = (vectors[7:8] * upstream).astype(BF16)
-        gathers.append(ring.gather(e2.at[own_rows(r)]))
+        g1_own[kept] = upstream
+        sums[1:2] += jnp.sum(upstream * a2_own[kept], 0, keepdims=True)
+        e2[split.own(r)] = (vectors[7:8] * upstream).astype(BF16)
+        gathers.append(line.start(False, split.rows_view(e2, r)))
+        if r == 0:
+            for job in feed:
+                job.spread()
+    for job in cross:
+        job.spread()
     word_copy.wait()
     for j in range(2):
         word_grads[j] = dot_tr(
             (word_sums[j] + word_side[j]).astype(BF16), spread[...]
         ).astype(BF16)
+    sent = scatters + gathers
 
     for copies in pending[2:]:
         wait_all(copies)
-    scatters = []
+    former, scatters = scatters, []
     for r in range(chunks):
-        spot = chunk_rows(r)
-        wait_all(gathers[r])
+        spot = split.chunk(r)
+        line.finish(gathers[r])
         context_grad(e2, spot, 2)
-
-        @pl.loop(0, heads)
-        def _(h):
-            lanes = head_lanes(h)
+        line.tick()
+        for h in range(heads):
+            lanes = slice(h * LANES, (h + 1) * LANES)
             parts = attention_pull(
                 q2[0, spot, lanes], q2[1, spot, lanes], q2[2, spot, lanes],
                 wide_grad[spot, lanes], group_mask[...] > 0.5, scale,
             )
             for i in range(3):
                 wide_parts[i, spot, lanes] = parts[i].astype(BF16)
-
-        @pl.loop(0, 3)
-        def _(i):
+            if h % 2:
+                line.tick()
+        total = None
+        for i in range(3):
             narrow_parts[i, spot] = dot_tr(wide_parts[i, spot], spread[...]).astype(BF16)
-
-        total = dot_tr(narrow_parts[0, spot], full[3])
-        for i in (1, 2):
-            total = total + dot_tr(narrow_parts[i, spot], full[3 + i])
-        partial[r] = total.astype(BF16)
-        scatters.append((ring.used, ring.scatter(partial.at[r], landing.at[ring.used])))
-    value_out[1] = dot_outer(e2[...], o2[...]).astype(BF16)
-
-    @pl.loop(0, 3)
-    def _(i):
-        query_out[1 + i] = dot_outer(h2[...], narrow_parts[i]).astype(BF16)
+            part = dot_tr(narrow_parts[i, spot], full[3 + i])
+            total = part if total is None else total + part
+        line.tick()
+        line.release(former[r])
+        sent.remove(former[r])
+        partial[spot] = total.astype(BF16)
+        scatters.append(scatter(r, 1))
+    sent += scatters
+    time_grads[0] = dot_outer(e2[...], o2[...]).astype(BF16)
+    line.tick(2)
+    for i in range(3):
+        time_grads[1 + i] = dot_outer(h2[...], narrow_parts[i]).astype(BF16)
+        line.tick(1)
 
     gathers = []
     for r in range(chunks):
-        stage, copies = scatters[r]
-        wait_all(copies)
-        grad = summed(partial.at[r], landing.at[stage], own, peers)
-        normed = n2_own[kept(r)]
-        time_sum = time_sum + jnp.sum(grad * normed, 0, keepdims=True)
-        upstream = g1_own[kept(r)] + norm_pull(
-            normed, inverses[0, kept(r)][:, 0:1], grad * vectors[6:7]
+        kept = split.kept(r)
+        line.finish(scatters[r])
+        grad = split.total(partial, landing.at[chunks + r], r)
+        normed = n2_own[kept]
+        sums[2:3] += jnp.sum(grad * normed, 0, keepdims=True)
+        upstream = g1_own[kept] + norm_pull(
+            normed, inverses[0, kept][:, 0:1], grad * vectors[6:7]
         )
-        g1_own[kept(r)] = upstream
-        e1[own_rows(r)] = (vectors[2:3] * upstream).astype(BF16)
-        gathers.append(ring.gather(e1.at[own_rows(r)]))
+        g1_own[kept] = upstream
+        e1[split.own(r)] = (vectors[2:3] * upstream).astype(BF16)
+        gathers.append(line.start(False, split.rows_view(e1, r)))
+    for r in range(chunks):
+        line.drain(gathers[r])
     feed[0].finish(up_out)
     feed[1].finish(down_out)
-    sums[...] = jnp.concatenate([gain_sum, gate_sum, time_sum, jnp.zeros((5, width), F32)], 0)
-    for copies in gathers:
-        wait_all(copies)
+    cross[0].finish(cross_out.at[0])
+    cross[1].finish(cross_out.at[1])
+    for move in gathers:
+        line.finish(move)
+    for move in sent + gathers:
+        line.release(move)
 
 
 def back_call(sizes, cols, acts, halves, gradients):
     e3, spread = acts[0], acts[9]
     tokens, width = e3.shape
-    key_live = acts[7]
-    rows = key_live.shape[1]
+    rows = acts[7].shape[1]
     chunks = tokens // rows
     quarter = rows // sizes[TENSOR]
-    peers = sizes[TENSOR] - 1
     head_width, padded = spread.shape
     full_rows = halves[0].shape[0] * sizes[WIDE]
     hidden = gradients[0].shape[1]
     block = width // (sizes[NARROW] * sizes[WIDE])
     s = jax.ShapeDtypeStruct
-    stages = 4 * chunks
+    moves = 4 * chunks
     outs = [
         s((quarter * chunks, width), F32), s((tokens, width), BF16),
-        s((4, width, head_width), BF16), s((2, width, head_width), BF16),
-        s((2, LANES, head_width), BF16),
-        s((block, hidden), F32), s((block, hidden), F32), s((8, width), F32),
+        s((4, width, head_width), BF16), s((2, LANES, head_width), BF16),
+        s((block, hidden), F32), s((block, hidden), F32), s((2, block, head_width), F32),
+        s((8, width), F32),
     ]
     return pl.pallas_call(
         functools.partial(back_kernel, {**sizes, COLS: cols}),
@@ -966,13 +1113,15 @@
             VMEM((3, tokens, head_width), BF16),
             VMEM((2, LANES, padded), F32), VMEM((2, LANES, padded), F32),
             VMEM((tokens, width), BF16),
-            VMEM((chunks, rows, width), BF16),
-            VMEM((stages, peers, quarter, width), BF16),
+            VMEM((tokens, width), BF16),
+            VMEM((2 * chunks, 4, quarter, width), BF16),
             VMEM((rows, rows), F32),
+            VMEM((2, width, head_width), BF16),
             DMA((6,)), DMA((6,)), DMA((6,)), DMA(()), DMA(()),
-            DMA((stages, peers)), DMA((stages, peers)),
+            DMA((moves, 4, GRANULES)), DMA((moves, 4, GRANULES)),
         ]
-        + reducer_scratch(sizes, 2, block, hidden),
+        + reducer_scratch(sizes, 2, block, hidden)
+        + reducer_scratch(sizes, 2, block, head_width),
         compiler_params=pltpu.CompilerParams(
             collective_id=3, has_side_effects=True, vmem_limit_bytes=60 << 20
         ),
@@ -982,177 +1131,233 @@
 def space_kernel(
     sizes,
     e1, g1_own, frames, a1_own, vectors, spread, h1, q1, side, o1, prompt, word_grads,
+    branch_part, x3_own, cotangent, live, mlp_sums, back_sums, condition,
     *refs,
 ):
-    halves, early_value, early_query = refs[:4], refs[4], refs[5]
-    frames_grad, early_out, space_out, prompt_out, sums = refs[6:11]
+    halves, gradients = refs[:4], refs[4]
+    frames_grad, output, early_out, space_out, prompt_out, merged, conditions = refs[5:12]
     (
         full, wide_grad, wide_parts, narrow_parts, key_sums, side_out, side_in, space_grads,
-        words, word_parts, partial, landing,
+        words, word_parts, partial, landing, tally, tally_side, tally_peers,
         local_sems, side_send, side_recv, key_send, key_recv, word_send, word_recv,
-        ring_send, ring_recv,
-    ) = refs[11:32]
+        tally_send, tally_recv, ring_send, ring_recv,
+    ) = refs[12:38]
+    early_scratch, late_scratch = refs[38:46], refs[46:54]
     place = Place(sizes)
-    peers = sizes[TENSOR] - 1
     clips = sizes[NARROW]
     frame_count, chunks, cols, width = frames.shape
-    rows = frame_count * cols
-    tokens = rows * chunks
-    quarter = rows // sizes[TENSOR]
-    own_frames = frame_count // sizes[TENSOR]
+    split = Split(place, frame_count, chunks, cols)
+    quarter = split.quarter
     heads = spread.shape[1] // LANES
-    half = chunks * cols
     scale = 1.0 / math.sqrt(HEAD_DIM)
-    ring = Ring(place, quarter, ring_send, ring_recv)
+    line = Line(place, ring_send, ring_recv)
     greet(all_partners(place))
+
+    def scatter(source, r, stage):
+        return line.start(
+            True,
+            split.rows_view(source, r),
+            split.landing_view(landing.at[stage * chunks + r]),
+        )
+
+    feed_scatters = [scatter(branch_part, r, 1) for r in range(chunks)]
     pending = fetch_weights(place, halves, full, local_sems, side_send, side_recv)
-    early_scratch, late_scratch = refs[32:40], refs[40:48]
-    sources = [early_value.at[0], early_query.at[0], early_value.at[1]] + [
-        early_query.at[1 + i] for i in range(3)
-    ]
-    early = reducers(place, sources, early_scratch)
+    early = reducers(place, [gradients.at[i] for i in range(4)], early_scratch)
     late = reducers(place, [space_grads.at[i] for i in range(4)], late_scratch)
+    for job in early:
+        job.split()
     block = words.shape[2]
+    far = [lax.rem(place.n + step, clips) for step in range(1, clips)]
     word_copies = []
-    for step in range(1, clips):
-        peer = lax.rem(place.n + step, clips)
-        lanes = pl.ds(
-            pl.multiple_of((peer * sizes[WIDE] + place.w) * block, block), block
-        )
+    for i, peer in enumerate(far):
+        lanes = pl.ds(pl.multiple_of((peer * sizes[WIDE] + place.w) * block, block), block)
         for j, (source, target) in enumerate(
-            ((prompt.at[:, lanes], words.at[step]), (word_grads, word_parts.at[step]))
+            (
+                (prompt.at[:, lanes], words.at[i + 1]),
+                (word_grads, word_parts.at[i + 1]),
+                (condition, conditions.at[place.n]),
+            )
         ):
             word_copies.append(
                 send(
-                    source, target, word_send.at[step - 1, j], word_recv.at[step - 1, j],
+                    source, target, word_send.at[i, j], word_recv.at[i, j],
                     place.over_narrow(peer),
                 )
             )
-    for job in early:
-        job.split()
     mine = pl.ds(pl.multiple_of((place.n * sizes[WIDE] + place.w) * block, block), block)
     words[0] = prompt[:, mine]
     word_parts[0] = word_grads[...]
-    own = pl.ds(pl.multiple_of(place.t * quarter, quarter), quarter)
-    own_spot = pl.ds(place.t * own_frames, own_frames)
-
-    for copies in pending:
-        wait_all(copies)
+    conditions[place.n] = condition[...]
+    tally[...] = jnp.zeros_like(tally)
+    tally[2:3] = jnp.sum(g1_own[...] * a1_own[...], 0, keepdims=True)
+    tally[3:5] = mlp_sums[0:2]
+    tally[6:9] = back_sums[0:3]
+
+    wait_all(pending[0])
     for r in range(chunks):
-        spot = pl.ds(r * rows, rows)
+        spot = split.chunk(r)
         narrow = dot(e1[spot], full[0]).astype(BF16)
         wide_grad[spot] = dot(narrow, spread[...]).astype(BF16)
-
-    @pl.loop(0, frame_count)
-    def _(f):
-        spots = [
-            pl.ds(pl.multiple_of(r * rows + f * cols, cols), cols) for r in range(chunks)
-        ]
-        queries = jnp.concatenate([q1[0, spot] for spot in spots], 0)
-        grads = jnp.concatenate([wide_grad[spot] for spot in spots], 0)
-        keys = jnp.concatenate(
-            [q1[1, spot] for spot in spots] + [side[0, spot] for spot in spots], 0
+        line.tick()
+
+    def attend(first, stop):
+        @pl.loop(first, stop)
+        def _(f):
+            spots = split.spots(f)
+            queries = jnp.concatenate([q1[0, spot] for spot in spots], 0)
+            grads = jnp.concatenate([wide_grad[spot] for spot in spots], 0)
+            keys = jnp.concatenate(
+                [q1[1, spot] for spot in spots] + [side[0, spot] for spot in spots], 0
+            )
+            values = jnp.concatenate(
+                [q1[2, spot] for spot in spots] + [side[1, spot] for spot in spots], 0
+            )
+            for h in range(heads):
+                lanes = slice(h * LANES, (h + 1) * LANES)
+                parts = attention_pull(
+                    queries[:, lanes], keys[:, lanes], values[:, lanes], grads[:, lanes],
+                    None, scale,
+                )
+                for r in range(chunks):
+                    here = slice(r * cols, (r + 1) * cols)
+                    there = slice((chunks + r) * cols, (chunks + r + 1) * cols)
+                    wide_parts[0, spots[r], lanes] = parts[0][here].astype(BF16)
+                    for j in range(2):
+                        key_sums[j, spots[r], lanes] = parts[1 + j][here]
+                        side_out[j, spots[r], lanes] = parts[1 + j][there].astype(BF16)
+
+    outputs = []
+
+    def finish_feed(r):
+        kept = split.kept(r)
+        line.finish(feed_scatters[r])
+        branch = split.total(branch_part, landing.at[chunks + r], r)
+        tally[5:6] += jnp.sum(
+            own_cotangent(cotangent, live, split, r) * branch, 0, keepdims=True
         )
-        values = jnp.concatenate(
-            [q1[2, spot] for spot in spots] + [side[1, spot] for spot in spots], 0
-        )
-        for h in range(heads):
-            lanes = slice(h * LANES, (h + 1) * LANES)
-            parts = attention_pull(
-                queries[:, lanes], keys[:, lanes], values[:, lanes], grads[:, lanes], None, scale
-            )
-            for r in range(chunks):
-                here = slice(r * cols, (r + 1) * cols)
-                there = slice(half + r * cols, half + (r + 1) * cols)
-                wide_parts[0, spots[r], lanes] = parts[0][here].astype(BF16)
-                for j in range(2):
-                    key_sums[j, spots[r], lanes] = parts[1 + j][here]
-                    side_out[j, spots[r], lanes] = parts[1 + j][there].astype(BF16)
-
+        after = (x3_own[kept] + vectors[5:6] * branch) * live_rows(live, split)
+        output[split.own_frames(), r] = after.astype(BF16).reshape(split.frames, cols, width)
+        outputs.append(line.start(False, split.frames_view(output, r)))
+
+    quarters = frame_count // 4
+    for part in range(4):
+        attend(part * quarters, (part + 1) * quarters)
+        line.tick(2)
+        if part >= 2 and part - 2 < chunks:
+            finish_feed(part - 2)
+    for r in range(2, chunks):
+        finish_feed(r)
     key_copy = send(side_out, side_in, key_send, key_recv, place.sibling())
     for job in early:
         job.spread()
-    space_grads[0] = dot_outer(e1[...], o1[...]).astype(BF16)
     narrow_parts[0] = dot_tr(wide_parts[0], spread[...]).astype(BF16)
+    line.tick(2)
+    for copies in pending[1:]:
+        wait_all(copies)
     key_copy.wait()
     for j in range(2):
         wide_parts[1 + j] = (key_sums[j] + side_in[j].astype(F32)).astype(BF16)
         narrow_parts[1 + j] = dot_tr(wide_parts[1 + j], spread[...]).astype(BF16)
+    line.tick(2)
     scatters = []
     for r in range(chunks):
-        spot = pl.ds(r * rows, rows)
+        spot = split.chunk(r)
         total = dot_tr(narrow_parts[0, spot], full[1])
         for i in (1, 2):
             total = total + dot_tr(narrow_parts[i, spot], full[1 + i])
-        partial[r] = total.astype(BF16)
-        scatters.append((ring.used, ring.scatter(partial.at[r], landing.at[ring.used])))
-
-    @pl.loop(0, 3)
-    def _(i):
+        partial[spot] = total.astype(BF16)
+        scatters.append(scatter(partial, r, 0))
+        line.tick(2)
+
+    space_grads[0] = dot_outer(e1[...], o1[...]).astype(BF16)
+    late[0].split()
+    for i in range(3):
         space_grads[1 + i] = dot_outer(h1[...], narrow_parts[i]).astype(BF16)
-
+        late[1 + i].split()
+        line.tick(2)
     for job in late:
-        job.split()
+        job.spread()
+    gathers = []
+    for r in range(chunks):
+        kept = split.kept(r)
+        line.finish(scatters[r])
+        grad = split.total(partial, landing.at[r], r)
+        x_own = frames[split.own_frames(), r].reshape(quarter, width).astype(F32)
+        normed, inverse = norm_tile(x_own)
+        tally[0:1] += jnp.sum(grad, 0, keepdims=True)
+        tally[1:2] += jnp.sum(grad * normed, 0, keepdims=True)
+        upstream = g1_own[kept] + norm_pull(normed, inverse, grad * vectors[1:2])
+        frames_grad[split.own_frames(), r] = upstream.astype(BF16).reshape(
+            split.frames, cols, width
+        )
+        gathers.append(line.start(False, split.frames_view(frames_grad, r)))
+
+    tally_copy = send(tally, tally_side, tally_send.at[0], tally_recv.at[0], place.sibling())
     wait_all(word_copies)
     for j in range(2):
         total = dot_outer(words[0], word_parts[0, j, 0 : prompt.shape[0]])
         for step in range(1, clips):
             total = total + dot_outer(words[step], word_parts[step, j, 0 : prompt.shape[0]])
         prompt_out[j] = total
-    for job in late:
-        job.spread()
-
-    gate_sum = jnp.zeros((1, width), F32)
-    shift_sum = jnp.zeros((1, width), F32)
-    scale_sum = jnp.zeros((1, width), F32)
-    gathers = []
-    for r in range(chunks):
-        kept = pl.ds(r * quarter, quarter)
-        stage, copies = scatters[r]
-        wait_all(copies)
-        grad = summed(partial.at[r], landing.at[stage], own, peers)
-        x_own = frames[own_spot, r].reshape(quarter, width).astype(F32)
-        normed, inverse = norm_tile(x_own)
-        gate_sum = gate_sum + jnp.sum(g1_own[kept] * a1_own[kept], 0, keepdims=True)
-        shift_sum = shift_sum + jnp.sum(grad, 0, keepdims=True)
-        scale_sum = scale_sum + jnp.sum(grad * normed, 0, keepdims=True)
-        upstream = g1_own[kept] + norm_pull(normed, inverse, grad * vectors[1:2])
-        frames_grad[own_spot, r] = upstream.astype(BF16).reshape(own_frames, cols, width)
-        gathers.append(ring.gather(frames_grad.at[own_spot, r]))
-    sums[...] = jnp.concatenate(
-        [shift_sum, scale_sum, gate_sum, jnp.zeros((5, width), F32)], 0
-    )
+    tally_copy.wait()
+    tally_side[...] = tally_side[...] + tally[...]
+    peer_copies = [
+        send(
+            tally_side, tally_peers.at[step - 1], tally_send.at[step], tally_recv.at[step],
+            place.over_tensor(step),
+        )
+        for step in range(1, sizes[TENSOR])
+    ]
+    for move in gathers:
+        line.drain(move)
     for i, job in enumerate(early):
         job.finish(early_out.at[i])
+    wait_all(peer_copies)
+    total = tally_side[...]
+    for step in range(sizes[TENSOR] - 1):
+        total = total + tally_peers[step]
+    merged[place.n] = total
+    base = sizes[TENSOR]
+    far_copies = [
+        send(
+            merged.at[place.n], merged.at[place.n],
+            tally_send.at[base + i], tally_recv.at[base + i], place.over_narrow(peer),
+        )
+        for i, peer in enumerate(far)
+    ]
     for i, job in enumerate(late):
         job.finish(space_out.at[i])
-    for copies in gathers:
-        wait_all(copies)
+    for move in outputs + gathers:
+        line.finish(move)
+    wait_all(far_copies)
+    for move in feed_scatters + outputs + scatters + gathers:
+        line.release(move)
 
 
 def space_call(sizes, acts, halves, gradients):
-    frames, spread, prompt = acts[2], acts[5], acts[10]
+    frames, spread, prompt, condition = acts[2], acts[5], acts[10], acts[18]
     frame_count, chunks, cols, width = frames.shape
     rows = frame_count * cols
     tokens = rows * chunks
     quarter = rows // sizes[TENSOR]
-    peers = sizes[TENSOR] - 1
     head_width, padded = spread.shape
     full_rows = halves[0].shape[0] * sizes[WIDE]
     parts = sizes[NARROW] * sizes[WIDE]
     block, word_block = width // parts, prompt.shape[1] // parts
-    clips = sizes[NARROW]
+    clips, peers = sizes[NARROW], sizes[TENSOR] - 1
     s = jax.ShapeDtypeStruct
-    stages = 2 * chunks
+    moves = 4 * chunks
     outs = [
-        s(frames.shape, BF16), s((6, block, head_width), F32), s((4, block, head_width), F32),
-        s((2, word_block, head_width), F32), s((8, width), F32),
+        s(frames.shape, BF16), s(frames.shape, BF16),
+        s((4, block, head_width), F32), s((4, block, head_width), F32),
+        s((2, word_block, head_width), F32), s((clips, 16, width), F32),
+        s((clips,) + condition.shape, F32),
     ]
     return pl.pallas_call(
         functools.partial(space_kernel, sizes),
         name="space",
         out_shape=outs,
-        in_specs=[VM] * len(acts) + [ANY] * 6,
+        in_specs=[VM] * len(acts) + [ANY] * 5,
         out_specs=[VM] * len(outs),
         scratch_shapes=[
             VMEM((4, full_rows, head_width), BF16),
@@ -1164,77 +1369,20 @@
             VMEM((4, width, head_width), BF16),
             VMEM((clips, prompt.shape[0], word_block), BF16),
             VMEM((clips, 2, LANES, head_width), BF16),
-            VMEM((chunks, rows, width), BF16),
-            VMEM((stages, peers, quarter, width), BF16),
+            VMEM((tokens, width), BF16),
+            VMEM((2 * chunks, 4, quarter, width), BF16),
+            VMEM((16, width), F32), VMEM((16, width), F32), VMEM((peers, 16, width), F32),
             DMA((4,)), DMA((4,)), DMA((4,)), DMA(()), DMA(()),
-            DMA((clips - 1, 2)), DMA((clips - 1, 2)),
-            DMA((stages, peers)), DMA((stages, peers)),
+            DMA((clips - 1, 3)), DMA((clips - 1, 3)),
+            DMA((peers + clips,)), DMA((peers + clips,)),
+            DMA((moves, 4, GRANULES)), DMA((moves, 4, GRANULES)),
         ]
-        + reducer_scratch(sizes, 6, block, head_width)
+        + reducer_scratch(sizes, 4, block, head_width)
         + reducer_scratch(sizes, 4, block, head_width),
         compiler_params=pltpu.CompilerParams(
             collective_id=4, has_side_effects=True, vmem_limit_bytes=61 << 20
         ),
-    )(*acts, *halves, *gradients)
-
-
-def tail_kernel(sizes, rows, condition, merged, conditions, landing, total, send_sems, recv_sems,
-                far_send, far_recv):
-    place = Place(sizes)
-    partners = []
-    for dw in range(sizes[WIDE]):
-        for dt in range(sizes[TENSOR]):
-            if dw or dt:
-                partners.append(
-                    (
-                        place.n,
-                        lax.rem(place.w + dw, sizes[WIDE]),
-                        lax.rem(place.t + dt, sizes[TENSOR]),
-                    )
-                )
-    far = [
-        place.over_narrow(lax.rem(place.n + step, sizes[NARROW]))
-        for step in range(1, sizes[NARROW])
-    ]
-    greet(partners + far)
-    copies = [
-        send(rows, landing.at[i], send_sems.at[i], recv_sems.at[i], partner)
-        for i, partner in enumerate(partners)
-    ]
-    cond_copies = [
-        send(condition, conditions.at[place.n], far_send.at[i, 1], far_recv.at[i, 1], partner)
-        for i, partner in enumerate(far)
-    ]
-    conditions[place.n] = condition[...]
-    wait_all(copies)
-    value = rows[...]
-    for i in range(len(partners)):
-        value = value + landing[i]
-    total[...] = value
-    far_copies = [
-        send(total, merged.at[place.n], far_send.at[i, 0], far_recv.at[i, 0], partner)
-        for i, partner in enumerate(far)
-    ]
-    merged[place.n] = value
-    wait_all(cond_copies + far_copies)
-
-
-def tail_call(sizes, rows, condition):
-    clips = sizes[NARROW]
-    group = sizes[WIDE] * sizes[TENSOR] - 1
-    s = jax.ShapeDtypeStruct
-    return pl.pallas_call(
-        functools.partial(tail_kernel, sizes),
-        name="tail",
-        out_shape=[s((clips,) + rows.shape, F32), s((clips,) + condition.shape, F32)],
-        in_specs=[VM, VM],
-        out_specs=[VM, VM],
-        scratch_shapes=[
-            VMEM((group,) + rows.shape, F32), VMEM(rows.shape, F32),
-            DMA((group,)), DMA((group,)), DMA((clips - 1, 2)), DMA((clips - 1, 2)),
-        ],
-        compiler_params=pltpu.CompilerParams(collective_id=5, has_side_effects=True),
-    )(rows, condition)
+    )(*acts, *halves, gradients)
 
 
 def fused_on_device(
@@ -1244,41 +1392,40 @@
     time_gain, time_query, time_key, time_value, time_out, time_gate, cross_gain, cross_query,
     prompt_key, prompt_value, cross_out, feed_up, feed_down,
 ):
-    width = frames.shape[4]
-    cols = frames.shape[3]
+    frame_count, width = frames.shape[1], frames.shape[4]
+    cols = frames.shape[2] * frames.shape[3] // CHUNKS
     head_width = space_query.shape[1]
     condition, vectors, live, key_live, word_live, spread = prepare(
         sizes, frames, timestep, clip_lengths, text_lengths, modulation_weight, modulation_bias,
         time_gain, time_gate, cross_gain, head_width,
     )
+    tiles = frames.reshape(frame_count, CHUNKS, cols, width)
+    pulls = cotangent.reshape(frame_count, CHUNKS, cols, width)
+    live = jnp.broadcast_to(live.astype(F32)[:, None, None], (frame_count, 8, LANES))
     (
         h1, q1, side, o1, h2, q2, o2, h3, q3, kv3, o3, h4,
         a1_own, a2_own, x3_own, n2_own, n3_own, n4_own, inverses,
     ) = forward_call(
-        sizes, frames[0], vectors, key_live, word_live, spread, prompt[0],
+        sizes, tiles, vectors, key_live, word_live, spread, prompt[0],
         [space_query, space_key, space_value, space_out, time_query, time_key, time_value,
          time_out, cross_query, cross_out, prompt_key, prompt_value],
     )
-    output, e3, g3_own, up_grad, down_grad, sums_four = mlp_call(
-        sizes, h4, cotangent[0], vectors, live, n4_own, inverses, x3_own, feed_up, feed_down
-    )
-    g1_own, e1, query_out, value_out, word_grads, up_out, down_out, sums_two = back_call(
+    branch_part, e3, g3_own, up_grad, down_grad, mlp_sums = mlp_call(
+        sizes, h4, pulls, vectors, live, n4_own, inverses, feed_up, feed_down
+    )
+    g1_own, e1, time_grads, word_grads, up_out, down_out, cross_grads, back_sums = back_call(
         sizes, cols,
         [e3, g3_own, n3_own, n2_own, inverses, a2_own, vectors, key_live, word_live, spread,
          h3, q3, kv3, o3, h2, q2, o2],
         [cross_out, cross_query, time_out, time_query, time_key, time_value],
         [up_grad, down_grad],
     )
-    frames_grad, early_out, late_out, prompt_out, sums_one = space_call(
+    frames_grad, output, early_out, late_out, prompt_out, merged, conditions = space_call(
         sizes,
-        [e1, g1_own, frames[0], a1_own, vectors, spread, h1, q1, side, o1, prompt[0], word_grads],
+        [e1, g1_own, tiles, a1_own, vectors, spread, h1, q1, side, o1, prompt[0], word_grads,
+         branch_part, x3_own, pulls, live, mlp_sums, back_sums, condition.astype(F32)[None]],
         [space_out, space_query, space_key, space_value],
-        [value_out, query_out],
-    )
-    merged, conditions = tail_call(
-        sizes,
-        jnp.concatenate([sums_one[:3], sums_four[:3], sums_two[:3], jnp.zeros((7, width), F32)]),
-        condition.astype(F32)[None],
+        time_grads,
     )
     part = lax.axis_index(NARROW) * sizes[WIDE] + lax.axis_index(WIDE)
     block = width // (sizes[NARROW] * sizes[WIDE])
@@ -1300,10 +1447,11 @@
     own_gate = jnp.tanh(lax.dynamic_slice_in_dim(time_gate, part * block, block))
     time_gate_grad = gate_rows * (1.0 - own_gate * own_gate)
     return (
-        output[None], frames_grad[None], modulation_weight_grad, modulation_bias_grad,
+        output.reshape(frames.shape), frames_grad.reshape(frames.shape),
+        modulation_weight_grad, modulation_bias_grad,
         late_out[1], late_out[2], late_out[3], late_out[0],
-        time_gain_grad, early_out[3], early_out[4], early_out[5], early_out[2], time_gate_grad,
-        cross_gain_grad, early_out[1], prompt_out[0], prompt_out[1], early_out[0],
+        time_gain_grad, early_out[1], early_out[2], early_out[3], early_out[0], time_gate_grad,
+        cross_gain_grad, cross_grads[1], prompt_out[0], prompt_out[1], cross_grads[0],
         up_out, down_out,
     )
 

time: 595 us -> 466 us (0.78)
  Pallas kernels: 547 us -> 417 us
    pallas_call x1, Pallas kernels: 119 us -> 58.7 us  [mlp_call(): pl.pallas_call(functools.partial(mlp_kernel, sizes), name='mlp', out_shap...]
    pallas_call x1, Pallas kernels: 184 us -> 155 us  [forward_call(): pl.pallas_call(functools.partial(forward_kernel, sizes), name='forward',...]
    pallas_call x1 -> x0, Pallas kernels: 26.5 us -> none  [tail_call(): pl.pallas_call(functools.partial(tail_kernel, sizes), name='tail', out_sh...]
    pallas_call x1, Pallas kernels: 120 us -> 96.8 us  [back_call(): pl.pallas_call(functools.partial(back_kernel, {**sizes, COLS: cols}), nam...]
    pallas_call x1, Pallas kernels: 87.1 us -> 96.2 us  [space_call(): pl.pallas_call(functools.partial(space_kernel, sizes), name='space', out_...]
    unnamed x65 -> x63, local copies, waits for them, and re-layouts: 21.8 us -> 20.8 us
where the time goes in v2:
time: 466 us; the launch traced here: 459 us
  Pallas kernels  417 us (89%)
  local copies, waits for them, and re-layouts  32.1 us (7%)
  other arithmetic  6.92 us (1%)
    pallas_call x1, Pallas kernels, forward_call(): pl.pallas_call(functools.partial(forward_kernel, sizes), name='forward',...  155 us
    pallas_call x1, Pallas kernels, back_call(): pl.pallas_call(functools.partial(back_kernel, {**sizes, COLS: cols}), nam...  96.8 us
    pallas_call x1, Pallas kernels, space_call(): pl.pallas_call(functools.partial(space_kernel, sizes), name='space', out_...  96.2 us
    pallas_call x1, Pallas kernels, mlp_call(): pl.pallas_call(functools.partial(mlp_kernel, sizes), name='mlp', out_shap...  58.7 us
    unnamed x63, local copies, waits for them, and re-layouts  20.8 us
    pallas_call x1, Pallas kernels, modulation_call(): pl.pallas_call(functools.partial(modulation_kernel, sizes), name='modulat...  10.3 us

profile of v2, /device:TPU:0, one launch (start us, length us, event | category | flops | bytes accessed | tf_op | source)
XLA Modules:
  0.0 458.9 jit_solution(12057916671859031486)
XLA Ops:
  0.7 0.0 copy-start.20
  2.6 0.5 compare_convert_fusion.word_live
  3.2 0.1 broadcast_in_dim.9
  3.2 0.6 convert_element_type.68.key_live
  3.9 0.7 stack.14
  4.6 0.7 stack.16
  5.3 0.1 multiply_convert_fusion
  5.4 0.7 convert_convert_fusion.condition
  6.1 0.7 tanh.6
  6.8 0.6 broadcast_in_dim.7.condition
  7.4 0.7 broadcast_in_dim.10.live
  8.1 10.3 %modulation.1 = f32[8,1,1728]{2,1,0:T(1,128)} custom-call(bf16[16,576]{1,0:T(8,128)(2,1)} %broadcast_in_dim.7.condition, bf16[576,1728]{1,0:T(8,128)(2,1)} %weight.1), custom_call_target="tpu_custom_call" | custom-call | tf_op jit(solution)/shard_map/modulation/pallas_call | solution.py:278
  18.4 0.0 copy-start.11
  18.4 0.0 copy-start.12
  18.5 1.0 reduce
  19.5 0.1 reshape.190
  19.6 0.1 reduce_sum.27
  19.7 0.0 copy-done.20
  19.8 1.3 stack.17.vectors
  21.1 0.8 fusion.spread
  21.9 0.0 copy-done.10
  21.9 1.0 copy.94.refs_0_.refs_1_
  22.8 0.0 copy-done.11
  22.8 1.0 copy.95.refs_1_.refs_2_
  23.8 1.0 copy.96.refs_2_.refs_3_
  24.8 1.0 copy.97.refs_3_.refs_0_
  25.7 1.0 copy.98.refs_4_.refs_3_
  26.7 1.0 copy.99.refs_5_.refs_4_
  27.7 1.0 copy.100.refs_6_.refs_5_
  28.6 0.9 copy.101.refs_7_.refs_2_
  29.6 1.0 copy.102.refs_8_.refs_1_
  30.6 1.0 copy.103.refs_9_.refs_0_
  31.6 1.6 copy.104.refs_10_
  33.2 0.0 copy-done.4
  33.2 1.5 copy.105.refs_11_
  34.7 154.9 %forward.1 = (bf16[512,1152]{1,0:T(8,128)(2,1)}, bf16[3,512,512]{2,1,0:T(8,128)(2,1)}, bf16[2,512,512]{2,1,0:T(8,128)(2,1)}, bf16[512,288]{1,0:T(8,128)(2,1)}, b...) custom-call(bf16[8,2,32,1152]{3,2,1,0:T(8,128)(2,1)} %bitcast.43, ...), custom_call_target="tpu_custom_call" | custom-call | tf_op jit(solution)/shard_map/forward/pallas_call | solution.py:591
  189.6 58.7 %mlp.1 = (bf16[512,1152]{1,0:T(8,128)(2,1)}, bf16[512,1152]{1,0:T(8,128)(2,1)}, f32[128,1152]{1,0:T(8,128)}, bf16[1152,1152]{1,0:T(8,128)(2,1)}, bf16[1152,1152]{1,0:T(8,128)(2,1)}, /*index=5*/f32[8,1152]{1,0:T(8,128)}) custom-call(bf16[512,1152]{1,0:T(8,128)(2,1)} %get-tuple-element.61.h4, bf16[8,2,32,1152]{3,2,1,0:T(8,128)(2,1)} %bitcast.45, ...), custom_call_target="tpu_custom_call" | custom-call | tf_op jit(solution)/shard_map/mlp/pallas_call | solution.py:782
  248.3 96.8 %back.1 = (f32[128,1152]{1,0:T(8,128)}, bf16[512,1152]{1,0:T(8,128)(2,1)}, bf16[4,1152,288]{2,1,0:T(8,128)(2,1)}, bf16[2,128,288]{2,1,0:T(8,128)(2,1)}, f32[144,...) custom-call(bf16[512,1152]{1,0:T(8,128)(2,1)} %get-tuple-element.64.e3, ...), custom_call_target="tpu_custom_call" | custom-call | tf_op jit(solution)/shard_map/back/pallas_call | solution.py:1103
  345.1 96.2 %space.1 = (bf16[8,2,32,1152]{3,2,1,0:T(8,128)(2,1)}, bf16[8,2,32,1152]{3,2,1,0:T(8,128)(2,1)}, f32[4,144,288]{2,1,0:T(8,128)}, f32[4,144,288]{2,1,0:T(8,128)}, ...) custom-call(bf16[512,1152]{1,0:T(8,128)(2,1)} %get-tuple-element.78.e1, ...), custom_call_target="tpu_custom_call" | custom-call | tf_op jit(solution)/shard_map/space/pallas_call | solution.py:1356
  441.3 0.9 constant_dynamic-slice_fusion.4
  442.2 1.0 reduce_sum.29
  443.2 0.9 slice_bitcast_fusion.12
  444.1 0.1 constant_dynamic-slice_fusion.3
  444.3 0.7 dynamic_slice.33
  445.0 0.6 constant_dynamic-slice_fusion
  445.6 0.1 constant_dynamic-slice_fusion.1
  445.7 1.3 subtract_multiply_fusion
  447.0 0.6 constant_dynamic-slice_fusion.2
  447.6 0.8 slice_bitcast_fusion.2
  448.4 0.0 copy-done.6
  448.4 0.9 slice_bitcast_fusion.8
  449.4 0.9 slice_bitcast_fusion.4
  450.3 1.3 multiply_reduce_fusion
  451.6 0.0 copy-done
  451.6 0.1 slice_bitcast_fusion
  451.7 0.0 copy-start.2
  451.7 1.1 copy.117
  452.8 1.1 copy.116
  453.9 1.0 copy.129
  454.9 0.7 copy-done.1
  455.6 1.0 copy.130
  456.6 0.5 copy-done.8
  457.1 0.8 copy.131
  457.9 0.8 copy.132
  (49 shorter events, 0.2 us)
Async XLA Ops:
  0.7 19.0 %copy-start.20 = (f32[6912]{0:T(1024)S(1)}, f32[6912]{0:T(1024)}, u32[]{:S(2)}) copy-start(f32[6912]{0:T(1024)} %param.32) | copy-start | bytes 82948
  8.1 13.7 %copy-start.10 = (bf16[576,288]{0,1:T(8,128)(2,1)S(1)}, bf16[576,288]{0,1:T(8,128)(2,1)}, u32[]{:S(2)}) copy-start(bf16[576,288]{0,1:T(8,128)(2,1)} %param.33) | copy-start | bytes 995332
  18.4 4.4 copy-start.11
  18.4 5.4 %copy-start.12 = (bf16[576,288]{0,1:T(8,128)(2,1)S(1)}, bf16[576,288]{0,1:T(8,128)(2,1)}, u32[]{:S(2)}) copy-start(bf16[576,288]{0,1:T(8,128)(2,1)} %param.35) | copy-start | bytes 995332
  21.1 3.7 copy-start.13
  22.8 2.9 copy-start.14
  23.8 2.9 copy-start.15
  24.8 2.9 copy-start.16
  25.7 2.9 copy-start.17
  26.7 2.9 copy-start.18
  27.7 2.9 copy-start.19
  28.6 2.9 copy-start.3
  31.6 1.6 copy-start.4
  345.1 102.5 %copy-start.9 = (f32[2,144,288]{2,1,0:T(8,128)S(1)}, f32[2,144,288]{2,1,0:T(8,128)}, u32[]{:S(2)}) copy-start(f32[2,144,288]{2,1,0:T(8,128)} %get-tuple-element.97) | copy-start | bytes 995332
  441.3 7.1 %copy-start.6 = (f32[4,144,288]{2,1,0:T(8,128)S(1)}, f32[4,144,288]{2,1,0:T(8,128)}, u32[]{:S(2)}) copy-start(f32[4,144,288]{2,1,0:T(8,128)} %get-tuple-element.95) | copy-start | bytes 1990660
  447.6 1.7 copy-start.5
  449.4 2.3 copy-start
  451.7 2.1 copy-start.2
  453.9 1.7 copy-start.1
  455.6 1.5 copy-start.8
  455.6 2.4 copy-start.7
